TPU v7x, 32 devices: a whole 2x2x4 slice. The times are simulated.
32 devices in a mesh: groups: 2 (over y), tile: 16 (over z, x, core).
Axes of the slice: x: 2, y: 2, z: 4, core: 2. Of those that a mesh axis runs over, the one named last changes fastest.
Arguments:
- features: bfloat16 [64, 12288], P(None, ('groups', 'tile')), parts along dimension 1, may hold values from -6 to 6
- rulebook: int32 [27, 12288], P(None, ('groups', 'tile')), parts along dimension 1, may hold values from 0 to 640, as said below
- send_lists: int32 [2, 32], P(None, ('groups', 'tile')), parts along dimension 1, may hold values from 0 to 3, as said below
- weight_first: bfloat16 [64, 1728], replicated, may hold values from -0.375 to 0.375
- weight_second: bfloat16 [64, 1728], replicated, may hold values from -0.75 to 0.75
- cotangent: bfloat16 [64, 12288], P(None, ('groups', 'tile')), parts along dimension 1, may hold values from -6 to 6
Outputs:
- out_features: bfloat16 [64, 12288], P(None, ('groups', 'tile')), parts along dimension 1
- d_features: bfloat16 [64, 12288], P(None, ('groups', 'tile')), parts along dimension 1
- grad_first: float32 [128, 1728], P('groups'), parts along dimension 0
- grad_second: float32 [128, 1728], P('groups'), parts along dimension 0
There are 2 independent parts, one for each index of `groups`. A program takes and returns all parts, laid end to end along the dimension named above; an argument that names none is the same for every part. Nothing has to cross between parts.
Inputs may be any that keep to these rules, and one draw needn't show every extreme that they name: `rulebook`: A tile's rows are occupied cells of its box of 3 x 64 x 16 lattice cells, exactly 128 of them in each plane; tile t borders tile t - 1 below and t + 1 above along the first dimension. Offset k = 9 (a + 1) + 3 (b + 1) + (c + 1), with a, b, c in -1, 0, 1, names the occupied cell at that displacement, or 640 where that cell is empty or outside the detector; offset 27 // 2 names the row itself. If offset k of voxel v names voxel u, then offset 27 - 1 - k of u names v. Every halo row that is named lies in a listed block. `send_lists`: row 0 of a tile lists the distinct blocks of it that hold the cells of its lowest plane, row 1 those that hold the cells of its highest plane, 1 block each; the first tile lists nothing in row 0 and the last nothing in row 1, their entries being 3.
All inputs are finite; a program needn't handle non-finite values.
Results may differ from a plain program's by a relative error of at most 0.0042.
Values may be sent and summed in bfloat16 or wider, within the bound.
No kernel may reach another device: no remote copies, remote signals or barrier semaphores. Data moves between devices by JAX's collectives and lax.ppermute only.
A program may use at most 64 MiB of HBM per device.

v0:
```python
import math

import jax
import jax.numpy as jnp
from jax import lax
from jax.sharding import PartitionSpec as P


def with_halo(block, sides, width):
    for axis, dim in sides:
        count = lax.axis_size(axis)
        forward = [(i, i + 1) for i in range(count - 1)]
        backward = [(target, source) for source, target in forward]
        low = lax.ppermute(
            lax.slice_in_dim(block, block.shape[dim] - width, None, axis=dim), axis, forward
        )
        high = lax.ppermute(lax.slice_in_dim(block, 0, width, axis=dim), axis, backward)
        block = jnp.concatenate([low, block, high], axis=dim)
    return block


def channel_major(weight):
    width = weight.shape[0]
    return weight.reshape(width, -1, width).transpose(0, 2, 1).reshape(width, -1)


def boundary_blocks(values, send_lists):
    width, rows = values.shape
    halo = send_lists.shape[1] * 128
    blocks = jnp.concatenate(
        [values.reshape(width, rows // 128, 128), jnp.zeros((width, 1, 128), values.dtype)], axis=1
    )
    lower = blocks[:, send_lists[0]].reshape(width, halo)
    upper = blocks[:, send_lists[1]].reshape(width, halo)
    return jnp.concatenate([lower, upper], axis=1)


def extended(values, received):
    width = values.shape[0]
    halo = received.shape[1] // 4
    return jnp.concatenate(
        [
            values,
            received[:, :halo],
            received[:, 3 * halo :],
            jnp.zeros((width, 128), values.dtype),
        ],
        axis=1,
    )


def share_rim(values, send_lists):
    halo = send_lists.shape[1] * 128
    received = with_halo(boundary_blocks(values, send_lists), (("tile", 1),), halo)
    return extended(values, received)


def gathered(table, rulebook, start, block):
    indices = rulebook[:, start : start + block]
    columns = table[:, indices]
    return columns.reshape(table.shape[0] * indices.shape[0], block)


def apply_conv(weight_major, table, rulebook, block):
    rows = rulebook.shape[1]
    pieces = [
        jnp.dot(
            weight_major,
            gathered(table, rulebook, start, block),
            preferred_element_type=jnp.float32,
        )
        for start in range(0, rows, block)
    ]
    return jnp.concatenate(pieces, axis=1)


def weight_grad(grads, table, rulebook, block):
    width, rows = grads.shape
    total = jnp.zeros((width, table.shape[0] * rulebook.shape[0]), jnp.float32)
    for start in range(0, rows, block):
        columns = gathered(table, rulebook, start, block)
        total = total + lax.dot_general(
            grads[:, start : start + block],
            columns,
            (((1,), (1,)), ((), ())),
            preferred_element_type=jnp.float32,
        )
    return total.reshape(width, width, -1).transpose(0, 2, 1).reshape(width, -1)


def transposed(weight, grads, rulebook, send_lists, block):
    width, rows = grads.shape
    halo = send_lists.shape[1] * 128
    received = with_halo(boundary_blocks(grads, send_lists), (("tile", 1),), halo)
    table = extended(grads, received)
    mirror = weight.reshape(width, -1, width).transpose(2, 0, 1).reshape(width, -1)
    result = apply_conv(mirror, table, rulebook[::-1], block)
    return result


def body(features, rulebook, send_lists, weight_first, weight_second, cotangent):
    width, rows = features.shape
    block = math.gcd(rows, 512)
    x_table = share_rim(features, send_lists)
    pre_first = apply_conv(channel_major(weight_first), x_table, rulebook, block)
    hidden = jax.nn.silu(pre_first).astype(jnp.bfloat16)
    h_table = share_rim(hidden, send_lists)
    second = apply_conv(channel_major(weight_second), h_table, rulebook, block)
    out_features = (second + features.astype(jnp.float32)).astype(jnp.bfloat16)
    scale = 1.0 / math.sqrt(rows * lax.axis_size("tile"))
    grad_second = weight_grad(cotangent, h_table, rulebook, block)
    d_hidden = transposed(weight_second, cotangent, rulebook, send_lists, block)
    sigma = jax.nn.sigmoid(pre_first)
    d_pre = (d_hidden * sigma * (1.0 + pre_first * (1.0 - sigma))).astype(jnp.bfloat16)
    grad_first = weight_grad(d_pre, x_table, rulebook, block)
    d_input = transposed(weight_first, d_pre, rulebook, send_lists, block)
    d_features = (cotangent.astype(jnp.float32) + d_input).astype(jnp.bfloat16)
    grad_second, grad_first = lax.psum((grad_second, grad_first), "tile")
    return (out_features, d_features, grad_first * scale, grad_second * scale)


def solution(mesh):
    placed = (
        P(None, ("groups", "tile")),
        P(None, ("groups", "tile")),
        P(None, ("groups", "tile")),
        P(),
        P(),
        P(None, ("groups", "tile")),
    )
    return jax.shard_map(
        body,
        mesh=mesh,
        in_specs=placed,
        out_specs=(
            P(None, ("groups", "tile")),
            P(None, ("groups", "tile")),
            P("groups", None),
            P("groups", None),
        ),
        check_vma=False,
    )
```

profile of v0, /device:TPU:28, one launch (start us, length us, event | category | flops | bytes accessed | tf_op | source)
XLA Modules:
  0.0 273.3 jit_solution(2894194336046067937)
XLA Ops:
  7.2 1.3 fusion.44
  13.6 1.9 collective-permute-start
  15.7 4.5 %collective-permute-start.1 = (bf16[64,128]{0,1:T(8,128)(2,1)S(1)}, bf16[64,128]{0,1:T(8,128)(2,1)S(1)}, u32[]{:S(2)}, u32[]{:S(2)}) collective-permute-start(bf16[64,128]{0,1:T(8,128)(2,1)S(1)} %bitcast.207), channel_id=1, source_target_pairs={{1,0},{2,1},{3,2},{4,3},{5,4},{6,5},{7,6},{8,7},{9,8},{10,9},{11,1... | collective-permute-start | bytes 49160 | tf_op jit(solution)/shard_map/ppermute | solution.py:17
  20.4 2.1 collective-permute-start.5
  22.5 2.4 collective-permute-start.4
  29.9 7.1 %gather_fusion.2 = bf16[3456,64]{1,0:T(8,128)(2,1)S(1)} fusion(bf16[64,768]{0,1:T(8,128)(2,1)S(1)} %get-tuple-element.115, s32[4096]{0:T(1024)S(1)} %get-tuple-element.120), kind=kCustom, calls=%fused_computation.2 | custom fusion | bytes 898560 | tf_op jit(solution)/shard_map/gather | solution.py:60
  37.0 1.6 copy.50
  38.6 2.0 reshape.117
  40.6 8.1 %gather_fusion.1 = bf16[3456,64]{1,0:T(8,128)(2,1)} fusion(bf16[64,768]{0,1:T(8,128)(2,1)S(1)} %get-tuple-element.115, s32[4096]{0:T(1024)S(1)} %get-tuple-element.121), kind=kCustom, calls=%fused_computation.1 | custom fusion | bytes 898560 | tf_op jit(solution)/shard_map/gather | solution.py:60
  50.3 1.6 copy.47
  51.9 2.0 reshape.116
  53.9 7.1 %gather_fusion = bf16[3456,64]{1,0:T(8,128)(2,1)S(1)} fusion(bf16[64,768]{0,1:T(8,128)(2,1)S(1)} %get-tuple-element.115, s32[4096]{0:T(1024)S(1)} %pad_clamp_fusion.5), kind=kCustom, calls=%fused_computation | custom fusion | bytes 898560 | tf_op jit(solution)/shard_map/gather | solution.py:60
  63.1 7.1 %gather_fusion.7 = bf16[3456,64]{1,0:T(8,128)(2,1)S(1)} fusion(bf16[64,768]{0,1:T(8,128)(2,1)S(1)} %get-tuple-element.114, s32[4096]{0:T(1024)S(1)} %pad_clamp_fusion.1), kind=kCustom, calls=%fused_computation.7 | custom fusion | bytes 898560 | tf_op jit(solution)/shard_map/gather | solution.py:60
  70.6 8.1 %gather_fusion.8 = bf16[3456,64]{1,0:T(8,128)(2,1)S(1)} fusion(bf16[64,768]{0,1:T(8,128)(2,1)S(1)} %get-tuple-element.114, s32[4096]{0:T(1024)} %pad_clamp_fusion), kind=kCustom, calls=%fused_computation.8 | custom fusion | bytes 898560 | tf_op jit(solution)/shard_map/gather | solution.py:60
  81.7 7.1 %gather_fusion.6 = bf16[3456,64]{1,0:T(8,128)(2,1)S(1)} fusion(bf16[64,768]{0,1:T(8,128)(2,1)S(1)} %get-tuple-element.114, s32[4096]{0:T(1024)S(1)} %pad_clamp_fusion.2), kind=kCustom, calls=%fused_computation.6 | custom fusion | bytes 898560 | tf_op jit(solution)/shard_map/gather | solution.py:60
  90.1 2.1 collective-permute-start.6
  92.2 4.3 %collective-permute-start.7 = (bf16[64,128]{1,0:T(8,128)(2,1)S(1)}, bf16[64,128]{1,0:T(8,128)(2,1)S(1)}, u32[]{:S(2)}, u32[]{:S(2)}) collective-permute-start(bf16[64,128]{1,0:T(8,128)(2,1)S(1)} %get-tuple-element.103), channel_id=1, source_target_pairs={{1,0},{2,1},{3,2},{4,3},{5,4},{6,5},{7,6},{8,7},{9,8},{10,9},{11,1... | collective-permute-start | bytes 49160 | tf_op jit(solution)/shard_map/ppermute | solution.py:17
  96.5 1.9 collective-permute-start.2
  98.5 4.7 %collective-permute-start.3 = (bf16[64,128]{1,0:T(8,128)(2,1)S(1)}, bf16[64,128]{1,0:T(8,128)(2,1)S(1)}, u32[]{:S(2)}, u32[]{:S(2)}) collective-permute-start(bf16[64,128]{1,0:T(8,128)(2,1)S(1)} %get-tuple-element.111), channel_id=1, source_target_pairs={{1,0},{2,1},{3,2},{4,3},{5,4},{6,5},{7,6},{8,7},{9,8},{10,9},{11,1... | collective-permute-start | bytes 49160 | tf_op jit(solution)/shard_map/ppermute | solution.py:17
  106.0 1.1 copy.85
  107.1 1.1 reshape.119
  109.0 8.1 %gather_fusion.5 = bf16[3456,64]{1,0:T(8,128)(2,1)} fusion(bf16[64,768]{0,1:T(8,128)(2,1)S(1)} %copy.53, s32[4096]{0:T(1024)S(1)} %copy-done.25), kind=kCustom, calls=%fused_computation.5 | custom fusion | bytes 898560 | tf_op jit(solution)/shard_map/gather | solution.py:60
  117.0 7.1 %gather_fusion.4 = bf16[3456,64]{1,0:T(8,128)(2,1)S(1)} fusion(bf16[64,768]{0,1:T(8,128)(2,1)S(1)} %copy.53, s32[4096]{0:T(1024)S(1)} %copy-done.23), kind=kCustom, calls=%fused_computation.4 | custom fusion | bytes 898560 | tf_op jit(solution)/shard_map/gather | solution.py:60
  124.2 7.1 %gather_fusion.3 = bf16[3456,64]{1,0:T(8,128)(2,1)S(1)} fusion(bf16[64,768]{0,1:T(8,128)(2,1)S(1)} %copy.53, s32[4096]{0:T(1024)S(1)} %copy-done.18), kind=kCustom, calls=%fused_computation.3 | custom fusion | bytes 898560 | tf_op jit(solution)/shard_map/gather | solution.py:60
  132.0 8.0 %gather_fusion.11 = bf16[3456,64]{1,0:T(8,128)(2,1)} fusion(bf16[64,768]{0,1:T(8,128)(2,1)S(1)} %copy.75, s32[4096]{0:T(1024)S(1)} %copy-done.19), kind=kCustom, calls=%fused_computation.11 | custom fusion | bytes 898560 | tf_op jit(solution)/shard_map/gather | solution.py:60
  140.1 8.1 %gather_fusion.10 = bf16[3456,64]{1,0:T(8,128)(2,1)} fusion(bf16[64,768]{0,1:T(8,128)(2,1)S(1)} %copy.75, s32[4096]{0:T(1024)S(1)} %copy-done.21), kind=kCustom, calls=%fused_computation.10 | custom fusion | bytes 898560 | tf_op jit(solution)/shard_map/gather | solution.py:60
  148.1 8.1 %gather_fusion.9 = bf16[3456,64]{1,0:T(8,128)(2,1)} fusion(bf16[64,768]{0,1:T(8,128)(2,1)S(1)} %copy.75, s32[4096]{0:T(1024)S(1)} %pad_clamp_fusion.2), kind=kCustom, calls=%fused_computation.9 | custom fusion | bytes 898560 | tf_op jit(solution)/shard_map/gather | solution.py:60
  156.2 1.9 copy.62
  159.0 1.6 convolution_bitcast_fusion
  166.6 1.1 reshape.124
  172.3 91.5 %all-reduce.7.cloned.1.call-done = (f32[64,1728]{1,0:T(8,128)}, f32[64,1728]{1,0:T(8,128)}) async-done(((f32[64,1728]{1,0:T(8,128)}, f32[64,1728]{1,0:T(8,128)}), (f32[64,1728]{1,0:T(8,128)}, f32[64,1728]{1,0:T(8,128)})) %all-reduce.7.cloned.1.call-update) | async-done | bytes 884752 | tf_op jit(solution)/shard_map/psum | solution.py:118
  263.8 1.9 broadcast_multiply_fusion.1
  (141 shorter events, 30.9 us)
Async XLA Ops:
  7.2 256.6 %all-reduce.7.cloned.1.call-start = ((), (), s32[]{:S(2)}) async-start(), calls=%async_computation | async-start | bytes 1835008 | tf_op jit(solution)/shard_map/psum | solution.py:118
  11.1 0.8 copy-start.9
  13.6 15.6 %collective-permute-start = (bf16[64,128]{0,1:T(8,128)(2,1)S(1)}, bf16[64,128]{0,1:T(8,128)(2,1)S(1)}, u32[]{:S(2)}, u32[]{:S(2)}) collective-permute-start(bf16[64,128]{0,1:T(8,128)(2,1)S(1)} %bitcast.206), channel_id=1, source_target_pairs={{0,1},{1,2},{2,3},{3,4},{4,5},{5,6},{6,7},{7,8},{8,9},{9,10},{10,1... | collective-permute-start | bytes 49160 | tf_op jit(solution)/shard_map/ppermute | solution.py:14
  15.7 13.6 %collective-permute-start.1 = (bf16[64,128]{0,1:T(8,128)(2,1)S(1)}, bf16[64,128]{0,1:T(8,128)(2,1)S(1)}, u32[]{:S(2)}, u32[]{:S(2)}) collective-permute-start(bf16[64,128]{0,1:T(8,128)(2,1)S(1)} %bitcast.207), channel_id=1, source_target_pairs={{1,0},{2,1},{3,2},{4,3},{5,4},{6,5},{7,6},{8,7},{9,8},{10,9},{11,1... | collective-permute-start | bytes 49160 | tf_op jit(solution)/shard_map/ppermute | solution.py:17
  20.3 4.6 %copy-start.26 = (s32[27,384]{1,0:T(8,128)S(1)}, s32[27,384]{1,0:T(8,128)}, u32[]{:S(2)}) copy-start(s32[27,384]{1,0:T(8,128)} %param.7) | copy-start | bytes 124420
  20.4 8.9 %collective-permute-start.5 = (bf16[64,128]{0,1:T(8,128)(2,1)S(1)}, bf16[64,128]{0,1:T(8,128)(2,1)S(1)}, u32[]{:S(2)}, u32[]{:S(2)}) collective-permute-start(bf16[64,128]{0,1:T(8,128)(2,1)S(1)} %bitcast.208), channel_id=1, source_target_pairs={{1,0},{2,1},{3,2},{4,3},{5,4},{6,5},{7,6},{8,7},{9,8},{10,9},{11,1... | collective-permute-start | bytes 49160 | tf_op jit(solution)/shard_map/ppermute | solution.py:17
  22.5 6.8 %collective-permute-start.4 = (bf16[64,128]{0,1:T(8,128)(2,1)S(1)}, bf16[64,128]{0,1:T(8,128)(2,1)S(1)}, u32[]{:S(2)}, u32[]{:S(2)}) collective-permute-start(bf16[64,128]{0,1:T(8,128)(2,1)S(1)} %bitcast.209), channel_id=1, source_target_pairs={{0,1},{1,2},{2,3},{3,4},{4,5},{5,6},{6,7},{7,8},{8,9},{9,10},{10,1... | collective-permute-start | bytes 49160 | tf_op jit(solution)/shard_map/ppermute | solution.py:14
  25.0 28.9 %copy-start.17 = (s32[4096]{0:T(1024)}, s32[4096]{0:T(1024)S(1)}, u32[]{:S(2)}) copy-start(s32[4096]{0:T(1024)S(1)} %pad_clamp_fusion.5) | copy-start | bytes 49156
  25.7 0.8 copy-start.11
  25.7 1.0 copy-start.15
  25.8 4.1 %copy-start.24 = (s32[4096]{0:T(1024)}, s32[4096]{0:T(1024)S(1)}, u32[]{:S(2)}) copy-start(s32[4096]{0:T(1024)S(1)} %get-tuple-element.120) | copy-start | bytes 49156
  25.8 14.8 %copy-start.22 = (s32[4096]{0:T(1024)}, s32[4096]{0:T(1024)S(1)}, u32[]{:S(2)}) copy-start(s32[4096]{0:T(1024)S(1)} %get-tuple-element.121) | copy-start | bytes 49156
  26.5 36.6 %copy-start.20 = (s32[4096]{0:T(1024)}, s32[4096]{0:T(1024)S(1)}, u32[]{:S(2)}) copy-start(s32[4096]{0:T(1024)S(1)} %pad_clamp_fusion.1) | copy-start | bytes 49156
  27.3 0.9 copy-start.16
  48.6 1.2 copy-start
  49.1 1.2 copy-start.1
  79.8 1.0 copy-start.5
  90.1 18.1 %collective-permute-start.6 = (bf16[64,128]{1,0:T(8,128)(2,1)S(1)}, bf16[64,128]{1,0:T(8,128)(2,1)S(1)}, u32[]{:S(2)}, u32[]{:S(2)}) collective-permute-start(bf16[64,128]{1,0:T(8,128)(2,1)S(1)} %get-tuple-element.102), channel_id=1, source_target_pairs={{0,1},{1,2},{2,3},{3,4},{4,5},{5,6},{6,7},{7,8},{8,9},{9,10},{10,1... | collective-permute-start | bytes 49160 | tf_op jit(solution)/shard_map/ppermute | solution.py:14
  92.2 16.0 %collective-permute-start.7 = (bf16[64,128]{1,0:T(8,128)(2,1)S(1)}, bf16[64,128]{1,0:T(8,128)(2,1)S(1)}, u32[]{:S(2)}, u32[]{:S(2)}) collective-permute-start(bf16[64,128]{1,0:T(8,128)(2,1)S(1)} %get-tuple-element.103), channel_id=1, source_target_pairs={{1,0},{2,1},{3,2},{4,3},{5,4},{6,5},{7,6},{8,7},{9,8},{10,9},{11,1... | collective-permute-start | bytes 49160 | tf_op jit(solution)/shard_map/ppermute | solution.py:17
  96.5 11.6 %collective-permute-start.2 = (bf16[64,128]{1,0:T(8,128)(2,1)S(1)}, bf16[64,128]{1,0:T(8,128)(2,1)S(1)}, u32[]{:S(2)}, u32[]{:S(2)}) collective-permute-start(bf16[64,128]{1,0:T(8,128)(2,1)S(1)} %get-tuple-element.110), channel_id=1, source_target_pairs={{0,1},{1,2},{2,3},{3,4},{4,5},{5,6},{6,7},{7,8},{8,9},{9,10},{10,1... | collective-permute-start | bytes 49160 | tf_op jit(solution)/shard_map/ppermute | solution.py:14
  98.5 9.7 %collective-permute-start.3 = (bf16[64,128]{1,0:T(8,128)(2,1)S(1)}, bf16[64,128]{1,0:T(8,128)(2,1)S(1)}, u32[]{:S(2)}, u32[]{:S(2)}) collective-permute-start(bf16[64,128]{1,0:T(8,128)(2,1)S(1)} %get-tuple-element.111), channel_id=1, source_target_pairs={{1,0},{2,1},{3,2},{4,3},{5,4},{6,5},{7,6},{8,7},{9,8},{10,9},{11,1... | collective-permute-start | bytes 49160 | tf_op jit(solution)/shard_map/ppermute | solution.py:17
  103.3 1.0 copy-start.7
  104.3 1.0 copy-start.6
  107.1 1.1 copy-start.28
  109.0 8.1 %copy-start.23 = (s32[4096]{0:T(1024)S(1)}, s32[4096]{0:T(1024)}, u32[]{:S(2)}) copy-start(s32[4096]{0:T(1024)} %copy-done.22) | copy-start | bytes 49156
  117.0 7.1 %copy-start.18 = (s32[4096]{0:T(1024)S(1)}, s32[4096]{0:T(1024)}, u32[]{:S(2)}) copy-start(s32[4096]{0:T(1024)} %copy-done.17) | copy-start | bytes 49156
  132.0 8.0 %copy-start.21 = (s32[4096]{0:T(1024)S(1)}, s32[4096]{0:T(1024)}, u32[]{:S(2)}) copy-start(s32[4096]{0:T(1024)} %copy-done.20) | copy-start | bytes 49156
  163.8 1.0 copy-start.8
  166.6 1.2 copy-start.3
  167.7 1.2 copy-start.4
  169.3 1.2 copy-start.2
  263.8 1.9 copy-start.10
  (6 other events, 4.3 us)
Sparse Core Ops, SparseCore 0:
  171.2 92.5 all-reduce.6
where the time goes:
time: 276 us; the launch traced here: 273 us
  local copies, waits for them, and re-layouts  125 us (45%)
  waiting for transfers between devices  91.5 us (33%)
  starting transfers between devices  24.1 us (9%)
  between operations  18.7 us (7%)
  matrix products  8.97 us (3%)
  other arithmetic  4.94 us (2%)
    gather x24, local copies, waits for them, and re-layouts, gathered(): columns = table[:, indices]  102 us
    psum x1, waiting for transfers between devices, body(): grad_second, grad_first = lax.psum((grad_second, grad_first), 'tile')  91.5 us
    ppermute x4, starting transfers between devices, with_halo(): lax.ppermute(lax.slice_in_dim(block, 0, width, axis=dim), axis, backward)  15.7 us
    ppermute x4, starting transfers between devices, with_halo(): lax.ppermute(lax.slice_in_dim(block, block.shape[dim] - width, None, axis...  8.36 us
    unnamed x60, local copies, waits for them, and re-layouts  7.86 us
    dot_general x12, matrix products, apply_conv(): jnp.dot(weight_major, gathered(table, rulebook, start, block), preferred_...  7.26 us
  transfers between devices with their start and end apart: 9, of which 1 were waited for; matrix products, arithmetic and copies ran while one was open for 3% of the time, Pallas kernels for 0%

commit v1 on v0

v1 whole, which is shorter than its diff:
```python
import functools
import math

import jax
import jax.numpy as jnp
from jax import lax
from jax.experimental import pallas as pl
from jax.experimental.pallas import tpu as pltpu
from jax.sharding import PartitionSpec as P

BLOCK = 128
F32, BF16 = jnp.float32, jnp.bfloat16
VMEM = pl.BlockSpec(memory_space=pltpu.VMEM)
SMEM = pl.BlockSpec(memory_space=pltpu.SMEM)
NT = (((1,), (1,)), ((), ()))


def pair_blocks(lists_ref, odd):
    lower, upper = lists_ref[0, 0], lists_ref[1, 0]
    return jnp.where(odd, lower, upper), jnp.where(odd, upper, lower)


def payload_kernel(lists_ref, odd_ref, top_ref, bottom_ref, near_ref, far_ref):
    width, rows = top_ref.shape
    blocks = rows // BLOCK
    picks = pair_blocks(lists_ref, odd_ref[0] == 1)
    for pick, out_ref in zip(picks, (near_ref, far_ref)):
        start = pl.multiple_of(jnp.minimum(pick, blocks - 1) * BLOCK, BLOCK)
        listed = pick < blocks
        for half, ref in enumerate((top_ref, bottom_ref)):
            piece = ref[:, pl.ds(start, BLOCK)]
            out_ref[half * width : (half + 1) * width, :] = jnp.where(
                listed, piece, jnp.zeros_like(piece)
            )


def fill_halo(table_ref, near_ref, far_ref, odd, blocks):
    near, far = near_ref[...], far_ref[...]
    table_ref[blocks] = jnp.where(odd, near, far)
    table_ref[blocks + 1] = jnp.where(odd, far, near)


def gather(table_ref, rule_ref, first_ref, second_ref, blocks):
    offsets = rule_ref.shape[0]
    group = offsets // 3
    sources, channels, _ = table_ref.shape
    width = channels // 2
    source_rows = lax.broadcasted_iota(jnp.int32, (BLOCK, BLOCK), 0)

    def store(k, low, high, found, mirrored):
        first_ref[k * width : (k + 1) * width, low:high] = found[:width].astype(BF16)
        second_ref[mirrored * width : (mirrored + 1) * width, low:high] = found[
            width:
        ].astype(BF16)

    strays = jnp.zeros((group, BLOCK), jnp.int32)
    for block in range(blocks):
        low, high = block * BLOCK, (block + 1) * BLOCK
        for side in range(3):
            entries = rule_ref[side * group : (side + 1) * group, low:high]
            if side == 1:
                source = block
            else:
                least = jnp.min(entries.astype(F32)).astype(jnp.int32)
                source = jnp.minimum(least // BLOCK, sources - 1)
            local = entries - source * BLOCK
            named = entries < sources * BLOCK
            strays = strays | (
                named & ((local < 0) | (local >= BLOCK))
            ).astype(jnp.int32)
            table = table_ref[source]
            for j in range(group):
                k = side * group + j
                choice = (source_rows == local[j : j + 1]).astype(F32).astype(BF16)
                found = jnp.dot(table, choice, preferred_element_type=F32)
                store(k, low, high, found, offsets - 1 - k)

    @pl.when(jnp.max(strays.astype(F32)) > 0)
    def _():
        rows = rule_ref.shape[1]
        every_row = lax.broadcasted_iota(jnp.int32, (BLOCK, rows), 0)

        def one(k, carry):
            line = rule_ref[pl.ds(k, 1), :]
            found = jnp.zeros((channels, rows), F32)
            for source in range(sources):
                choice = (every_row == line - source * BLOCK).astype(F32).astype(BF16)
                found += jnp.dot(table_ref[source], choice, preferred_element_type=F32)
            here = pl.multiple_of(k * width, width)
            there = pl.multiple_of((offsets - 1 - k) * width, width)
            first_ref[pl.ds(here, width), :] = found[:width].astype(BF16)
            second_ref[pl.ds(there, width), :] = found[width:].astype(BF16)
            return carry

        lax.fori_loop(0, offsets, one, 0)


def turn(weight_ref, turned_ref):
    width, depth = weight_ref.shape
    offsets = depth // width
    for k in range(0, offsets, 2):
        count = min(2, offsets - k)
        block = weight_ref[:, k * width : (k + count) * width].astype(F32).T
        pieces = [block[i * width : (i + 1) * width] for i in range(count)]
        joined = pieces[0] if count == 1 else jnp.concatenate(pieces, axis=1)
        turned_ref[:, k * width : (k + count) * width] = joined.astype(BF16)


def first_kernel(
    lists_ref, odd_ref, rule_ref, x_ref, g_ref, near_ref, far_ref, w1_ref, w2_ref,
    state_ref, near_out, far_out, keep_ref, send_ref,
    table_ref, xs_ref, gs_ref, turned_ref,
):
    width, rows = x_ref.shape
    blocks = rows // BLOCK
    offsets = rule_ref.shape[0]
    odd = odd_ref[0] == 1
    for block in range(blocks):
        low, high = block * BLOCK, (block + 1) * BLOCK
        table_ref[block, :width] = x_ref[:, low:high]
        table_ref[block, width:] = g_ref[:, low:high]
    fill_halo(table_ref, near_ref, far_ref, odd, blocks)
    turn(w2_ref, turned_ref)
    gather(table_ref, rule_ref, xs_ref, gs_ref, blocks)
    pre = jnp.dot(w1_ref[...], xs_ref[...], preferred_element_type=F32)
    d_hidden = jnp.dot(turned_ref[...], gs_ref[...], preferred_element_type=F32)
    sigma = jax.nn.sigmoid(pre)
    hidden = (pre * sigma).astype(BF16)
    d_pre = (d_hidden * sigma * (1.0 + pre * (1.0 - sigma))).astype(BF16)
    for block in range(blocks):
        low, high = block * BLOCK, (block + 1) * BLOCK
        state_ref[block, :width] = hidden[:, low:high]
        state_ref[block, width:] = d_pre[:, low:high]
    for pick, out_ref in zip(pair_blocks(lists_ref, odd), (near_out, far_out)):
        piece = state_ref[jnp.minimum(pick, blocks - 1)]
        out_ref[...] = jnp.where(pick < blocks, piece, jnp.zeros_like(piece))
    grad_first = lax.dot_general(d_pre, xs_ref[...], NT, preferred_element_type=F32)
    stacked = lax.dot_general(gs_ref[...], hidden, NT, preferred_element_type=F32)
    for k in range(0, offsets, 2):
        count = min(2, offsets - k)
        low, high = k * width, (k + count) * width
        pieces = [stacked[low + i * width : low + (i + 1) * width] for i in range(count)]
        second = pieces[0] if count == 1 else jnp.concatenate(pieces, axis=1)
        first = grad_first[:, low:high]
        keep_ref[:, low:high] = jnp.where(odd, second, first)
        send_ref[:, low:high] = jnp.where(odd, first, second).astype(BF16)


def second_kernel(
    odd_ref, rule_ref, state_ref, near_ref, far_ref, w1_ref, w2_ref, x_ref, g_ref,
    out_ref, dx_ref,
    table_ref, hs_ref, ds_ref, turned_ref,
):
    width, rows = x_ref.shape
    blocks = rows // BLOCK
    odd = odd_ref[0] == 1
    for block in range(blocks):
        table_ref[block] = state_ref[block]
    fill_halo(table_ref, near_ref, far_ref, odd, blocks)
    turn(w1_ref, turned_ref)
    gather(table_ref, rule_ref, hs_ref, ds_ref, blocks)
    second = jnp.dot(w2_ref[...], hs_ref[...], preferred_element_type=F32)
    out_ref[...] = (second + x_ref[...].astype(F32)).astype(BF16)
    d_input = jnp.dot(turned_ref[...], ds_ref[...], preferred_element_type=F32)
    dx_ref[...] = (d_input + g_ref[...].astype(F32)).astype(BF16)


def neighbour_pairs(count):
    near = [(i, i ^ 1) for i in range(count) if i ^ 1 < count]
    far = [(i, i + 1 if i % 2 else i - 1) for i in range(count)]
    return near, [(i, j) for i, j in far if 0 <= j < count]


def total_over_tiles(keep, send, odd, first_scale):
    count = lax.axis_size("tile")
    received = lax.ppermute(send, "tile", [(i, i ^ 1) for i in range(count)])
    total = keep + received.astype(F32)
    bits = [1 << b for b in range(1, count.bit_length() - 1)]
    for step, (even_bit, odd_bit) in enumerate(zip(bits, bits[-1:] + bits[:-1])):
        wire = BF16 if step >= len(bits) - 3 else F32
        pairs = [(i, i ^ (odd_bit if i % 2 else even_bit)) for i in range(count)]
        sent = total.astype(wire)
        total = sent.astype(F32) + lax.ppermute(sent, "tile", pairs).astype(F32)
    total = total * first_scale
    other = lax.ppermute(total, "tile", [(i, i ^ 1) for i in range(count)])
    return jnp.where(odd, other, total), jnp.where(odd, total, other)


def body(features, rulebook, send_lists, weight_first, weight_second, cotangent):
    width, rows = features.shape
    offsets = rulebook.shape[0]
    blocks = rows // BLOCK
    count = lax.axis_size("tile")
    parity = lax.axis_index("tile") % 2
    odd = parity == 1
    parity = parity.reshape(1).astype(jnp.int32)
    near_pairs, far_pairs = neighbour_pairs(count)
    shape = jax.ShapeDtypeStruct
    rim = shape((2 * width, BLOCK), BF16)

    near, far = pl.pallas_call(
        payload_kernel,
        out_shape=(rim, rim),
        in_specs=[SMEM, SMEM, VMEM, VMEM],
        out_specs=(VMEM, VMEM),
    )(send_lists, parity, features, cotangent)
    near = lax.ppermute(near, "tile", near_pairs)
    far = lax.ppermute(far, "tile", far_pairs)

    scratch = [
        pltpu.VMEM((blocks + 2, 2 * width, BLOCK), BF16),
        pltpu.VMEM((offsets * width, rows), BF16),
        pltpu.VMEM((offsets * width, rows), BF16),
        pltpu.VMEM((width, offsets * width), BF16),
    ]
    state, near, far, keep, send = pl.pallas_call(
        first_kernel,
        out_shape=(
            shape((blocks, 2 * width, BLOCK), BF16), rim, rim,
            shape((width, offsets * width), F32), shape((width, offsets * width), BF16),
        ),
        in_specs=[SMEM, SMEM] + [VMEM] * 7,
        out_specs=(VMEM,) * 5,
        scratch_shapes=scratch,
    )(send_lists, parity, rulebook, features, cotangent, near, far, weight_first, weight_second)

    near = lax.ppermute(near, "tile", near_pairs)
    far = lax.ppermute(far, "tile", far_pairs)
    out_features, d_features = pl.pallas_call(
        second_kernel,
        out_shape=(shape((width, rows), BF16), shape((width, rows), BF16)),
        in_specs=[SMEM] + [VMEM] * 8,
        out_specs=(VMEM, VMEM),
        scratch_shapes=scratch,
        cost_estimate=pl.CostEstimate(
            flops=2 * 2 * width * offsets * rows * (width + BLOCK),
            bytes_accessed=4 * offsets * width * rows,
            transcendentals=0,
        ),
    )(parity, rulebook, state, near, far, weight_first, weight_second, features, cotangent)

    scale = 1.0 / math.sqrt(rows * count)
    grad_first, grad_second = total_over_tiles(keep, send, odd, scale)
    return out_features, d_features, grad_first, grad_second


def solution(mesh):
    placed = (
        P(None, ("groups", "tile")),
        P(None, ("groups", "tile")),
        P(None, ("groups", "tile")),
        P(),
        P(),
        P(None, ("groups", "tile")),
    )
    return jax.shard_map(
        body,
        mesh=mesh,
        in_specs=placed,
        out_specs=(
            P(None, ("groups", "tile")),
            P(None, ("groups", "tile")),
            P("groups", None),
            P("groups", None),
        ),
        check_vma=False,
    )
```

time: 276 us -> 51.6 us (0.19)
  local copies, waits for them, and re-layouts: 125 us -> 2.55 us
  waiting for transfers between devices: 91.5 us -> 29 us
  between operations: 18.7 us -> 0.76 us
  starting transfers between devices: 24.1 us -> 7.36 us
  Pallas kernels: 0 us -> 9.46 us
  matrix products: 8.97 us -> 0 us
    gather x24 -> x0, local copies, waits for them, and re-layouts: 102 us -> none  [gathered(): columns = table[:, indices]]
    psum x1 -> x0, waiting for transfers between devices: 91.5 us -> none  [body(): grad_second, grad_first = lax.psum((grad_second, grad_first), 'tile')]
    ppermute x8 -> x9, waiting for transfers between devices: 0.02 us -> 29 us  [the longest x3 20.1 us: total_over_tiles(): total = sent.astype(F32) + lax.ppermute(sent, 'tile', pairs).astype(F32)]
    ppermute x8 -> x9, starting transfers between devices: 24 us -> 7.36 us  [the longest x2 5.29 us: body(): far = lax.ppermute(far, 'tile', far_pairs)]
    reshape x16 -> x0, local copies, waits for them, and re-layouts: 9.49 us -> none  [the longest x6 5.29 us: gathered(): return columns.reshape(table.shape[0] * indices.shape[0], block)]
    pallas_call x0 -> x3, Pallas kernels: none -> 9.46 us  [the longest x1 4.54 us: body(): pl.pallas_call(first_kernel, out_shape=(shape((blocks, 2 * width, BLOCK),...]
    dot_general x18 -> x0, matrix products: 8.97 us -> none  [the longest x12 7.26 us: apply_conv(): jnp.dot(weight_major, gathered(table, rulebook, start, block), preferred_...]
    unnamed x60 -> x15, local copies, waits for them, and re-layouts: 7.86 us -> 2.55 us
  transfers between devices with their start and end apart: 9 -> 9, of which waited for: 1 -> 6; matrix products, arithmetic and copies ran while one was open for 3% -> 0% of each run, Pallas kernels for 0% -> 7%
where the time goes in v1:
time: 51.6 us; the launch traced here: 51.3 us
  waiting for transfers between devices  29 us (56%)
  Pallas kernels  9.46 us (18%)
  starting transfers between devices  7.36 us (14%)
  local copies, waits for them, and re-layouts  2.55 us (5%)
  other arithmetic  2.26 us (4%)
  between operations  0.76 us (1%)
    ppermute x3, waiting for transfers between devices, total_over_tiles(): total = sent.astype(F32) + lax.ppermute(sent, 'tile', pairs).astype(F32)  20.1 us
    ppermute x2, waiting for transfers between devices, body(): far = lax.ppermute(far, 'tile', far_pairs)  7.19 us
    ppermute x2, starting transfers between devices, body(): far = lax.ppermute(far, 'tile', far_pairs)  5.29 us
    pallas_call x1, Pallas kernels, body(): pl.pallas_call(first_kernel, out_shape=(shape((blocks, 2 * width, BLOCK),...  4.54 us
    pallas_call x1, Pallas kernels, body(): pl.pallas_call(second_kernel, out_shape=(shape((width, rows), BF16), shap...  3.44 us
    unnamed x15, local copies, waits for them, and re-layouts  2.55 us
    ppermute x1, waiting for transfers between devices, total_over_tiles(): received = lax.ppermute(send, 'tile', [(i, i ^ 1) for i in range(count)])  1.68 us
    ppermute x3, starting transfers between devices, total_over_tiles(): total = sent.astype(F32) + lax.ppermute(sent, 'tile', pairs).astype(F32)  1.48 us
  transfers between devices with their start and end apart: 9, of which 6 were waited for; matrix products, arithmetic and copies ran while one was open for 0% of the time, Pallas kernels for 7%

profile of v1, /device:TPU:28, one launch (start us, length us, event | category | flops | bytes accessed | tf_op | source)
XLA Modules:
  0.0 51.3 jit_solution(16386833999849781152)
XLA Ops:
  0.6 0.6 %copy-done.6 = s32[2,1]{0,1:T(1,128)S(1)} copy-done((s32[2,1]{0,1:T(1,128)S(1)}, s32[2,1]{0,1:T(1,128)}, u32[]{:S(2)}) %copy-start.6) | copy-done | bytes 32
  1.3 0.6 %copy.11.lists_ref = s32[2,1]{1,0:T(2,128)} copy(s32[2,1]{0,1:T(1,128)S(1)} %copy-done.6) | data formatting | bytes 16 | tf_op args[2]
  1.9 1.5 %shard_map.93 = (bf16[128,128]{1,0:T(8,128)(2,1)}, bf16[128,128]{1,0:T(8,128)(2,1)}) custom-call(s32[2,1]{1,0:T(2,128)} %copy.11.lists_ref, s32[1]{0:T(128)} %bitcast.odd_ref, bf16[64,384]{1,0:T(8,128)(2,1)} %x_ref.3, bf16[64,384]{1,0:T(8,128)(2,1)} %g_ref.3), custom_call_target="tpu_custom_call" | custom-call | tf_op jit(solution)/shard_map/pallas_call | solution.py:201
  3.4 0.0 collective-permute-start
  3.4 3.4 %collective-permute-start.1 = (bf16[128,128]{1,0:T(8,128)(2,1)}, bf16[128,128]{1,0:T(8,128)(2,1)S(1)}, u32[]{:S(2)}, u32[]{:S(2)}) collective-permute-start(bf16[128,128]{1,0:T(8,128)(2,1)} %get-tuple-element.14), channel_id=1, source_target_pairs={{1,2},{2,1},{3,4},{4,3},{5,6},{6,5},{7,8},{8,7},{9,10},{10,9},{11,... | collective-permute-start | bytes 98312 | tf_op jit(solution)/shard_map/ppermute | solution.py:208
  6.8 0.0 collective-permute-done.near_ref
  6.8 0.0 copy-start
  6.8 3.0 %collective-permute-done.1.far_ref = bf16[128,128]{1,0:T(8,128)(2,1)S(1)} collective-permute-done((bf16[128,128]{1,0:T(8,128)(2,1)}, bf16[128,128]{1,0:T(8,128)(2,1)S(1)}, u32[]{:S(2)}, u32[]{:S(2)}) %collective-permute-start.1) | collective-permute-done | bytes 32800 | tf_op jit(solution)/shard_map/ppermute | solution.py:208
  9.9 0.6 %copy-done.1 = bf16[128,128]{1,0:T(8,128)(2,1)} copy-done((bf16[128,128]{1,0:T(8,128)(2,1)}, bf16[128,128]{1,0:T(8,128)(2,1)S(1)}, u32[]{:S(2)}) %copy-start.1) | copy-done | bytes 32792
  10.5 4.5 %shard_map.94 = (bf16[3,128,128]{2,1,0:T(8,128)(2,1)}, bf16[128,128]{1,0:T(8,128)(2,1)}, bf16[128,128]{1,0:T(8,128)(2,1)}, f32[64,1728]{1,0:T(8,128)}, bf16[64,1728]{1,0:T(8,128)(2,1)}) custom-call(s32[2,1]{1,0:T(2,128)} %copy.11.lists_ref, s32[1]{0:T(128)} %bitcast.odd_ref, s32[27,384]{1,0:T(8,128)} %rule_ref.3, bf16[64,384]{1,0:T(8,128)(2,1)} %x_ref.3, ...), custom_call_target="tpu_custom_call" | custom-call | tf_op jit(solution)/shard_map/pallas_call | solution.py:216
  15.0 0.0 collective-permute-start.4
  15.0 1.7 %collective-permute-done.4 = bf16[64,1728]{1,0:T(8,128)(2,1)S(1)} collective-permute-done((bf16[64,1728]{1,0:T(8,128)(2,1)}, bf16[64,1728]{1,0:T(8,128)(2,1)S(1)}, u32[]{:S(2)}, u32[]{:S(2)}) %collective-permute-start.4) | collective-permute-done | bytes 221216 | tf_op jit(solution)/shard_map/ppermute | solution.py:176
  16.7 1.1 %add_convert_fusion.2 = bf16[64,1728]{1,0:T(8,128)(2,1)S(1)} fusion(f32[64,1728]{1,0:T(8,128)} %get-tuple-element.20, bf16[64,1728]{1,0:T(8,128)(2,1)S(1)} %collective-permute-done.4), kind=kLoop, calls=%fused_computation.3 | loop fusion | flops 331776 | bytes 884736 | tf_op jit(solution)/shard_map/convert_element_type | solution.py:182
  17.8 0.6 %collective-permute-start.5 = (bf16[64,1728]{1,0:T(8,128)(2,1)S(1)}, bf16[64,1728]{1,0:T(8,128)(2,1)S(1)}, u32[]{:S(2)}, u32[]{:S(2)}) collective-permute-start(bf16[64,1728]{1,0:T(8,128)(2,1)S(1)} %add_convert_fusion.2), channel_id=1, source_target_pairs={{0,2},{1,9},{2,0},{3,11},{4,6},{5,13},{6,4},{7,15},{8,10},{9,1},{1... | collective-permute-start | bytes 663560 | tf_op jit(solution)/shard_map/ppermute | solution.py:183
  18.4 5.5 %collective-permute-done.5 = bf16[64,1728]{1,0:T(8,128)(2,1)S(1)} collective-permute-done((bf16[64,1728]{1,0:T(8,128)(2,1)S(1)}, bf16[64,1728]{1,0:T(8,128)(2,1)S(1)}, u32[]{:S(2)}, u32[]{:S(2)}) %collective-permute-start.5) | collective-permute-done | bytes 221216 | tf_op jit(solution)/shard_map/ppermute | solution.py:183
  23.9 0.1 add_convert_fusion.1
  23.9 0.5 %collective-permute-start.6 = (bf16[64,1728]{1,0:T(8,128)(2,1)S(1)}, bf16[64,1728]{1,0:T(8,128)(2,1)S(1)}, u32[]{:S(2)}, u32[]{:S(2)}) collective-permute-start(bf16[64,1728]{1,0:T(8,128)(2,1)S(1)} %add_convert_fusion.1), channel_id=1, source_target_pairs={{0,4},{1,3},{2,6},{3,1},{4,0},{5,7},{6,2},{7,5},{8,12},{9,11},{10,... | collective-permute-start | bytes 663560 | tf_op jit(solution)/shard_map/ppermute | solution.py:183
  24.5 5.6 %collective-permute-done.6 = bf16[64,1728]{1,0:T(8,128)(2,1)S(1)} collective-permute-done((bf16[64,1728]{1,0:T(8,128)(2,1)S(1)}, bf16[64,1728]{1,0:T(8,128)(2,1)S(1)}, u32[]{:S(2)}, u32[]{:S(2)}) %collective-permute-start.6) | collective-permute-done | bytes 221216 | tf_op jit(solution)/shard_map/ppermute | solution.py:183
  30.0 0.1 add_convert_fusion
  30.1 0.4 collective-permute-start.7
  30.5 9.0 %collective-permute-done.7 = bf16[64,1728]{1,0:T(8,128)(2,1)S(1)} collective-permute-done((bf16[64,1728]{1,0:T(8,128)(2,1)S(1)}, bf16[64,1728]{1,0:T(8,128)(2,1)S(1)}, u32[]{:S(2)}, u32[]{:S(2)}) %collective-permute-start.7) | collective-permute-done | bytes 221216 | tf_op jit(solution)/shard_map/ppermute | solution.py:183
  39.5 0.1 add_multiply_fusion
  39.6 0.1 collective-permute-start.8
  39.6 0.5 collective-permute-start.2
  40.1 1.9 %collective-permute-start.3 = (bf16[128,128]{1,0:T(8,128)(2,1)S(1)}, bf16[128,128]{1,0:T(8,128)(2,1)S(1)}, u32[]{:S(2)}, u32[]{:S(2)}) collective-permute-start(bf16[128,128]{1,0:T(8,128)(2,1)S(1)} %copy-done.2), channel_id=1, source_target_pairs={{1,2},{2,1},{3,4},{4,3},{5,6},{6,5},{7,8},{8,7},{9,10},{10,9},{11,... | collective-permute-start | bytes 98312 | tf_op jit(solution)/shard_map/ppermute | solution.py:228
  42.1 0.0 collective-permute-done.2.near_ref
  42.1 0.0 copy-start.4
  42.1 4.2 %collective-permute-done.3.far_ref = bf16[128,128]{1,0:T(8,128)(2,1)S(1)} collective-permute-done((bf16[128,128]{1,0:T(8,128)(2,1)S(1)}, bf16[128,128]{1,0:T(8,128)(2,1)S(1)}, u32[]{:S(2)}, u32[]{:S(2)}) %collective-permute-start.3) | collective-permute-done | bytes 32800 | tf_op jit(solution)/shard_map/ppermute | solution.py:228
  46.3 0.6 %copy-done.5 = bf16[128,128]{1,0:T(8,128)(2,1)} copy-done((bf16[128,128]{1,0:T(8,128)(2,1)}, bf16[128,128]{1,0:T(8,128)(2,1)S(1)}, u32[]{:S(2)}) %copy-start.5) | copy-done | bytes 32792
  46.9 3.4 %shard_map.95 = (bf16[64,384]{1,0:T(8,128)(2,1)}, bf16[64,384]{1,0:T(8,128)(2,1)}) custom-call(s32[1]{0:T(128)} %bitcast.odd_ref, s32[27,384]{1,0:T(8,128)} %rule_ref.3, bf16[3,128,128]{2,1,0:T(8,128)(2,1)} %get-tuple-element.15.state_ref, bf16[128,128]{1,0:T(8,128)(2,1)} %copy-done.4, bf16[128,128]{1,0:T(8,128)(2,1)} %copy-done.5, bf16[64,1728]{1,0:T(8,128)(2,1)} %w1_ref.3, ...), custom_call_target="tpu_custom_call" | custom-call | flops 509607936 | bytes 2654208 | tf_op jit(solution)/shard_map/pallas_call | solution.py:229
  50.3 0.0 collective-permute-done.8
  50.3 1.0 %broadcast_select_fusion = (f32[64,1728]{1,0:T(8,128)}, f32[64,1728]{1,0:T(8,128)}) fusion(f32[64,1728]{1,0:T(8,128)S(1)} %collective-permute-done.8, pred[]{:T(512)S(6)} %eq.5, bf16[64,1728]{1,0:T(8,128)(2,1)S(1)} %collective-permute-done.7, bf16[64,1728]{1,0:T(8,128)(2,1)S(1)} %add_convert_fusion), kind=kLoop, calls=%fused_computation.4 | loop fusion | flops 663552 | bytes 1769473 | tf_op jit(solution)/shard_map/jit(_where)/select_n | solution.py:186
  (9 shorter events, 0.0 us)
Async XLA Ops:
  0.6 0.7 %copy-start.6 = (s32[2,1]{0,1:T(1,128)S(1)}, s32[2,1]{0,1:T(1,128)}, u32[]{:S(2)}) copy-start(s32[2,1]{0,1:T(1,128)} %param.8) | copy-start | bytes 28
  3.4 3.4 %collective-permute-start = (bf16[128,128]{1,0:T(8,128)(2,1)}, bf16[128,128]{1,0:T(8,128)(2,1)S(1)}, u32[]{:S(2)}, u32[]{:S(2)}) collective-permute-start(bf16[128,128]{1,0:T(8,128)(2,1)} %get-tuple-element.13), channel_id=1, source_target_pairs={{0,1},{1,0},{2,3},{3,2},{4,5},{5,4},{6,7},{7,6},{8,9},{9,8},{10,11... | collective-permute-start | bytes 98312 | tf_op jit(solution)/shard_map/ppermute | solution.py:207
  3.4 6.4 %collective-permute-start.1 = (bf16[128,128]{1,0:T(8,128)(2,1)}, bf16[128,128]{1,0:T(8,128)(2,1)S(1)}, u32[]{:S(2)}, u32[]{:S(2)}) collective-permute-start(bf16[128,128]{1,0:T(8,128)(2,1)} %get-tuple-element.14), channel_id=1, source_target_pairs={{1,2},{2,1},{3,4},{4,3},{5,6},{6,5},{7,8},{8,7},{9,10},{10,9},{11,... | collective-permute-start | bytes 98312 | tf_op jit(solution)/shard_map/ppermute | solution.py:208
  6.8 3.0 %copy-start = (bf16[128,128]{1,0:T(8,128)(2,1)}, bf16[128,128]{1,0:T(8,128)(2,1)S(1)}, u32[]{:S(2)}) copy-start(bf16[128,128]{1,0:T(8,128)(2,1)S(1)} %collective-permute-done.near_ref) | copy-start | bytes 98308
  9.9 0.6 %copy-start.1 = (bf16[128,128]{1,0:T(8,128)(2,1)}, bf16[128,128]{1,0:T(8,128)(2,1)S(1)}, u32[]{:S(2)}) copy-start(bf16[128,128]{1,0:T(8,128)(2,1)S(1)} %collective-permute-done.1.far_ref) | copy-start | bytes 98308
  15.0 1.7 %collective-permute-start.4 = (bf16[64,1728]{1,0:T(8,128)(2,1)}, bf16[64,1728]{1,0:T(8,128)(2,1)S(1)}, u32[]{:S(2)}, u32[]{:S(2)}) collective-permute-start(bf16[64,1728]{1,0:T(8,128)(2,1)} %get-tuple-element.21), channel_id=1, source_target_pairs={{0,1},{1,0},{2,3},{3,2},{4,5},{5,4},{6,7},{7,6},{8,9},{9,8},{10,11... | collective-permute-start | bytes 663560 | tf_op jit(solution)/shard_map/ppermute | solution.py:176
  17.8 6.1 %collective-permute-start.5 = (bf16[64,1728]{1,0:T(8,128)(2,1)S(1)}, bf16[64,1728]{1,0:T(8,128)(2,1)S(1)}, u32[]{:S(2)}, u32[]{:S(2)}) collective-permute-start(bf16[64,1728]{1,0:T(8,128)(2,1)S(1)} %add_convert_fusion.2), channel_id=1, source_target_pairs={{0,2},{1,9},{2,0},{3,11},{4,6},{5,13},{6,4},{7,15},{8,10},{9,1},{1... | collective-permute-start | bytes 663560 | tf_op jit(solution)/shard_map/ppermute | solution.py:183
  23.9 6.1 %collective-permute-start.6 = (bf16[64,1728]{1,0:T(8,128)(2,1)S(1)}, bf16[64,1728]{1,0:T(8,128)(2,1)S(1)}, u32[]{:S(2)}, u32[]{:S(2)}) collective-permute-start(bf16[64,1728]{1,0:T(8,128)(2,1)S(1)} %add_convert_fusion.1), channel_id=1, source_target_pairs={{0,4},{1,3},{2,6},{3,1},{4,0},{5,7},{6,2},{7,5},{8,12},{9,11},{10,... | collective-permute-start | bytes 663560 | tf_op jit(solution)/shard_map/ppermute | solution.py:183
  30.1 9.6 %copy-start.3 = (bf16[128,128]{1,0:T(8,128)(2,1)S(1)}, bf16[128,128]{1,0:T(8,128)(2,1)}, u32[]{:S(2)}) copy-start(bf16[128,128]{1,0:T(8,128)(2,1)} %get-tuple-element.16) | copy-start | bytes 98308
  30.1 10.0 %copy-start.2 = (bf16[128,128]{1,0:T(8,128)(2,1)S(1)}, bf16[128,128]{1,0:T(8,128)(2,1)}, u32[]{:S(2)}) copy-start(bf16[128,128]{1,0:T(8,128)(2,1)} %get-tuple-element.17) | copy-start | bytes 98308
  30.1 9.4 %collective-permute-start.7 = (bf16[64,1728]{1,0:T(8,128)(2,1)S(1)}, bf16[64,1728]{1,0:T(8,128)(2,1)S(1)}, u32[]{:S(2)}, u32[]{:S(2)}) collective-permute-start(bf16[64,1728]{1,0:T(8,128)(2,1)S(1)} %add_convert_fusion), channel_id=1, source_target_pairs={{0,8},{1,5},{2,10},{3,7},{4,12},{5,1},{6,14},{7,3},{8,0},{9,13},{1... | collective-permute-start | bytes 663560 | tf_op jit(solution)/shard_map/ppermute | solution.py:183
  39.6 10.8 %collective-permute-start.8 = (f32[64,1728]{1,0:T(8,128)S(1)}, f32[64,1728]{1,0:T(8,128)S(1)}, u32[]{:S(2)}, u32[]{:S(2)}) collective-permute-start(f32[64,1728]{1,0:T(8,128)S(1)} %add_multiply_fusion), channel_id=1, source_target_pairs={{0,1},{1,0},{2,3},{3,2},{4,5},{5,4},{6,7},{7,6},{8,9},{9,8},{10,11... | collective-permute-start | bytes 1327112 | tf_op jit(solution)/shard_map/ppermute | solution.py:185
  39.6 2.4 %collective-permute-start.2 = (bf16[128,128]{1,0:T(8,128)(2,1)S(1)}, bf16[128,128]{1,0:T(8,128)(2,1)S(1)}, u32[]{:S(2)}, u32[]{:S(2)}) collective-permute-start(bf16[128,128]{1,0:T(8,128)(2,1)S(1)} %copy-done.3), channel_id=1, source_target_pairs={{0,1},{1,0},{2,3},{3,2},{4,5},{5,4},{6,7},{7,6},{8,9},{9,8},{10,11... | collective-permute-start | bytes 98312 | tf_op jit(solution)/shard_map/ppermute | solution.py:227
  40.1 6.1 %collective-permute-start.3 = (bf16[128,128]{1,0:T(8,128)(2,1)S(1)}, bf16[128,128]{1,0:T(8,128)(2,1)S(1)}, u32[]{:S(2)}, u32[]{:S(2)}) collective-permute-start(bf16[128,128]{1,0:T(8,128)(2,1)S(1)} %copy-done.2), channel_id=1, source_target_pairs={{1,2},{2,1},{3,4},{4,3},{5,6},{6,5},{7,8},{8,7},{9,10},{10,9},{11,... | collective-permute-start | bytes 98312 | tf_op jit(solution)/shard_map/ppermute | solution.py:228
  42.1 4.2 %copy-start.4 = (bf16[128,128]{1,0:T(8,128)(2,1)}, bf16[128,128]{1,0:T(8,128)(2,1)S(1)}, u32[]{:S(2)}) copy-start(bf16[128,128]{1,0:T(8,128)(2,1)S(1)} %collective-permute-done.2.near_ref) | copy-start | bytes 98308
  46.3 0.6 %copy-start.5 = (bf16[128,128]{1,0:T(8,128)(2,1)}, bf16[128,128]{1,0:T(8,128)(2,1)S(1)}, u32[]{:S(2)}) copy-start(bf16[128,128]{1,0:T(8,128)(2,1)S(1)} %collective-permute-done.3.far_ref) | copy-start | bytes 98308

commit v2 on v1

--- a/solution.py
+++ b/solution.py
@@ -1,4 +1,3 @@
-import functools
 import math
 
 import jax
@@ -8,30 +7,44 @@
 from jax.experimental.pallas import tpu as pltpu
 from jax.sharding import PartitionSpec as P
 
+
 BLOCK = 128
 F32, BF16 = jnp.float32, jnp.bfloat16
+HBM = pl.BlockSpec(memory_space=pltpu.HBM)
+SMALL = pltpu.CompilerParams(vmem_limit_bytes=1 << 20)
+MEDIUM = pltpu.CompilerParams(vmem_limit_bytes=20 << 20)
 VMEM = pl.BlockSpec(memory_space=pltpu.VMEM)
 SMEM = pl.BlockSpec(memory_space=pltpu.SMEM)
 NT = (((1,), (1,)), ((), ()))
 
 
 def pair_blocks(lists_ref, odd):
-    lower, upper = lists_ref[0, 0], lists_ref[1, 0]
+    lower, upper = lists_ref[0], lists_ref[1]
     return jnp.where(odd, lower, upper), jnp.where(odd, upper, lower)
 
 
-def payload_kernel(lists_ref, odd_ref, top_ref, bottom_ref, near_ref, far_ref):
-    width, rows = top_ref.shape
-    blocks = rows // BLOCK
+def fetch(sources, targets, sems):
+    copies = [
+        pltpu.make_async_copy(source, target, sems.at[i])
+        for i, (source, target) in enumerate(zip(sources, targets))
+    ]
+    for copy in copies:
+        copy.start()
+    return copies
+
+
+def payload_kernel(
+    lists_hbm, odd_ref, x_hbm, g_hbm, near_ref, far_ref, lists_ref, x_ref, g_ref, sems
+):
+    width, rows = x_ref.shape
+    copies = fetch((lists_hbm, x_hbm, g_hbm), (lists_ref, x_ref, g_ref), sems)
+    for copy in copies:
+        copy.wait()
     picks = pair_blocks(lists_ref, odd_ref[0] == 1)
     for pick, out_ref in zip(picks, (near_ref, far_ref)):
-        start = pl.multiple_of(jnp.minimum(pick, blocks - 1) * BLOCK, BLOCK)
-        listed = pick < blocks
-        for half, ref in enumerate((top_ref, bottom_ref)):
-            piece = ref[:, pl.ds(start, BLOCK)]
-            out_ref[half * width : (half + 1) * width, :] = jnp.where(
-                listed, piece, jnp.zeros_like(piece)
-            )
+        start = pl.multiple_of(jnp.minimum(pick, rows // BLOCK - 1) * BLOCK, BLOCK)
+        out_ref[:width, :] = x_ref[:, pl.ds(start, BLOCK)]
+        out_ref[width:, :] = g_ref[:, pl.ds(start, BLOCK)]
 
 
 def fill_halo(table_ref, near_ref, far_ref, odd, blocks):
@@ -107,21 +120,31 @@
 
 
 def first_kernel(
-    lists_ref, odd_ref, rule_ref, x_ref, g_ref, near_ref, far_ref, w1_ref, w2_ref,
+    odd_ref, near_ref, far_ref, lists_hbm, rule_hbm, x_hbm, g_hbm, w1_hbm, w2_hbm,
     state_ref, near_out, far_out, keep_ref, send_ref,
     table_ref, xs_ref, gs_ref, turned_ref,
+    lists_ref, rule_ref, x_ref, g_ref, w1_ref, w2_ref, sems,
 ):
+    copies = fetch(
+        (lists_hbm, rule_hbm, x_hbm, g_hbm, w2_hbm, w1_hbm),
+        (lists_ref, rule_ref, x_ref, g_ref, w2_ref, w1_ref),
+        sems,
+    )
     width, rows = x_ref.shape
     blocks = rows // BLOCK
     offsets = rule_ref.shape[0]
     odd = odd_ref[0] == 1
+    for copy in copies[:4]:
+        copy.wait()
     for block in range(blocks):
         low, high = block * BLOCK, (block + 1) * BLOCK
         table_ref[block, :width] = x_ref[:, low:high]
         table_ref[block, width:] = g_ref[:, low:high]
     fill_halo(table_ref, near_ref, far_ref, odd, blocks)
+    gather(table_ref, rule_ref, xs_ref, gs_ref, blocks)
+    for copy in copies[4:]:
+        copy.wait()
     turn(w2_ref, turned_ref)
-    gather(table_ref, rule_ref, xs_ref, gs_ref, blocks)
     pre = jnp.dot(w1_ref[...], xs_ref[...], preferred_element_type=F32)
     d_hidden = jnp.dot(turned_ref[...], gs_ref[...], preferred_element_type=F32)
     sigma = jax.nn.sigmoid(pre)
@@ -147,18 +170,27 @@
 
 
 def second_kernel(
-    odd_ref, rule_ref, state_ref, near_ref, far_ref, w1_ref, w2_ref, x_ref, g_ref,
+    odd_ref, near_ref, far_ref, state_ref, rule_hbm, x_hbm, g_hbm, w1_hbm, w2_hbm,
     out_ref, dx_ref,
     table_ref, hs_ref, ds_ref, turned_ref,
+    rule_ref, x_ref, g_ref, w1_ref, w2_ref, sems,
 ):
-    width, rows = x_ref.shape
+    copies = fetch(
+        (rule_hbm, w1_hbm, w2_hbm, x_hbm, g_hbm),
+        (rule_ref, w1_ref, w2_ref, x_ref, g_ref),
+        sems,
+    )
+    _, rows = x_ref.shape
     blocks = rows // BLOCK
     odd = odd_ref[0] == 1
     for block in range(blocks):
         table_ref[block] = state_ref[block]
     fill_halo(table_ref, near_ref, far_ref, odd, blocks)
+    copies[0].wait()
+    gather(table_ref, rule_ref, hs_ref, ds_ref, blocks)
+    for copy in copies[1:]:
+        copy.wait()
     turn(w1_ref, turned_ref)
-    gather(table_ref, rule_ref, hs_ref, ds_ref, blocks)
     second = jnp.dot(w2_ref[...], hs_ref[...], preferred_element_type=F32)
     out_ref[...] = (second + x_ref[...].astype(F32)).astype(BF16)
     d_input = jnp.dot(turned_ref[...], ds_ref[...], preferred_element_type=F32)
@@ -180,7 +212,8 @@
         wire = BF16 if step >= len(bits) - 3 else F32
         pairs = [(i, i ^ (odd_bit if i % 2 else even_bit)) for i in range(count)]
         sent = total.astype(wire)
-        total = sent.astype(F32) + lax.ppermute(sent, "tile", pairs).astype(F32)
+        received = lax.ppermute(sent, "tile", pairs)
+        total = sent.astype(F32) + received.astype(F32)
     total = total * first_scale
     other = lax.ppermute(total, "tile", [(i, i ^ 1) for i in range(count)])
     return jnp.where(odd, other, total), jnp.where(odd, total, other)
@@ -194,6 +227,11 @@
     parity = lax.axis_index("tile") % 2
     odd = parity == 1
     parity = parity.reshape(1).astype(jnp.int32)
+    send_lists = send_lists.reshape(2)
+    features, cotangent, rulebook, weight_first, weight_second, send_lists = (
+        pltpu.with_memory_space_constraint(array, pltpu.HBM)
+        for array in (features, cotangent, rulebook, weight_first, weight_second, send_lists)
+    )
     near_pairs, far_pairs = neighbour_pairs(count)
     shape = jax.ShapeDtypeStruct
     rim = shape((2 * width, BLOCK), BF16)
@@ -201,11 +239,18 @@
     near, far = pl.pallas_call(
         payload_kernel,
         out_shape=(rim, rim),
-        in_specs=[SMEM, SMEM, VMEM, VMEM],
+        in_specs=[HBM, SMEM, HBM, HBM],
         out_specs=(VMEM, VMEM),
+        scratch_shapes=[
+            pltpu.SMEM((2,), jnp.int32),
+            pltpu.VMEM((width, rows), BF16),
+            pltpu.VMEM((width, rows), BF16),
+            pltpu.SemaphoreType.DMA((3,)),
+        ],
+        compiler_params=SMALL,
     )(send_lists, parity, features, cotangent)
+    far = lax.ppermute(far, "tile", far_pairs)
     near = lax.ppermute(near, "tile", near_pairs)
-    far = lax.ppermute(far, "tile", far_pairs)
 
     scratch = [
         pltpu.VMEM((blocks + 2, 2 * width, BLOCK), BF16),
@@ -213,31 +258,45 @@
         pltpu.VMEM((offsets * width, rows), BF16),
         pltpu.VMEM((width, offsets * width), BF16),
     ]
+    inputs = [
+        pltpu.VMEM((offsets, rows), jnp.int32),
+        pltpu.VMEM((width, rows), BF16),
+        pltpu.VMEM((width, rows), BF16),
+        pltpu.VMEM((width, offsets * width), BF16),
+        pltpu.VMEM((width, offsets * width), BF16),
+        pltpu.SemaphoreType.DMA((6,)),
+    ]
+    arrays = (rulebook, features, cotangent, weight_first, weight_second)
     state, near, far, keep, send = pl.pallas_call(
         first_kernel,
         out_shape=(
             shape((blocks, 2 * width, BLOCK), BF16), rim, rim,
             shape((width, offsets * width), F32), shape((width, offsets * width), BF16),
         ),
-        in_specs=[SMEM, SMEM] + [VMEM] * 7,
+        in_specs=[SMEM, VMEM, VMEM] + [HBM] * 6,
         out_specs=(VMEM,) * 5,
-        scratch_shapes=scratch,
-    )(send_lists, parity, rulebook, features, cotangent, near, far, weight_first, weight_second)
+        scratch_shapes=scratch + [pltpu.SMEM((2,), jnp.int32)] + inputs,
+        compiler_params=MEDIUM,
+    )(parity, near, far, send_lists, *arrays)
 
     near = lax.ppermute(near, "tile", near_pairs)
     far = lax.ppermute(far, "tile", far_pairs)
-    out_features, d_features = pl.pallas_call(
+    second_phase = pl.pallas_call(
         second_kernel,
         out_shape=(shape((width, rows), BF16), shape((width, rows), BF16)),
-        in_specs=[SMEM] + [VMEM] * 8,
+        in_specs=[SMEM] + [VMEM] * 3 + [HBM] * 5,
         out_specs=(VMEM, VMEM),
-        scratch_shapes=scratch,
+        scratch_shapes=scratch + inputs,
+        compiler_params=MEDIUM,
         cost_estimate=pl.CostEstimate(
             flops=2 * 2 * width * offsets * rows * (width + BLOCK),
             bytes_accessed=4 * offsets * width * rows,
             transcendentals=0,
         ),
-    )(parity, rulebook, state, near, far, weight_first, weight_second, features, cotangent)
+    )
+    out_features, d_features = second_phase(
+        parity, near, far, state, *arrays
+    )
 
     scale = 1.0 / math.sqrt(rows * count)
     grad_first, grad_second = total_over_tiles(keep, send, odd, scale)
@@ -245,23 +304,11 @@
 
 
 def solution(mesh):
-    placed = (
-        P(None, ("groups", "tile")),
-        P(None, ("groups", "tile")),
-        P(None, ("groups", "tile")),
-        P(),
-        P(),
-        P(None, ("groups", "tile")),
-    )
+    tiles = P(None, ("groups", "tile"))
     return jax.shard_map(
         body,
         mesh=mesh,
-        in_specs=placed,
-        out_specs=(
-            P(None, ("groups", "tile")),
-            P(None, ("groups", "tile")),
-            P("groups", None),
-            P("groups", None),
-        ),
+        in_specs=(tiles, tiles, tiles, P(), P(), tiles),
+        out_specs=(tiles, tiles, P("groups", None), P("groups", None)),
         check_vma=False,
     )

time: 51.6 us -> 46 us (0.89)
  local copies, waits for them, and re-layouts: 2.55 us -> 0 us
  Pallas kernels: 9.46 us -> 7.71 us
  other arithmetic: 2.26 us -> 1.23 us
    unnamed x15 -> x0, local copies, waits for them, and re-layouts: 2.55 us -> none
    convert_element_type x3, other arithmetic: 1.18 us -> 0.15 us  [total_over_tiles(): sent = total.astype(wire)]
    pallas_call x1, Pallas kernels: 4.54 us -> 3.59 us  [body(): pl.pallas_call(first_kernel, out_shape=(shape((blocks, 2 * width, BLOCK),...]
    pallas_call x2, Pallas kernels: 4.92 us -> 4.12 us  [the longest x1 3.26 us: body(): out_features, d_features = second_phase(parity, near, far, state, *arrays)]
where the time goes in v2:
time: 46 us; the launch traced here: 45.7 us
  waiting for transfers between devices  28.6 us (62%)
  Pallas kernels  7.71 us (17%)
  starting transfers between devices  7.47 us (16%)
  other arithmetic  1.23 us (3%)
  between operations  0.74 us (2%)
    ppermute x3, waiting for transfers between devices, total_over_tiles(): received = lax.ppermute(sent, 'tile', pairs)  20.1 us
    ppermute x2, waiting for transfers between devices, body(): far = lax.ppermute(far, 'tile', far_pairs)  7.03 us
    ppermute x2, starting transfers between devices, body(): far = lax.ppermute(far, 'tile', far_pairs)  5.28 us
    pallas_call x1, Pallas kernels, body(): pl.pallas_call(first_kernel, out_shape=(shape((blocks, 2 * width, BLOCK),...  3.59 us
    pallas_call x1, Pallas kernels, body(): out_features, d_features = second_phase(parity, near, far, state, *arrays)  3.26 us
    ppermute x1, waiting for transfers between devices, total_over_tiles(): received = lax.ppermute(send, 'tile', [(i, i ^ 1) for i in range(count)])  1.47 us
    ppermute x3, starting transfers between devices, total_over_tiles(): received = lax.ppermute(sent, 'tile', pairs)  1.47 us
    select_n x1, other arithmetic, total_over_tiles(): return (jnp.where(odd, other, total), jnp.where(odd, total, other))  1.01 us
  transfers between devices with their start and end apart: 9, of which 6 were waited for; matrix products, arithmetic and copies ran while one was open for 0% of the time, Pallas kernels for 7%

profile of v2, /device:TPU:28, one launch (start us, length us, event | category | flops | bytes accessed | tf_op | source)
XLA Modules:
  0.0 45.7 jit_solution(665166596582125106)
XLA Ops:
  0.6 0.9 %shard_map.93 = (bf16[128,128]{1,0:T(8,128)(2,1)S(1)}, bf16[128,128]{1,0:T(8,128)(2,1)S(1)}) custom-call(s32[2]{0:T(128)} %bitcast.2, s32[1]{0:T(128)} %bitcast.odd_ref, bf16[64,384]{1,0:T(8,128)(2,1)} %x_hbm.5, bf16[64,384]{1,0:T(8,128)(2,1)} %g_hbm.5), custom_call_target="tpu_custom_call" | custom-call | tf_op jit(solution)/shard_map/pallas_call | solution.py:239
  1.5 0.1 collective-permute-start
  1.6 3.4 %collective-permute-start.1 = (bf16[128,128]{1,0:T(8,128)(2,1)S(1)}, bf16[128,128]{1,0:T(8,128)(2,1)S(1)}, u32[]{:S(2)}, u32[]{:S(2)}) collective-permute-start(bf16[128,128]{1,0:T(8,128)(2,1)S(1)} %get-tuple-element.14), channel_id=1, source_target_pairs={{1,2},{2,1},{3,4},{4,3},{5,6},{6,5},{7,8},{8,7},{9,10},{10,9},{11,... | collective-permute-start | bytes 98312 | tf_op jit(solution)/shard_map/ppermute | solution.py:252
  5.0 0.0 collective-permute-done.near_ref
  5.0 2.8 %collective-permute-done.1.far_ref = bf16[128,128]{1,0:T(8,128)(2,1)S(1)} collective-permute-done((bf16[128,128]{1,0:T(8,128)(2,1)S(1)}, bf16[128,128]{1,0:T(8,128)(2,1)S(1)}, u32[]{:S(2)}, u32[]{:S(2)}) %collective-permute-start.1) | collective-permute-done | bytes 32800 | tf_op jit(solution)/shard_map/ppermute | solution.py:252
  7.8 3.6 %shard_map.94 = (bf16[3,128,128]{2,1,0:T(8,128)(2,1)S(1)}, bf16[128,128]{1,0:T(8,128)(2,1)S(1)}, bf16[128,128]{1,0:T(8,128)(2,1)S(1)}, f32[64,1728]{1,0:T(8,128)S(1)}, bf16[64,1728]{1,0:T(8,128)(2,1)S(1)}) custom-call(s32[1]{0:T(128)} %bitcast.odd_ref, bf16[128,128]{1,0:T(8,128)(2,1)S(1)} %collective-permute-done.near_ref, ...), custom_call_target="tpu_custom_call" | custom-call | tf_op jit(solution)/shard_map/pallas_call | solution.py:270
  11.4 0.1 collective-permute-start.4
  11.5 1.5 %collective-permute-done.4 = bf16[64,1728]{1,0:T(8,128)(2,1)S(1)} collective-permute-done((bf16[64,1728]{1,0:T(8,128)(2,1)S(1)}, bf16[64,1728]{1,0:T(8,128)(2,1)S(1)}, u32[]{:S(2)}, u32[]{:S(2)}) %collective-permute-start.4) | collective-permute-done | bytes 221216 | tf_op jit(solution)/shard_map/ppermute | solution.py:208
  13.0 0.6 %collective-permute-start.5 = (bf16[64,1728]{1,0:T(8,128)(2,1)S(1)}, bf16[64,1728]{1,0:T(8,128)(2,1)S(1)}, u32[]{:S(2)}, u32[]{:S(2)}) collective-permute-start(bf16[64,1728]{1,0:T(8,128)(2,1)S(1)} %add_convert_fusion.2), channel_id=1, source_target_pairs={{0,2},{1,9},{2,0},{3,11},{4,6},{5,13},{6,4},{7,15},{8,10},{9,1},{1... | collective-permute-start | bytes 663560 | tf_op jit(solution)/shard_map/ppermute | solution.py:215
  13.6 5.5 %collective-permute-done.5 = bf16[64,1728]{1,0:T(8,128)(2,1)S(1)} collective-permute-done((bf16[64,1728]{1,0:T(8,128)(2,1)S(1)}, bf16[64,1728]{1,0:T(8,128)(2,1)S(1)}, u32[]{:S(2)}, u32[]{:S(2)}) %collective-permute-start.5) | collective-permute-done | bytes 221216 | tf_op jit(solution)/shard_map/ppermute | solution.py:215
  19.1 0.1 add_convert_fusion.1
  19.2 0.5 %collective-permute-start.6 = (bf16[64,1728]{1,0:T(8,128)(2,1)S(1)}, bf16[64,1728]{1,0:T(8,128)(2,1)S(1)}, u32[]{:S(2)}, u32[]{:S(2)}) collective-permute-start(bf16[64,1728]{1,0:T(8,128)(2,1)S(1)} %add_convert_fusion.1), channel_id=1, source_target_pairs={{0,4},{1,3},{2,6},{3,1},{4,0},{5,7},{6,2},{7,5},{8,12},{9,11},{10,... | collective-permute-start | bytes 663560 | tf_op jit(solution)/shard_map/ppermute | solution.py:215
  19.7 5.6 %collective-permute-done.6 = bf16[64,1728]{1,0:T(8,128)(2,1)S(1)} collective-permute-done((bf16[64,1728]{1,0:T(8,128)(2,1)S(1)}, bf16[64,1728]{1,0:T(8,128)(2,1)S(1)}, u32[]{:S(2)}, u32[]{:S(2)}) %collective-permute-start.6) | collective-permute-done | bytes 221216 | tf_op jit(solution)/shard_map/ppermute | solution.py:215
  25.3 0.1 add_convert_fusion
  25.3 0.4 collective-permute-start.7
  25.7 9.0 %collective-permute-done.7 = bf16[64,1728]{1,0:T(8,128)(2,1)S(1)} collective-permute-done((bf16[64,1728]{1,0:T(8,128)(2,1)S(1)}, bf16[64,1728]{1,0:T(8,128)(2,1)S(1)}, u32[]{:S(2)}, u32[]{:S(2)}) %collective-permute-start.7) | collective-permute-done | bytes 221216 | tf_op jit(solution)/shard_map/ppermute | solution.py:215
  34.7 0.1 add_multiply_fusion
  34.8 0.1 collective-permute-start.8
  34.8 0.5 %collective-permute-start.2 = (bf16[128,128]{1,0:T(8,128)(2,1)S(1)}, bf16[128,128]{1,0:T(8,128)(2,1)S(1)}, u32[]{:S(2)}, u32[]{:S(2)}) collective-permute-start(bf16[128,128]{1,0:T(8,128)(2,1)S(1)} %get-tuple-element.15), channel_id=1, source_target_pairs={{0,1},{1,0},{2,3},{3,2},{4,5},{5,4},{6,7},{7,6},{8,9},{9,8},{10,11... | collective-permute-start | bytes 98312 | tf_op jit(solution)/shard_map/ppermute | solution.py:282
  35.3 1.9 %collective-permute-start.3 = (bf16[128,128]{1,0:T(8,128)(2,1)S(1)}, bf16[128,128]{1,0:T(8,128)(2,1)S(1)}, u32[]{:S(2)}, u32[]{:S(2)}) collective-permute-start(bf16[128,128]{1,0:T(8,128)(2,1)S(1)} %get-tuple-element.16), channel_id=1, source_target_pairs={{1,2},{2,1},{3,4},{4,3},{5,6},{6,5},{7,8},{8,7},{9,10},{10,9},{11,... | collective-permute-start | bytes 98312 | tf_op jit(solution)/shard_map/ppermute | solution.py:283
  37.3 0.0 collective-permute-done.2.near_ref
  37.3 4.2 %collective-permute-done.3.far_ref = bf16[128,128]{1,0:T(8,128)(2,1)S(1)} collective-permute-done((bf16[128,128]{1,0:T(8,128)(2,1)S(1)}, bf16[128,128]{1,0:T(8,128)(2,1)S(1)}, u32[]{:S(2)}, u32[]{:S(2)}) %collective-permute-start.3) | collective-permute-done | bytes 32800 | tf_op jit(solution)/shard_map/ppermute | solution.py:283
  41.5 3.3 %shard_map.95 = (bf16[64,384]{1,0:T(8,128)(2,1)}, bf16[64,384]{1,0:T(8,128)(2,1)}) custom-call(s32[1]{0:T(128)} %bitcast.odd_ref, bf16[128,128]{1,0:T(8,128)(2,1)S(1)} %collective-permute-done.2.near_ref, bf16[128,128]{1,0:T(8,128)(2,1)S(1)} %collective-permute-done.3.far_ref, bf16[3,128,128]{2,1,0:T(8,128)(2,1)S(1)} %get-tuple-element.17.state_ref, ...), custom_call_target="tpu_custom_call" | custom-call | flops 509607936 | bytes 2654208 | tf_op jit(solution)/shard_map/pallas_call | solution.py:297
  44.7 0.0 collective-permute-done.8
  44.7 1.0 %broadcast_select_fusion = (f32[64,1728]{1,0:T(8,128)}, f32[64,1728]{1,0:T(8,128)}) fusion(f32[64,1728]{1,0:T(8,128)S(1)} %collective-permute-done.8, pred[]{:T(512)S(6)} %eq.5, bf16[64,1728]{1,0:T(8,128)(2,1)S(1)} %collective-permute-done.7, bf16[64,1728]{1,0:T(8,128)(2,1)S(1)} %add_convert_fusion), kind=kLoop, calls=%fused_computation.4 | loop fusion | flops 663552 | bytes 1769473 | tf_op jit(solution)/shard_map/jit(_where)/select_n | solution.py:219
  (1 shorter events, 0.0 us)
Async XLA Ops:
  1.5 3.5 %collective-permute-start = (bf16[128,128]{1,0:T(8,128)(2,1)S(1)}, bf16[128,128]{1,0:T(8,128)(2,1)S(1)}, u32[]{:S(2)}, u32[]{:S(2)}) collective-permute-start(bf16[128,128]{1,0:T(8,128)(2,1)S(1)} %get-tuple-element.13), channel_id=1, source_target_pairs={{0,1},{1,0},{2,3},{3,2},{4,5},{5,4},{6,7},{7,6},{8,9},{9,8},{10,11... | collective-permute-start | bytes 98312 | tf_op jit(solution)/shard_map/ppermute | solution.py:253
  1.6 6.2 %collective-permute-start.1 = (bf16[128,128]{1,0:T(8,128)(2,1)S(1)}, bf16[128,128]{1,0:T(8,128)(2,1)S(1)}, u32[]{:S(2)}, u32[]{:S(2)}) collective-permute-start(bf16[128,128]{1,0:T(8,128)(2,1)S(1)} %get-tuple-element.14), channel_id=1, source_target_pairs={{1,2},{2,1},{3,4},{4,3},{5,6},{6,5},{7,8},{8,7},{9,10},{10,9},{11,... | collective-permute-start | bytes 98312 | tf_op jit(solution)/shard_map/ppermute | solution.py:252
  11.4 1.6 %collective-permute-start.4 = (bf16[64,1728]{1,0:T(8,128)(2,1)S(1)}, bf16[64,1728]{1,0:T(8,128)(2,1)S(1)}, u32[]{:S(2)}, u32[]{:S(2)}) collective-permute-start(bf16[64,1728]{1,0:T(8,128)(2,1)S(1)} %get-tuple-element.21), channel_id=1, source_target_pairs={{0,1},{1,0},{2,3},{3,2},{4,5},{5,4},{6,7},{7,6},{8,9},{9,8},{10,11... | collective-permute-start | bytes 663560 | tf_op jit(solution)/shard_map/ppermute | solution.py:208
  13.0 6.1 %collective-permute-start.5 = (bf16[64,1728]{1,0:T(8,128)(2,1)S(1)}, bf16[64,1728]{1,0:T(8,128)(2,1)S(1)}, u32[]{:S(2)}, u32[]{:S(2)}) collective-permute-start(bf16[64,1728]{1,0:T(8,128)(2,1)S(1)} %add_convert_fusion.2), channel_id=1, source_target_pairs={{0,2},{1,9},{2,0},{3,11},{4,6},{5,13},{6,4},{7,15},{8,10},{9,1},{1... | collective-permute-start | bytes 663560 | tf_op jit(solution)/shard_map/ppermute | solution.py:215
  19.2 6.1 %collective-permute-start.6 = (bf16[64,1728]{1,0:T(8,128)(2,1)S(1)}, bf16[64,1728]{1,0:T(8,128)(2,1)S(1)}, u32[]{:S(2)}, u32[]{:S(2)}) collective-permute-start(bf16[64,1728]{1,0:T(8,128)(2,1)S(1)} %add_convert_fusion.1), channel_id=1, source_target_pairs={{0,4},{1,3},{2,6},{3,1},{4,0},{5,7},{6,2},{7,5},{8,12},{9,11},{10,... | collective-permute-start | bytes 663560 | tf_op jit(solution)/shard_map/ppermute | solution.py:215
  25.3 9.4 %collective-permute-start.7 = (bf16[64,1728]{1,0:T(8,128)(2,1)S(1)}, bf16[64,1728]{1,0:T(8,128)(2,1)S(1)}, u32[]{:S(2)}, u32[]{:S(2)}) collective-permute-start(bf16[64,1728]{1,0:T(8,128)(2,1)S(1)} %add_convert_fusion), channel_id=1, source_target_pairs={{0,8},{1,5},{2,10},{3,7},{4,12},{5,1},{6,14},{7,3},{8,0},{9,13},{1... | collective-permute-start | bytes 663560 | tf_op jit(solution)/shard_map/ppermute | solution.py:215
  34.8 10.0 %collective-permute-start.8 = (f32[64,1728]{1,0:T(8,128)S(1)}, f32[64,1728]{1,0:T(8,128)S(1)}, u32[]{:S(2)}, u32[]{:S(2)}) collective-permute-start(f32[64,1728]{1,0:T(8,128)S(1)} %add_multiply_fusion), channel_id=1, source_target_pairs={{0,1},{1,0},{2,3},{3,2},{4,5},{5,4},{6,7},{7,6},{8,9},{9,8},{10,11... | collective-permute-start | bytes 1327112 | tf_op jit(solution)/shard_map/ppermute | solution.py:218
  34.8 2.4 %collective-permute-start.2 = (bf16[128,128]{1,0:T(8,128)(2,1)S(1)}, bf16[128,128]{1,0:T(8,128)(2,1)S(1)}, u32[]{:S(2)}, u32[]{:S(2)}) collective-permute-start(bf16[128,128]{1,0:T(8,128)(2,1)S(1)} %get-tuple-element.15), channel_id=1, source_target_pairs={{0,1},{1,0},{2,3},{3,2},{4,5},{5,4},{6,7},{7,6},{8,9},{9,8},{10,11... | collective-permute-start | bytes 98312 | tf_op jit(solution)/shard_map/ppermute | solution.py:282
  35.3 6.1 %collective-permute-start.3 = (bf16[128,128]{1,0:T(8,128)(2,1)S(1)}, bf16[128,128]{1,0:T(8,128)(2,1)S(1)}, u32[]{:S(2)}, u32[]{:S(2)}) collective-permute-start(bf16[128,128]{1,0:T(8,128)(2,1)S(1)} %get-tuple-element.16), channel_id=1, source_target_pairs={{1,2},{2,1},{3,4},{4,3},{5,6},{6,5},{7,8},{8,7},{9,10},{10,9},{11,... | collective-permute-start | bytes 98312 | tf_op jit(solution)/shard_map/ppermute | solution.py:283

commit v3 on v2

--- a/solution.py
+++ b/solution.py
@@ -14,8 +14,11 @@
 SMALL = pltpu.CompilerParams(vmem_limit_bytes=1 << 20)
 MEDIUM = pltpu.CompilerParams(vmem_limit_bytes=20 << 20)
 VMEM = pl.BlockSpec(memory_space=pltpu.VMEM)
-SMEM = pl.BlockSpec(memory_space=pltpu.SMEM)
 NT = (((1,), (1,)), ((), ()))
+
+
+def is_odd():
+    return lax.axis_index("tile") % 2 == 1
 
 
 def pair_blocks(lists_ref, odd):
@@ -34,13 +37,13 @@
 
 
 def payload_kernel(
-    lists_hbm, odd_ref, x_hbm, g_hbm, near_ref, far_ref, lists_ref, x_ref, g_ref, sems
+    lists_hbm, x_hbm, g_hbm, near_ref, far_ref, lists_ref, x_ref, g_ref, sems
 ):
     width, rows = x_ref.shape
     copies = fetch((lists_hbm, x_hbm, g_hbm), (lists_ref, x_ref, g_ref), sems)
     for copy in copies:
         copy.wait()
-    picks = pair_blocks(lists_ref, odd_ref[0] == 1)
+    picks = pair_blocks(lists_ref, is_odd())
     for pick, out_ref in zip(picks, (near_ref, far_ref)):
         start = pl.multiple_of(jnp.minimum(pick, rows // BLOCK - 1) * BLOCK, BLOCK)
         out_ref[:width, :] = x_ref[:, pl.ds(start, BLOCK)]
@@ -51,6 +54,10 @@
     near, far = near_ref[...], far_ref[...]
     table_ref[blocks] = jnp.where(odd, near, far)
     table_ref[blocks + 1] = jnp.where(odd, far, near)
+
+
+def one_hot(rows, line):
+    return (rows == line).astype(F32).astype(BF16)
 
 
 def gather(table_ref, rule_ref, first_ref, second_ref, blocks):
@@ -84,7 +91,7 @@
             table = table_ref[source]
             for j in range(group):
                 k = side * group + j
-                choice = (source_rows == local[j : j + 1]).astype(F32).astype(BF16)
+                choice = one_hot(source_rows, local[j : j + 1])
                 found = jnp.dot(table, choice, preferred_element_type=F32)
                 store(k, low, high, found, offsets - 1 - k)
 
@@ -97,7 +104,7 @@
             line = rule_ref[pl.ds(k, 1), :]
             found = jnp.zeros((channels, rows), F32)
             for source in range(sources):
-                choice = (every_row == line - source * BLOCK).astype(F32).astype(BF16)
+                choice = one_hot(every_row, line - source * BLOCK)
                 found += jnp.dot(table_ref[source], choice, preferred_element_type=F32)
             here = pl.multiple_of(k * width, width)
             there = pl.multiple_of((offsets - 1 - k) * width, width)
@@ -119,58 +126,122 @@
         turned_ref[:, k * width : (k + count) * width] = joined.astype(BF16)
 
 
-def first_kernel(
-    odd_ref, near_ref, far_ref, lists_hbm, rule_hbm, x_hbm, g_hbm, w1_hbm, w2_hbm,
-    state_ref, near_out, far_out, keep_ref, send_ref,
-    table_ref, xs_ref, gs_ref, turned_ref,
-    lists_ref, rule_ref, x_ref, g_ref, w1_ref, w2_ref, sems,
+def own_kernel(
+    rule_hbm, x_hbm, g_hbm, w1_hbm, w2_hbm,
+    xs_ref, gs_ref, pre_ref, d_hidden_ref, rule_ref, w1_ref, turned_ref,
+    table_ref, x_ref, g_ref, w2_ref, sems,
 ):
     copies = fetch(
-        (lists_hbm, rule_hbm, x_hbm, g_hbm, w2_hbm, w1_hbm),
-        (lists_ref, rule_ref, x_ref, g_ref, w2_ref, w1_ref),
-        sems,
+        (rule_hbm, x_hbm, g_hbm, w2_hbm, w1_hbm), (rule_ref, x_ref, g_ref, w2_ref, w1_ref), sems
     )
     width, rows = x_ref.shape
     blocks = rows // BLOCK
-    offsets = rule_ref.shape[0]
-    odd = odd_ref[0] == 1
-    for copy in copies[:4]:
+    for copy in copies[:3]:
         copy.wait()
     for block in range(blocks):
         low, high = block * BLOCK, (block + 1) * BLOCK
         table_ref[block, :width] = x_ref[:, low:high]
         table_ref[block, width:] = g_ref[:, low:high]
-    fill_halo(table_ref, near_ref, far_ref, odd, blocks)
+    table_ref[blocks:] = jnp.zeros_like(table_ref[blocks:])
     gather(table_ref, rule_ref, xs_ref, gs_ref, blocks)
-    for copy in copies[4:]:
+    for copy in copies[3:]:
         copy.wait()
     turn(w2_ref, turned_ref)
-    pre = jnp.dot(w1_ref[...], xs_ref[...], preferred_element_type=F32)
-    d_hidden = jnp.dot(turned_ref[...], gs_ref[...], preferred_element_type=F32)
+    pre_ref[...] = jnp.dot(w1_ref[...], xs_ref[...], preferred_element_type=F32)
+    d_hidden_ref[...] = jnp.dot(turned_ref[...], gs_ref[...], preferred_element_type=F32)
+
+
+def rim_kernel(
+    lists_hbm, near_ref, far_ref, xs_ref, gs_ref, pre_in, d_hidden_in, rule_ref, w1_ref, turned_ref,
+    state_ref, near_out, far_out, keep_ref, send_ref,
+    pre_ref, d_hidden_ref, rim_x_ref, rim_g_ref, lists_ref, sems,
+):
+    copies = fetch((lists_hbm,), (lists_ref,), sems)
+    width, rows = pre_in.shape
+    blocks = rows // BLOCK
+    offsets = rule_ref.shape[0]
+    group = offsets // 3
+    odd = is_odd()
+    near, far = near_ref[...], far_ref[...]
+    tables = (jnp.where(odd, near, far), jnp.where(odd, far, near))
+    pre_ref[...] = pre_in[...]
+    d_hidden_ref[...] = d_hidden_in[...]
+    source_rows = lax.broadcasted_iota(jnp.int32, (BLOCK, BLOCK), 0)
+    copies[0].wait()
+    sides = []
+    for side in range(2):
+        block = jnp.minimum(lists_ref[side], blocks - 1)
+        columns = pl.ds(pl.multiple_of(block * BLOCK, BLOCK), BLOCK)
+        start = 2 * side * group
+        mirrored = offsets - group - start
+        local = rule_ref[start : start + group, columns] - (blocks + side) * BLOCK
+        for j in range(group):
+            found = jnp.dot(
+                tables[side], one_hot(source_rows, local[j : j + 1]), preferred_element_type=F32
+            )
+            rim_x_ref[side, j * width : (j + 1) * width] = found[:width].astype(BF16)
+            place = (group - 1 - j) * width
+            rim_g_ref[side, place : place + width] = found[width:].astype(BF16)
+        span = slice(start * width, (start + group) * width)
+        mirror_span = slice(mirrored * width, (mirrored + group) * width)
+        pre_ref[:, columns] += jnp.dot(
+            w1_ref[:, span], rim_x_ref[side], preferred_element_type=F32
+        )
+        d_hidden_ref[:, columns] += jnp.dot(
+            turned_ref[:, mirror_span], rim_g_ref[side], preferred_element_type=F32
+        )
+        sides.append((block, start, mirrored))
+    pre = pre_ref[...]
     sigma = jax.nn.sigmoid(pre)
     hidden = (pre * sigma).astype(BF16)
-    d_pre = (d_hidden * sigma * (1.0 + pre * (1.0 - sigma))).astype(BF16)
+    d_pre = (d_hidden_ref[...] * sigma * (1.0 + pre * (1.0 - sigma))).astype(BF16)
     for block in range(blocks):
         low, high = block * BLOCK, (block + 1) * BLOCK
         state_ref[block, :width] = hidden[:, low:high]
         state_ref[block, width:] = d_pre[:, low:high]
     for pick, out_ref in zip(pair_blocks(lists_ref, odd), (near_out, far_out)):
-        piece = state_ref[jnp.minimum(pick, blocks - 1)]
-        out_ref[...] = jnp.where(pick < blocks, piece, jnp.zeros_like(piece))
+        out_ref[...] = state_ref[jnp.minimum(pick, blocks - 1)]
     grad_first = lax.dot_general(d_pre, xs_ref[...], NT, preferred_element_type=F32)
     stacked = lax.dot_general(gs_ref[...], hidden, NT, preferred_element_type=F32)
+    rims = [
+        (
+            lax.dot_general(
+                state_ref[block, width:], rim_x_ref[side], NT, preferred_element_type=F32
+            ),
+            lax.dot_general(
+                rim_g_ref[side], state_ref[block, :width], NT, preferred_element_type=F32
+            ),
+        )
+        for side, (block, _, _) in enumerate(sides)
+    ]
+
+    def first_of(k):
+        term = grad_first[:, k * width : (k + 1) * width]
+        for (rim, _), (_, start, _) in zip(rims, sides):
+            if start <= k < start + group:
+                term = term + rim[:, (k - start) * width : (k - start + 1) * width]
+        return term
+
+    def second_of(k):
+        term = stacked[k * width : (k + 1) * width]
+        for (_, rim), (_, _, mirrored) in zip(rims, sides):
+            if mirrored <= k < mirrored + group:
+                term = term + rim[(k - mirrored) * width : (k - mirrored + 1) * width]
+        return term
+
     for k in range(0, offsets, 2):
         count = min(2, offsets - k)
         low, high = k * width, (k + count) * width
-        pieces = [stacked[low + i * width : low + (i + 1) * width] for i in range(count)]
-        second = pieces[0] if count == 1 else jnp.concatenate(pieces, axis=1)
-        first = grad_first[:, low:high]
+        first = [first_of(k + i) for i in range(count)]
+        second = [second_of(k + i) for i in range(count)]
+        first = first[0] if count == 1 else jnp.concatenate(first, axis=1)
+        second = second[0] if count == 1 else jnp.concatenate(second, axis=1)
         keep_ref[:, low:high] = jnp.where(odd, second, first)
         send_ref[:, low:high] = jnp.where(odd, first, second).astype(BF16)
 
 
 def second_kernel(
-    odd_ref, near_ref, far_ref, state_ref, rule_hbm, x_hbm, g_hbm, w1_hbm, w2_hbm,
+    near_ref, far_ref, state_ref, rule_hbm, x_hbm, g_hbm, w1_hbm, w2_hbm,
     out_ref, dx_ref,
     table_ref, hs_ref, ds_ref, turned_ref,
     rule_ref, x_ref, g_ref, w1_ref, w2_ref, sems,
@@ -182,7 +253,7 @@
     )
     _, rows = x_ref.shape
     blocks = rows // BLOCK
-    odd = odd_ref[0] == 1
+    odd = is_odd()
     for block in range(blocks):
         table_ref[block] = state_ref[block]
     fill_halo(table_ref, near_ref, far_ref, odd, blocks)
@@ -224,9 +295,7 @@
     offsets = rulebook.shape[0]
     blocks = rows // BLOCK
     count = lax.axis_size("tile")
-    parity = lax.axis_index("tile") % 2
-    odd = parity == 1
-    parity = parity.reshape(1).astype(jnp.int32)
+    odd = is_odd()
     send_lists = send_lists.reshape(2)
     features, cotangent, rulebook, weight_first, weight_second, send_lists = (
         pltpu.with_memory_space_constraint(array, pltpu.HBM)
@@ -239,7 +308,7 @@
     near, far = pl.pallas_call(
         payload_kernel,
         out_shape=(rim, rim),
-        in_specs=[HBM, SMEM, HBM, HBM],
+        in_specs=[HBM, HBM, HBM],
         out_specs=(VMEM, VMEM),
         scratch_shapes=[
             pltpu.SMEM((2,), jnp.int32),
@@ -248,45 +317,25 @@
             pltpu.SemaphoreType.DMA((3,)),
         ],
         compiler_params=SMALL,
-    )(send_lists, parity, features, cotangent)
+    )(send_lists, features, cotangent)
     far = lax.ppermute(far, "tile", far_pairs)
     near = lax.ppermute(near, "tile", near_pairs)
 
-    scratch = [
-        pltpu.VMEM((blocks + 2, 2 * width, BLOCK), BF16),
-        pltpu.VMEM((offsets * width, rows), BF16),
-        pltpu.VMEM((offsets * width, rows), BF16),
-        pltpu.VMEM((width, offsets * width), BF16),
-    ]
-    inputs = [
-        pltpu.VMEM((offsets, rows), jnp.int32),
-        pltpu.VMEM((width, rows), BF16),
-        pltpu.VMEM((width, rows), BF16),
-        pltpu.VMEM((width, offsets * width), BF16),
-        pltpu.VMEM((width, offsets * width), BF16),
-        pltpu.SemaphoreType.DMA((6,)),
-    ]
+    table = pltpu.VMEM((blocks + 2, 2 * width, BLOCK), BF16)
+    rows_of_tile = pltpu.VMEM((width, rows), BF16)
+    weight = pltpu.VMEM((width, offsets * width), BF16)
     arrays = (rulebook, features, cotangent, weight_first, weight_second)
-    state, near, far, keep, send = pl.pallas_call(
-        first_kernel,
+    own_phase = pl.pallas_call(
+        own_kernel,
         out_shape=(
-            shape((blocks, 2 * width, BLOCK), BF16), rim, rim,
-            shape((width, offsets * width), F32), shape((width, offsets * width), BF16),
+            shape((offsets * width, rows), BF16), shape((offsets * width, rows), BF16),
+            shape((width, rows), F32), shape((width, rows), F32),
+            shape(rulebook.shape, jnp.int32), shape(weight_first.shape, BF16),
+            shape(weight_first.shape, BF16),
         ),
-        in_specs=[SMEM, VMEM, VMEM] + [HBM] * 6,
-        out_specs=(VMEM,) * 5,
-        scratch_shapes=scratch + [pltpu.SMEM((2,), jnp.int32)] + inputs,
-        compiler_params=MEDIUM,
-    )(parity, near, far, send_lists, *arrays)
-
-    near = lax.ppermute(near, "tile", near_pairs)
-    far = lax.ppermute(far, "tile", far_pairs)
-    second_phase = pl.pallas_call(
-        second_kernel,
-        out_shape=(shape((width, rows), BF16), shape((width, rows), BF16)),
-        in_specs=[SMEM] + [VMEM] * 3 + [HBM] * 5,
-        out_specs=(VMEM, VMEM),
-        scratch_shapes=scratch + inputs,
+        in_specs=[HBM] * 5,
+        out_specs=(VMEM,) * 7,
+        scratch_shapes=[table, rows_of_tile, rows_of_tile, weight, pltpu.SemaphoreType.DMA((5,))],
         compiler_params=MEDIUM,
         cost_estimate=pl.CostEstimate(
             flops=2 * 2 * width * offsets * rows * (width + BLOCK),
@@ -294,8 +343,51 @@
             transcendentals=0,
         ),
     )
+    own = own_phase(*arrays)
+    state, near, far, keep, send = pl.pallas_call(
+        rim_kernel,
+        out_shape=(
+            shape((blocks, 2 * width, BLOCK), BF16), rim, rim,
+            shape((width, offsets * width), F32), shape((width, offsets * width), BF16),
+        ),
+        in_specs=[HBM] + [VMEM] * 9,
+        out_specs=(VMEM,) * 5,
+        scratch_shapes=[
+            pltpu.VMEM((width, rows), F32),
+            pltpu.VMEM((width, rows), F32),
+            pltpu.VMEM((2, offsets // 3 * width, BLOCK), BF16),
+            pltpu.VMEM((2, offsets // 3 * width, BLOCK), BF16),
+            pltpu.SMEM((2,), jnp.int32),
+            pltpu.SemaphoreType.DMA((1,)),
+        ],
+        compiler_params=MEDIUM,
+    )(send_lists, near, far, *own)
+
+    near = lax.ppermute(near, "tile", near_pairs)
+    far = lax.ppermute(far, "tile", far_pairs)
+    second_phase = pl.pallas_call(
+        second_kernel,
+        out_shape=(shape((width, rows), BF16), shape((width, rows), BF16)),
+        in_specs=[VMEM] * 3 + [HBM] * 5,
+        out_specs=(VMEM, VMEM),
+        scratch_shapes=[
+            table,
+            pltpu.VMEM((offsets * width, rows), BF16),
+            pltpu.VMEM((offsets * width, rows), BF16),
+            weight,
+            pltpu.VMEM(rulebook.shape, jnp.int32),
+            rows_of_tile, rows_of_tile, weight, weight,
+            pltpu.SemaphoreType.DMA((5,)),
+        ],
+        compiler_params=MEDIUM,
+        cost_estimate=pl.CostEstimate(
+            flops=2 * 2 * width * offsets * rows * (width + BLOCK),
+            bytes_accessed=4 * offsets * width * rows,
+            transcendentals=0,
+        ),
+    )
     out_features, d_features = second_phase(
-        parity, near, far, state, *arrays
+        near, far, state, *arrays
     )
 
     scale = 1.0 / math.sqrt(rows * count)

time: 46 us -> 44.8 us (0.974)
  waiting for transfers between devices: 28.6 us -> 25.8 us
  Pallas kernels: 7.71 us -> 9.21 us
    ppermute x2, waiting for transfers between devices: 7.03 us -> 4.32 us  [body(): far = lax.ppermute(far, 'tile', far_pairs)]
    pallas_call x3 -> x4, Pallas kernels: 7.71 us -> 9.21 us  [the longest x1 3.24 us: body(): out_features, d_features = second_phase(near, far, state, *arrays)]
  transfers between devices with their start and end apart: 9 -> 9, of which waited for: 6 -> 6; matrix products, arithmetic and copies ran while one was open for 0% -> 0% of each run, Pallas kernels for 7% -> 13%
where the time goes in v3:
time: 44.8 us; the launch traced here: 44.6 us
  waiting for transfers between devices  25.8 us (58%)
  Pallas kernels  9.21 us (21%)
  starting transfers between devices  7.54 us (17%)
  other arithmetic  1.24 us (3%)
  between operations  0.75 us (2%)
    ppermute x3, waiting for transfers between devices, total_over_tiles(): received = lax.ppermute(sent, 'tile', pairs)  20 us
    ppermute x2, starting transfers between devices, body(): far = lax.ppermute(far, 'tile', far_pairs)  5.28 us
    ppermute x2, waiting for transfers between devices, body(): far = lax.ppermute(far, 'tile', far_pairs)  4.32 us
    pallas_call x1, Pallas kernels, body(): out_features, d_features = second_phase(near, far, state, *arrays)  3.24 us
    pallas_call x1, Pallas kernels, body(): own = own_phase(*arrays)  2.69 us
    pallas_call x1, Pallas kernels, body(): pl.pallas_call(rim_kernel, out_shape=(shape((blocks, 2 * width, BLOCK), B...  2.41 us
    ppermute x3, starting transfers between devices, total_over_tiles(): received = lax.ppermute(sent, 'tile', pairs)  1.53 us
    ppermute x1, waiting for transfers between devices, total_over_tiles(): received = lax.ppermute(send, 'tile', [(i, i ^ 1) for i in range(count)])  1.46 us
  transfers between devices with their start and end apart: 9, of which 6 were waited for; matrix products, arithmetic and copies ran while one was open for 0% of the time, Pallas kernels for 13%

profile of v3, /device:TPU:28, one launch (start us, length us, event | category | flops | bytes accessed | tf_op | source)
XLA Modules:
  0.0 44.6 jit_solution(3552624151654633690)
XLA Ops:
  0.6 0.9 %shard_map.93 = (bf16[128,128]{1,0:T(8,128)(2,1)S(1)}, bf16[128,128]{1,0:T(8,128)(2,1)S(1)}) custom-call(s32[2]{0:T(128)} %bitcast.1, bf16[64,384]{1,0:T(8,128)(2,1)} %x_hbm.5, bf16[64,384]{1,0:T(8,128)(2,1)} %g_hbm.5), custom_call_target="tpu_custom_call" | custom-call | tf_op jit(solution)/shard_map/pallas_call | solution.py:308
  1.5 0.1 collective-permute-start
  1.6 3.4 %collective-permute-start.1 = (bf16[128,128]{1,0:T(8,128)(2,1)S(1)}, bf16[128,128]{1,0:T(8,128)(2,1)S(1)}, u32[]{:S(2)}, u32[]{:S(2)}) collective-permute-start(bf16[128,128]{1,0:T(8,128)(2,1)S(1)} %get-tuple-element.21), channel_id=1, source_target_pairs={{1,2},{2,1},{3,4},{4,3},{5,6},{6,5},{7,8},{8,7},{9,10},{10,9},{11,... | collective-permute-start | bytes 98312 | tf_op jit(solution)/shard_map/ppermute | solution.py:321
  5.0 2.7 %shard_map.94 = (bf16[1728,384]{1,0:T(8,128)(2,1)S(1)}, bf16[1728,384]{1,0:T(8,128)(2,1)S(1)}, f32[64,384]{1,0:T(8,128)S(1)}, f32[64,384]{1,0:T(8,128)S(1)}, s32...) custom-call(s32[27,384]{1,0:T(8,128)} %rule_hbm.3, bf16[64,384]{1,0:T(8,128)(2,1)} %x_hbm.5, ...), custom_call_target="tpu_custom_call" | custom-call | flops 509607936 | bytes 2654208 | tf_op jit(solution)/shard_map/pallas_call | solution.py:346
  7.7 0.0 collective-permute-done.near_ref
  7.7 0.1 collective-permute-done.1.far_ref
  7.8 2.4 %shard_map.95 = (bf16[3,128,128]{2,1,0:T(8,128)(2,1)S(1)}, bf16[128,128]{1,0:T(8,128)(2,1)S(1)}, bf16[128,128]{1,0:T(8,128)(2,1)S(1)}, f32[64,1728]{1,0:T(8,128)S(1)}, bf16[64,1728]{1,0:T(8,128)(2,1)S(1)}) custom-call(s32[2]{0:T(128)} %bitcast.2, bf16[128,128]{1,0:T(8,128)(2,1)S(1)} %collective-permute-done.near_ref, ...), custom_call_target="tpu_custom_call" | custom-call | tf_op jit(solution)/shard_map/pallas_call | solution.py:347
  10.2 0.1 collective-permute-start.4
  10.3 1.5 %collective-permute-done.4 = bf16[64,1728]{1,0:T(8,128)(2,1)S(1)} collective-permute-done((bf16[64,1728]{1,0:T(8,128)(2,1)S(1)}, bf16[64,1728]{1,0:T(8,128)(2,1)S(1)}, u32[]{:S(2)}, u32[]{:S(2)}) %collective-permute-start.4) | collective-permute-done | bytes 221216 | tf_op jit(solution)/shard_map/ppermute | solution.py:279
  11.8 0.1 add_convert_fusion.2
  11.8 0.6 %collective-permute-start.5 = (bf16[64,1728]{1,0:T(8,128)(2,1)S(1)}, bf16[64,1728]{1,0:T(8,128)(2,1)S(1)}, u32[]{:S(2)}, u32[]{:S(2)}) collective-permute-start(bf16[64,1728]{1,0:T(8,128)(2,1)S(1)} %add_convert_fusion.2), channel_id=1, source_target_pairs={{0,2},{1,9},{2,0},{3,11},{4,6},{5,13},{6,4},{7,15},{8,10},{9,1},{1... | collective-permute-start | bytes 663560 | tf_op jit(solution)/shard_map/ppermute | solution.py:286
  12.4 5.5 %collective-permute-done.5 = bf16[64,1728]{1,0:T(8,128)(2,1)S(1)} collective-permute-done((bf16[64,1728]{1,0:T(8,128)(2,1)S(1)}, bf16[64,1728]{1,0:T(8,128)(2,1)S(1)}, u32[]{:S(2)}, u32[]{:S(2)}) %collective-permute-start.5) | collective-permute-done | bytes 221216 | tf_op jit(solution)/shard_map/ppermute | solution.py:286
  17.9 0.1 add_convert_fusion.1
  18.0 0.5 %collective-permute-start.6 = (bf16[64,1728]{1,0:T(8,128)(2,1)S(1)}, bf16[64,1728]{1,0:T(8,128)(2,1)S(1)}, u32[]{:S(2)}, u32[]{:S(2)}) collective-permute-start(bf16[64,1728]{1,0:T(8,128)(2,1)S(1)} %add_convert_fusion.1), channel_id=1, source_target_pairs={{0,4},{1,3},{2,6},{3,1},{4,0},{5,7},{6,2},{7,5},{8,12},{9,11},{10,... | collective-permute-start | bytes 663560 | tf_op jit(solution)/shard_map/ppermute | solution.py:286
  18.5 5.6 %collective-permute-done.6 = bf16[64,1728]{1,0:T(8,128)(2,1)S(1)} collective-permute-done((bf16[64,1728]{1,0:T(8,128)(2,1)S(1)}, bf16[64,1728]{1,0:T(8,128)(2,1)S(1)}, u32[]{:S(2)}, u32[]{:S(2)}) %collective-permute-start.6) | collective-permute-done | bytes 221216 | tf_op jit(solution)/shard_map/ppermute | solution.py:286
  24.1 0.1 add_convert_fusion
  24.1 0.4 collective-permute-start.7
  24.6 9.0 %collective-permute-done.7 = bf16[64,1728]{1,0:T(8,128)(2,1)S(1)} collective-permute-done((bf16[64,1728]{1,0:T(8,128)(2,1)S(1)}, bf16[64,1728]{1,0:T(8,128)(2,1)S(1)}, u32[]{:S(2)}, u32[]{:S(2)}) %collective-permute-start.7) | collective-permute-done | bytes 221216 | tf_op jit(solution)/shard_map/ppermute | solution.py:286
  33.5 0.1 add_multiply_fusion
  33.6 0.1 collective-permute-start.8
  33.7 0.5 %collective-permute-start.2 = (bf16[128,128]{1,0:T(8,128)(2,1)S(1)}, bf16[128,128]{1,0:T(8,128)(2,1)S(1)}, u32[]{:S(2)}, u32[]{:S(2)}) collective-permute-start(bf16[128,128]{1,0:T(8,128)(2,1)S(1)} %get-tuple-element.29), channel_id=1, source_target_pairs={{0,1},{1,0},{2,3},{3,2},{4,5},{5,4},{6,7},{7,6},{8,9},{9,8},{10,11... | collective-permute-start | bytes 98312 | tf_op jit(solution)/shard_map/ppermute | solution.py:366
  34.2 1.9 %collective-permute-start.3 = (bf16[128,128]{1,0:T(8,128)(2,1)S(1)}, bf16[128,128]{1,0:T(8,128)(2,1)S(1)}, u32[]{:S(2)}, u32[]{:S(2)}) collective-permute-start(bf16[128,128]{1,0:T(8,128)(2,1)S(1)} %get-tuple-element.30), channel_id=1, source_target_pairs={{1,2},{2,1},{3,4},{4,3},{5,6},{6,5},{7,8},{8,7},{9,10},{10,9},{11,... | collective-permute-start | bytes 98312 | tf_op jit(solution)/shard_map/ppermute | solution.py:367
  36.1 0.0 collective-permute-done.2.near_ref
  36.1 4.2 %collective-permute-done.3.far_ref = bf16[128,128]{1,0:T(8,128)(2,1)S(1)} collective-permute-done((bf16[128,128]{1,0:T(8,128)(2,1)S(1)}, bf16[128,128]{1,0:T(8,128)(2,1)S(1)}, u32[]{:S(2)}, u32[]{:S(2)}) %collective-permute-start.3) | collective-permute-done | bytes 32800 | tf_op jit(solution)/shard_map/ppermute | solution.py:367
  40.3 3.2 %shard_map.96 = (bf16[64,384]{1,0:T(8,128)(2,1)}, bf16[64,384]{1,0:T(8,128)(2,1)}) custom-call(bf16[128,128]{1,0:T(8,128)(2,1)S(1)} %collective-permute-done.2.near_ref, bf16[128,128]{1,0:T(8,128)(2,1)S(1)} %collective-permute-done.3.far_ref, bf16[3,128,128]{2,1,0:T(8,128)(2,1)S(1)} %get-tuple-element.31.state_ref, s32[27,384]{1,0:T(8,128)} %rule_hbm.3, ...), custom_call_target="tpu_custom_call" | custom-call | flops 509607936 | bytes 2654208 | tf_op jit(solution)/shard_map/pallas_call | solution.py:389
  43.5 0.0 collective-permute-done.8
  43.6 1.0 %broadcast_select_fusion = (f32[64,1728]{1,0:T(8,128)}, f32[64,1728]{1,0:T(8,128)}) fusion(f32[64,1728]{1,0:T(8,128)S(1)} %collective-permute-done.8, pred[]{:T(512)S(6)} %eq.5, bf16[64,1728]{1,0:T(8,128)(2,1)S(1)} %collective-permute-done.7, bf16[64,1728]{1,0:T(8,128)(2,1)S(1)} %add_convert_fusion), kind=kLoop, calls=%fused_computation.4 | loop fusion | flops 663552 | bytes 1769473 | tf_op jit(solution)/shard_map/jit(_where)/select_n | solution.py:290
Async XLA Ops:
  1.5 6.2 %collective-permute-start = (bf16[128,128]{1,0:T(8,128)(2,1)S(1)}, bf16[128,128]{1,0:T(8,128)(2,1)S(1)}, u32[]{:S(2)}, u32[]{:S(2)}) collective-permute-start(bf16[128,128]{1,0:T(8,128)(2,1)S(1)} %get-tuple-element.20), channel_id=1, source_target_pairs={{0,1},{1,0},{2,3},{3,2},{4,5},{5,4},{6,7},{7,6},{8,9},{9,8},{10,11... | collective-permute-start | bytes 98312 | tf_op jit(solution)/shard_map/ppermute | solution.py:322
  1.6 6.2 %collective-permute-start.1 = (bf16[128,128]{1,0:T(8,128)(2,1)S(1)}, bf16[128,128]{1,0:T(8,128)(2,1)S(1)}, u32[]{:S(2)}, u32[]{:S(2)}) collective-permute-start(bf16[128,128]{1,0:T(8,128)(2,1)S(1)} %get-tuple-element.21), channel_id=1, source_target_pairs={{1,2},{2,1},{3,4},{4,3},{5,6},{6,5},{7,8},{8,7},{9,10},{10,9},{11,... | collective-permute-start | bytes 98312 | tf_op jit(solution)/shard_map/ppermute | solution.py:321
  10.2 1.6 %collective-permute-start.4 = (bf16[64,1728]{1,0:T(8,128)(2,1)S(1)}, bf16[64,1728]{1,0:T(8,128)(2,1)S(1)}, u32[]{:S(2)}, u32[]{:S(2)}) collective-permute-start(bf16[64,1728]{1,0:T(8,128)(2,1)S(1)} %get-tuple-element.35), channel_id=1, source_target_pairs={{0,1},{1,0},{2,3},{3,2},{4,5},{5,4},{6,7},{7,6},{8,9},{9,8},{10,11... | collective-permute-start | bytes 663560 | tf_op jit(solution)/shard_map/ppermute | solution.py:279
  11.8 6.1 %collective-permute-start.5 = (bf16[64,1728]{1,0:T(8,128)(2,1)S(1)}, bf16[64,1728]{1,0:T(8,128)(2,1)S(1)}, u32[]{:S(2)}, u32[]{:S(2)}) collective-permute-start(bf16[64,1728]{1,0:T(8,128)(2,1)S(1)} %add_convert_fusion.2), channel_id=1, source_target_pairs={{0,2},{1,9},{2,0},{3,11},{4,6},{5,13},{6,4},{7,15},{8,10},{9,1},{1... | collective-permute-start | bytes 663560 | tf_op jit(solution)/shard_map/ppermute | solution.py:286
  18.0 6.1 %collective-permute-start.6 = (bf16[64,1728]{1,0:T(8,128)(2,1)S(1)}, bf16[64,1728]{1,0:T(8,128)(2,1)S(1)}, u32[]{:S(2)}, u32[]{:S(2)}) collective-permute-start(bf16[64,1728]{1,0:T(8,128)(2,1)S(1)} %add_convert_fusion.1), channel_id=1, source_target_pairs={{0,4},{1,3},{2,6},{3,1},{4,0},{5,7},{6,2},{7,5},{8,12},{9,11},{10,... | collective-permute-start | bytes 663560 | tf_op jit(solution)/shard_map/ppermute | solution.py:286
  24.1 9.4 %collective-permute-start.7 = (bf16[64,1728]{1,0:T(8,128)(2,1)S(1)}, bf16[64,1728]{1,0:T(8,128)(2,1)S(1)}, u32[]{:S(2)}, u32[]{:S(2)}) collective-permute-start(bf16[64,1728]{1,0:T(8,128)(2,1)S(1)} %add_convert_fusion), channel_id=1, source_target_pairs={{0,8},{1,5},{2,10},{3,7},{4,12},{5,1},{6,14},{7,3},{8,0},{9,13},{1... | collective-permute-start | bytes 663560 | tf_op jit(solution)/shard_map/ppermute | solution.py:286
  33.6 9.9 %collective-permute-start.8 = (f32[64,1728]{1,0:T(8,128)S(1)}, f32[64,1728]{1,0:T(8,128)S(1)}, u32[]{:S(2)}, u32[]{:S(2)}) collective-permute-start(f32[64,1728]{1,0:T(8,128)S(1)} %add_multiply_fusion), channel_id=1, source_target_pairs={{0,1},{1,0},{2,3},{3,2},{4,5},{5,4},{6,7},{7,6},{8,9},{9,8},{10,11... | collective-permute-start | bytes 1327112 | tf_op jit(solution)/shard_map/ppermute | solution.py:289
  33.7 2.4 %collective-permute-start.2 = (bf16[128,128]{1,0:T(8,128)(2,1)S(1)}, bf16[128,128]{1,0:T(8,128)(2,1)S(1)}, u32[]{:S(2)}, u32[]{:S(2)}) collective-permute-start(bf16[128,128]{1,0:T(8,128)(2,1)S(1)} %get-tuple-element.29), channel_id=1, source_target_pairs={{0,1},{1,0},{2,3},{3,2},{4,5},{5,4},{6,7},{7,6},{8,9},{9,8},{10,11... | collective-permute-start | bytes 98312 | tf_op jit(solution)/shard_map/ppermute | solution.py:366
  34.2 6.1 %collective-permute-start.3 = (bf16[128,128]{1,0:T(8,128)(2,1)S(1)}, bf16[128,128]{1,0:T(8,128)(2,1)S(1)}, u32[]{:S(2)}, u32[]{:S(2)}) collective-permute-start(bf16[128,128]{1,0:T(8,128)(2,1)S(1)} %get-tuple-element.30), channel_id=1, source_target_pairs={{1,2},{2,1},{3,4},{4,3},{5,6},{6,5},{7,8},{8,7},{9,10},{10,9},{11,... | collective-permute-start | bytes 98312 | tf_op jit(solution)/shard_map/ppermute | solution.py:367

commit v4 on v3

v4 whole, which is shorter than its diff:
```python
import math

import jax
import jax.numpy as jnp
from jax import lax
from jax.experimental import pallas as pl
from jax.experimental.pallas import tpu as pltpu
from jax.sharding import PartitionSpec as P


BLOCK = 128
F32, BF16 = jnp.float32, jnp.bfloat16
HBM = pl.BlockSpec(memory_space=pltpu.HBM)
SMALL = pltpu.CompilerParams(vmem_limit_bytes=1 << 20)
MEDIUM = pltpu.CompilerParams(vmem_limit_bytes=20 << 20)
VMEM = pl.BlockSpec(memory_space=pltpu.VMEM)
NT = (((1,), (1,)), ((), ()))


def is_odd():
    return lax.axis_index("tile") % 2 == 1


def pair_blocks(listed, odd):
    lower, upper = listed
    return jnp.where(odd, lower, upper), jnp.where(odd, upper, lower)


def fetch(sources, targets, sems):
    copies = [
        pltpu.make_async_copy(source, target, sems.at[i])
        for i, (source, target) in enumerate(zip(sources, targets))
    ]
    for copy in copies:
        copy.start()
    return copies


def load_kernel(
    lists_hbm, x_hbm, g_hbm, rule_hbm, w2_hbm, w1_hbm,
    near_ref, far_ref, lists_out, x_ref, g_ref, rule_ref, w2_ref, w1_ref,
    lists_ref, sems,
):
    width, rows = x_ref.shape
    copies = fetch(
        (lists_hbm, x_hbm, g_hbm, rule_hbm, w2_hbm, w1_hbm),
        (lists_ref, x_ref, g_ref, rule_ref, w2_ref, w1_ref),
        sems,
    )
    for copy in copies[:3]:
        copy.wait()
    picks = pair_blocks((lists_ref[0], lists_ref[1]), is_odd())
    for pick, out_ref in zip(picks, (near_ref, far_ref)):
        start = pl.multiple_of(jnp.minimum(pick, rows // BLOCK - 1) * BLOCK, BLOCK)
        out_ref[:width, :] = x_ref[:, pl.ds(start, BLOCK)]
        out_ref[width:, :] = g_ref[:, pl.ds(start, BLOCK)]
    for side in range(2):
        lists_out[side] = jnp.full(lists_out.shape[1:], lists_ref[side], jnp.int32)
    for copy in copies[3:]:
        copy.wait()


def fill_halo(table_ref, near_ref, far_ref, odd, blocks):
    near, far = near_ref[...], far_ref[...]
    table_ref[blocks] = jnp.where(odd, near, far)
    table_ref[blocks + 1] = jnp.where(odd, far, near)


def one_hot(rows, line):
    return (rows == line).astype(F32).astype(BF16)


def gather(table_ref, rule_ref, first_ref, second_ref, blocks):
    offsets = rule_ref.shape[0]
    group = offsets // 3
    sources, channels, _ = table_ref.shape
    width = channels // 2
    source_rows = lax.broadcasted_iota(jnp.int32, (BLOCK, BLOCK), 0)

    def store(k, low, high, found, mirrored):
        first_ref[k * width : (k + 1) * width, low:high] = found[:width].astype(BF16)
        second_ref[mirrored * width : (mirrored + 1) * width, low:high] = found[
            width:
        ].astype(BF16)

    strays = jnp.zeros((group, BLOCK), jnp.int32)
    for block in range(blocks):
        low, high = block * BLOCK, (block + 1) * BLOCK
        for side in range(3):
            entries = rule_ref[side * group : (side + 1) * group, low:high]
            if side == 1:
                source = block
            else:
                least = jnp.min(entries.astype(F32)).astype(jnp.int32)
                source = jnp.minimum(least // BLOCK, sources - 1)
            local = entries - source * BLOCK
            named = entries < sources * BLOCK
            strays = strays | (
                named & ((local < 0) | (local >= BLOCK))
            ).astype(jnp.int32)
            table = table_ref[source]
            for j in range(group):
                k = side * group + j
                choice = one_hot(source_rows, local[j : j + 1])
                found = jnp.dot(table, choice, preferred_element_type=F32)
                store(k, low, high, found, offsets - 1 - k)

    @pl.when(jnp.max(strays.astype(F32)) > 0)
    def _():
        rows = rule_ref.shape[1]
        every_row = lax.broadcasted_iota(jnp.int32, (BLOCK, rows), 0)

        def one(k, carry):
            line = rule_ref[pl.ds(k, 1), :]
            found = jnp.zeros((channels, rows), F32)
            for source in range(sources):
                choice = one_hot(every_row, line - source * BLOCK)
                found += jnp.dot(table_ref[source], choice, preferred_element_type=F32)
            here = pl.multiple_of(k * width, width)
            there = pl.multiple_of((offsets - 1 - k) * width, width)
            first_ref[pl.ds(here, width), :] = found[:width].astype(BF16)
            second_ref[pl.ds(there, width), :] = found[width:].astype(BF16)
            return carry

        lax.fori_loop(0, offsets, one, 0)


def turn(weight_ref, turned_ref):
    width, depth = weight_ref.shape
    offsets = depth // width
    for k in range(0, offsets, 2):
        count = min(2, offsets - k)
        block = weight_ref[:, k * width : (k + count) * width].astype(F32).T
        pieces = [block[i * width : (i + 1) * width] for i in range(count)]
        joined = pieces[0] if count == 1 else jnp.concatenate(pieces, axis=1)
        turned_ref[:, k * width : (k + count) * width] = joined.astype(BF16)


def own_kernel(
    rule_ref, x_ref, g_ref, w1_ref, w2_ref,
    xs_ref, gs_ref, pre_ref, d_hidden_ref, turned_ref,
    table_ref,
):
    width, rows = x_ref.shape
    blocks = rows // BLOCK
    for block in range(blocks):
        low, high = block * BLOCK, (block + 1) * BLOCK
        table_ref[block, :width] = x_ref[:, low:high]
        table_ref[block, width:] = g_ref[:, low:high]
    table_ref[blocks:] = jnp.zeros_like(table_ref[blocks:])
    gather(table_ref, rule_ref, xs_ref, gs_ref, blocks)
    turn(w2_ref, turned_ref)
    pre_ref[...] = jnp.dot(w1_ref[...], xs_ref[...], preferred_element_type=F32)
    d_hidden_ref[...] = jnp.dot(turned_ref[...], gs_ref[...], preferred_element_type=F32)


def first_terms(state_ref, xs_ref, out_ref):
    blocks = state_ref.shape[0]
    width = state_ref.shape[1] // 2
    depth = xs_ref.shape[0]
    d_pre = jnp.concatenate([state_ref[block, width:] for block in range(blocks)], axis=1)
    for low in range(0, depth, 8 * width):
        high = min(depth, low + 8 * width)
        terms = lax.dot_general(d_pre, xs_ref[low:high], NT, preferred_element_type=F32)
        out_ref[:, low:high] = terms.astype(out_ref.dtype)


def second_terms(state_ref, gs_ref, out_ref):
    blocks = state_ref.shape[0]
    width = state_ref.shape[1] // 2
    depth = gs_ref.shape[0]
    hidden = jnp.concatenate([state_ref[block, :width] for block in range(blocks)], axis=1)
    for low in range(0, depth, 4 * width):
        high = min(depth, low + 4 * width)
        terms = lax.dot_general(gs_ref[low:high], hidden, NT, preferred_element_type=F32)
        for at in range(low, high, 2 * width):
            pieces = [
                terms[i - low : i - low + width] for i in range(at, min(high, at + 2 * width), width)
            ]
            joined = pieces[0] if len(pieces) == 1 else jnp.concatenate(pieces, axis=1)
            out_ref[:, at : at + joined.shape[1]] = joined.astype(out_ref.dtype)


def rim_kernel(
    lists_ref, near_ref, far_ref, pre_in, d_hidden_in, rule_ref, w1_ref, turned_ref, xs_in, gs_in,
    state_ref, near_out, far_out, send_ref, xs_ref, gs_ref,
    pre_ref, d_hidden_ref,
):
    width, rows = pre_in.shape
    blocks = rows // BLOCK
    offsets = rule_ref.shape[0]
    group = offsets // 3
    odd = is_odd()
    listed = [jnp.max(lists_ref[side].astype(F32)).astype(jnp.int32) for side in range(2)]
    near, far = near_ref[...], far_ref[...]
    tables = (jnp.where(odd, near, far), jnp.where(odd, far, near))
    pre_ref[...] = pre_in[...]
    d_hidden_ref[...] = d_hidden_in[...]
    source_rows = lax.broadcasted_iota(jnp.int32, (BLOCK, BLOCK), 0)
    for side in range(2):
        columns = pl.ds(pl.multiple_of(jnp.minimum(listed[side], blocks - 1) * BLOCK, BLOCK), BLOCK)
        start = 2 * side * group
        mirrored = offsets - group - start
        local = rule_ref[start : start + group, columns] - (blocks + side) * BLOCK
        rim_x, rim_g = [], []
        for j in range(group):
            found = jnp.dot(
                tables[side], one_hot(source_rows, local[j : j + 1]), preferred_element_type=F32
            )
            rim_x.append(found[:width].astype(BF16))
            rim_g.append(found[width:].astype(BF16))
        rim_x = jnp.concatenate(rim_x, axis=0)
        rim_g = jnp.concatenate(rim_g[::-1], axis=0)
        span = slice(start * width, (start + group) * width)
        mirror_span = slice(mirrored * width, (mirrored + group) * width)
        pre_ref[:, columns] += jnp.dot(w1_ref[:, span], rim_x, preferred_element_type=F32)
        d_hidden_ref[:, columns] += jnp.dot(
            turned_ref[:, mirror_span], rim_g, preferred_element_type=F32
        )

        @pl.when(listed[side] < blocks)
        def _():
            xs_ref[span, columns] = rim_x
            gs_ref[mirror_span, columns] = rim_g

    pre = pre_ref[...]
    sigma = jax.nn.sigmoid(pre)
    hidden = (pre * sigma).astype(BF16)
    d_pre = (d_hidden_ref[...] * sigma * (1.0 + pre * (1.0 - sigma))).astype(BF16)
    for block in range(blocks):
        low, high = block * BLOCK, (block + 1) * BLOCK
        state_ref[block, :width] = hidden[:, low:high]
        state_ref[block, width:] = d_pre[:, low:high]
    for pick, out_ref in zip(pair_blocks(listed, odd), (near_out, far_out)):
        out_ref[...] = state_ref[jnp.minimum(pick, blocks - 1)]

    @pl.when(odd)
    def _():
        first_terms(state_ref, xs_ref, send_ref)

    @pl.when(jnp.logical_not(odd))
    def _():
        second_terms(state_ref, gs_ref, send_ref)


def keep_kernel(state_ref, xs_ref, gs_ref, keep_ref):
    odd = is_odd()

    @pl.when(odd)
    def _():
        second_terms(state_ref, gs_ref, keep_ref)

    @pl.when(jnp.logical_not(odd))
    def _():
        first_terms(state_ref, xs_ref, keep_ref)


def put(source, for_odd, for_even, sem):
    odd = is_odd()
    for chosen, target in ((odd, for_odd), (jnp.logical_not(odd), for_even)):

        @pl.when(chosen)
        def _():
            copy = pltpu.make_async_copy(source, target, sem)
            copy.start()
            copy.wait()


def put_own_kernel(total_ref, first_hbm, second_hbm, sem):
    put(total_ref, second_hbm, first_hbm, sem)


def put_other_kernel(other_ref, first_in, second_in, first_hbm, second_hbm, sem):
    put(other_ref, first_hbm, second_hbm, sem)


def second_kernel(
    near_ref, far_ref, state_ref, rule_ref, x_ref, g_ref, w1_ref, w2_ref,
    out_ref, dx_ref,
    table_ref, hs_ref, ds_ref, turned_ref,
):
    _, rows = x_ref.shape
    blocks = rows // BLOCK
    odd = is_odd()
    for block in range(blocks):
        table_ref[block] = state_ref[block]
    fill_halo(table_ref, near_ref, far_ref, odd, blocks)
    gather(table_ref, rule_ref, hs_ref, ds_ref, blocks)
    turn(w1_ref, turned_ref)
    second = jnp.dot(w2_ref[...], hs_ref[...], preferred_element_type=F32)
    out_ref[...] = (second + x_ref[...].astype(F32)).astype(BF16)
    d_input = jnp.dot(turned_ref[...], ds_ref[...], preferred_element_type=F32)
    dx_ref[...] = (d_input + g_ref[...].astype(F32)).astype(BF16)


def neighbour_pairs(count):
    near = [(i, i ^ 1) for i in range(count) if i ^ 1 < count]
    far = [(i, i + 1 if i % 2 else i - 1) for i in range(count)]
    return near, [(i, j) for i, j in far if 0 <= j < count]


def total_over_tiles(keep, send, scale):
    count = lax.axis_size("tile")
    cores = [(i, i ^ 1) for i in range(count)]
    received = lax.ppermute(send, "tile", cores)
    total = keep + received.astype(F32)
    bits = [1 << b for b in range(1, count.bit_length() - 1)]
    for step, (even_bit, odd_bit) in enumerate(zip(bits, bits[-1:] + bits[:-1])):
        wire = BF16 if step >= len(bits) - 3 else F32
        pairs = [(i, i ^ (odd_bit if i % 2 else even_bit)) for i in range(count)]
        sent = total.astype(wire)
        received = lax.ppermute(sent, "tile", pairs)
        total = sent.astype(F32) + received.astype(F32)
    total = total * scale
    other = lax.ppermute(total, "tile", cores)
    result = jax.ShapeDtypeStruct(total.shape, F32)
    put_own = pl.pallas_call(
        put_own_kernel,
        out_shape=(result, result),
        in_specs=[VMEM],
        out_specs=(HBM, HBM),
        scratch_shapes=[pltpu.SemaphoreType.DMA],
        compiler_params=SMALL,
    )
    half = put_own(total)
    return pl.pallas_call(
        put_other_kernel,
        out_shape=(result, result),
        in_specs=[VMEM, HBM, HBM],
        out_specs=(HBM, HBM),
        scratch_shapes=[pltpu.SemaphoreType.DMA],
        input_output_aliases={1: 0, 2: 1},
        compiler_params=SMALL,
    )(other, *half)


def body(features, rulebook, send_lists, weight_first, weight_second, cotangent):
    width, rows = features.shape
    offsets = rulebook.shape[0]
    blocks = rows // BLOCK
    count = lax.axis_size("tile")
    near_pairs, far_pairs = neighbour_pairs(count)
    send_lists = send_lists.reshape(2)
    features, cotangent, rulebook, weight_first, weight_second, send_lists = (
        pltpu.with_memory_space_constraint(array, pltpu.HBM)
        for array in (features, cotangent, rulebook, weight_first, weight_second, send_lists)
    )
    shape = jax.ShapeDtypeStruct
    rim = shape((2 * width, BLOCK), BF16)
    values = shape((width, rows), BF16)
    sums = shape((width, rows), F32)
    gathered = shape((offsets * width, rows), BF16)
    weight = shape((width, offsets * width), BF16)
    terms = shape((width, offsets * width), F32)
    state_shape = shape((blocks, 2 * width, BLOCK), BF16)
    table = pltpu.VMEM((blocks + 2, 2 * width, BLOCK), BF16)

    near, far, lists, x, g, rule, w2, w1 = pl.pallas_call(
        load_kernel,
        out_shape=(
            rim, rim, shape((2, 8, BLOCK), jnp.int32), values, values,
            shape(rulebook.shape, jnp.int32), weight, weight,
        ),
        in_specs=[HBM] * 6,
        out_specs=(VMEM,) * 8,
        scratch_shapes=[pltpu.SMEM((2,), jnp.int32), pltpu.SemaphoreType.DMA((6,))],
        compiler_params=MEDIUM,
    )(send_lists, features, cotangent, rulebook, weight_second, weight_first)
    far = lax.ppermute(far, "tile", far_pairs)
    near = lax.ppermute(near, "tile", near_pairs)

    work = pl.CostEstimate(
        flops=2 * 2 * width * offsets * rows * (width + BLOCK),
        bytes_accessed=4 * offsets * width * rows,
        transcendentals=0,
    )
    own_phase = pl.pallas_call(
        own_kernel,
        out_shape=(gathered, gathered, sums, sums, weight),
        in_specs=[VMEM] * 5,
        out_specs=(VMEM,) * 5,
        scratch_shapes=[table],
        compiler_params=MEDIUM,
        cost_estimate=work,
    )
    xs, gs, pre, d_hidden, turned = own_phase(rule, x, g, w1, w2)
    state, near, far, send, xs, gs = pl.pallas_call(
        rim_kernel,
        out_shape=(state_shape, rim, rim, weight, gathered, gathered),
        in_specs=[VMEM] * 10,
        out_specs=(VMEM,) * 6,
        scratch_shapes=[pltpu.VMEM((width, rows), F32), pltpu.VMEM((width, rows), F32)],
        input_output_aliases={8: 4, 9: 5},
        compiler_params=MEDIUM,
    )(lists, near, far, pre, d_hidden, rule, w1, turned, xs, gs)
    keep_terms = pl.pallas_call(
        keep_kernel,
        out_shape=terms,
        in_specs=[VMEM] * 3,
        out_specs=VMEM,
        compiler_params=MEDIUM,
    )
    keep = keep_terms(state, xs, gs)

    near = lax.ppermute(near, "tile", near_pairs)
    far = lax.ppermute(far, "tile", far_pairs)
    second_phase = pl.pallas_call(
        second_kernel,
        out_shape=(values, values),
        in_specs=[VMEM] * 8,
        out_specs=(VMEM, VMEM),
        scratch_shapes=[
            table,
            pltpu.VMEM((offsets * width, rows), BF16),
            pltpu.VMEM((offsets * width, rows), BF16),
            pltpu.VMEM((width, offsets * width), BF16),
        ],
        compiler_params=MEDIUM,
        cost_estimate=work,
    )
    out_features, d_features = second_phase(near, far, state, rule, x, g, w1, w2)

    scale = 1.0 / math.sqrt(rows * count)
    grad_first, grad_second = total_over_tiles(keep, send, scale)
    return out_features, d_features, grad_first, grad_second


def solution(mesh):
    tiles = P(None, ("groups", "tile"))
    return jax.shard_map(
        body,
        mesh=mesh,
        in_specs=(tiles, tiles, tiles, P(), P(), tiles),
        out_specs=(tiles, tiles, P("groups", None), P("groups", None)),
        check_vma=False,
    )
```

time: 44.8 us -> 44 us (0.982)
  other arithmetic: 1.24 us -> 0.21 us
    select_n x1 -> x0, other arithmetic: 1.01 us -> none  [total_over_tiles(): return (jnp.where(odd, other, total), jnp.where(odd, total, other))]
    ppermute x2, waiting for transfers between devices: 4.32 us -> 5.23 us  [body(): far = lax.ppermute(far, 'tile', far_pairs)]
    ppermute x2, waiting for transfers between devices: 1.46 us -> 0.9 us  [the longest x1 0.9 us: total_over_tiles(): received = lax.ppermute(send, 'tile', cores)]
    pallas_call x4 -> x7, Pallas kernels: 9.21 us -> 9.18 us  [the longest x1 2.39 us: body(): second_phase(near, far, state, rule, x, g, w1, w2)]
where the time goes in v4:
time: 44 us; the launch traced here: 43.8 us
  waiting for transfers between devices  26.2 us (60%)
  Pallas kernels  9.18 us (21%)
  starting transfers between devices  7.48 us (17%)
  between operations  0.74 us (2%)
    ppermute x3, waiting for transfers between devices, total_over_tiles(): received = lax.ppermute(sent, 'tile', pairs)  20.1 us
    ppermute x2, starting transfers between devices, body(): far = lax.ppermute(far, 'tile', far_pairs)  5.28 us
    ppermute x2, waiting for transfers between devices, body(): far = lax.ppermute(far, 'tile', far_pairs)  5.23 us
    pallas_call x1, Pallas kernels, body(): second_phase(near, far, state, rule, x, g, w1, w2)  2.39 us
    pallas_call x1, Pallas kernels, body(): xs, gs, pre, d_hidden, turned = own_phase(rule, x, g, w1, w2)  1.79 us
    pallas_call x1, Pallas kernels, body(): pl.pallas_call(rim_kernel, out_shape=(state_shape, rim, rim, weight, gath...  1.66 us
    ppermute x3, starting transfers between devices, total_over_tiles(): received = lax.ppermute(sent, 'tile', pairs)  1.48 us
    pallas_call x1, Pallas kernels, body(): pl.pallas_call(load_kernel, out_shape=(rim, rim, shape((2, 8, BLOCK), jnp...  1.19 us
  transfers between devices with their start and end apart: 9, of which 6 were waited for; matrix products, arithmetic and copies ran while one was open for 0% of the time, Pallas kernels for 13%

profile of v4, /device:TPU:28, one launch (start us, length us, event | category | flops | bytes accessed | tf_op | source)
XLA Modules:
  0.0 43.8 jit_solution(11995246658430955049)
XLA Ops:
  0.6 1.2 %shard_map.93 = (bf16[128,128]{1,0:T(8,128)(2,1)S(1)}, bf16[128,128]{1,0:T(8,128)(2,1)S(1)}, s32[2,8,128]{2,1,0:T(8,128)S(1)}, bf16[64,384]{1,0:T(8,128)(2,1)S(1...) custom-call(s32[2]{0:T(128)} %bitcast.1, ...), custom_call_target="tpu_custom_call" | custom-call | tf_op jit(solution)/shard_map/pallas_call | solution.py:358
  1.8 0.1 collective-permute-start
  1.9 3.4 %collective-permute-start.1 = (bf16[128,128]{1,0:T(8,128)(2,1)S(1)}, bf16[128,128]{1,0:T(8,128)(2,1)S(1)}, u32[]{:S(2)}, u32[]{:S(2)}) collective-permute-start(bf16[128,128]{1,0:T(8,128)(2,1)S(1)} %get-tuple-element.31), channel_id=1, source_target_pairs={{1,2},{2,1},{3,4},{4,3},{5,6},{6,5},{7,8},{8,7},{9,10},{10,9},{11,... | collective-permute-start | bytes 98312 | tf_op jit(solution)/shard_map/ppermute | solution.py:369
  5.3 1.8 %shard_map.94 = (bf16[1728,384]{1,0:T(8,128)(2,1)S(1)}, bf16[1728,384]{1,0:T(8,128)(2,1)S(1)}, f32[64,384]{1,0:T(8,128)S(1)}, f32[64,384]{1,0:T(8,128)S(1)}, bf16[64,1728]{1,0:T(8,128)(2,1)S(1)}) custom-call(s32[27,384]{1,0:T(8,128)S(1)} %get-tuple-element.32.rule_ref, bf16[64,384]{1,0:T(8,128)(2,1)S(1)} %get-tuple-element.33.x_ref, ...), custom_call_target="tpu_custom_call" | custom-call | flops 509607936 | bytes 2654208 | tf_op jit(solution)/shard_map/pallas_call | solution.py:386
  7.1 0.0 collective-permute-done.near_ref
  7.1 1.0 %collective-permute-done.1.far_ref = bf16[128,128]{1,0:T(8,128)(2,1)S(1)} collective-permute-done((bf16[128,128]{1,0:T(8,128)(2,1)S(1)}, bf16[128,128]{1,0:T(8,128)(2,1)S(1)}, u32[]{:S(2)}, u32[]{:S(2)}) %collective-permute-start.1) | collective-permute-done | bytes 32800 | tf_op jit(solution)/shard_map/ppermute | solution.py:369
  8.1 1.7 %shard_map.95 = (bf16[3,128,128]{2,1,0:T(8,128)(2,1)S(1)}, bf16[128,128]{1,0:T(8,128)(2,1)S(1)}, bf16[128,128]{1,0:T(8,128)(2,1)S(1)}, bf16[64,1728]{1,0:T(8,128...) custom-call(s32[2,8,128]{2,1,0:T(8,128)S(1)} %get-tuple-element.29.l, ...), custom_call_target="tpu_custom_call", output_to_operand_aliasing={{4}: (8, {}), {5}: (9, {})} | custom-call | tf_op jit(solution)/shard_map/pallas_call | solution.py:387
  9.8 0.1 collective-permute-start.4
  9.9 0.6 %shard_map.97 = f32[64,1728]{1,0:T(8,128)S(1)} custom-call(bf16[3,128,128]{2,1,0:T(8,128)(2,1)S(1)} %get-tuple-element.44.state_ref, bf16[1728,384]{1,0:T(8,128)(2,1)S(1)} %get-tuple-element.47.xs_ref, bf16[1728,384]{1,0:T(8,128)(2,1)S(1)} %get-tuple-element.48.gs_ref), custom_call_target="tpu_custom_call" | custom-call | tf_op jit(solution)/shard_map/pallas_call | solution.py:403
  10.5 0.9 %collective-permute-done.4 = bf16[64,1728]{1,0:T(8,128)(2,1)S(1)} collective-permute-done((bf16[64,1728]{1,0:T(8,128)(2,1)S(1)}, bf16[64,1728]{1,0:T(8,128)(2,1)S(1)}, u32[]{:S(2)}, u32[]{:S(2)}) %collective-permute-start.4) | collective-permute-done | bytes 221216 | tf_op jit(solution)/shard_map/ppermute | solution.py:305
  11.4 0.6 %collective-permute-start.5 = (bf16[64,1728]{1,0:T(8,128)(2,1)S(1)}, bf16[64,1728]{1,0:T(8,128)(2,1)S(1)}, u32[]{:S(2)}, u32[]{:S(2)}) collective-permute-start(bf16[64,1728]{1,0:T(8,128)(2,1)S(1)} %add_convert_fusion.2), channel_id=1, source_target_pairs={{0,2},{1,9},{2,0},{3,11},{4,6},{5,13},{6,4},{7,15},{8,10},{9,1},{1... | collective-permute-start | bytes 663560 | tf_op jit(solution)/shard_map/ppermute | solution.py:312
  12.0 5.5 %collective-permute-done.5 = bf16[64,1728]{1,0:T(8,128)(2,1)S(1)} collective-permute-done((bf16[64,1728]{1,0:T(8,128)(2,1)S(1)}, bf16[64,1728]{1,0:T(8,128)(2,1)S(1)}, u32[]{:S(2)}, u32[]{:S(2)}) %collective-permute-start.5) | collective-permute-done | bytes 221216 | tf_op jit(solution)/shard_map/ppermute | solution.py:312
  17.5 0.1 add_convert_fusion.1
  17.6 0.5 %collective-permute-start.6 = (bf16[64,1728]{1,0:T(8,128)(2,1)S(1)}, bf16[64,1728]{1,0:T(8,128)(2,1)S(1)}, u32[]{:S(2)}, u32[]{:S(2)}) collective-permute-start(bf16[64,1728]{1,0:T(8,128)(2,1)S(1)} %add_convert_fusion.1), channel_id=1, source_target_pairs={{0,4},{1,3},{2,6},{3,1},{4,0},{5,7},{6,2},{7,5},{8,12},{9,11},{10,... | collective-permute-start | bytes 663560 | tf_op jit(solution)/shard_map/ppermute | solution.py:312
  18.1 5.6 %collective-permute-done.6 = bf16[64,1728]{1,0:T(8,128)(2,1)S(1)} collective-permute-done((bf16[64,1728]{1,0:T(8,128)(2,1)S(1)}, bf16[64,1728]{1,0:T(8,128)(2,1)S(1)}, u32[]{:S(2)}, u32[]{:S(2)}) %collective-permute-start.6) | collective-permute-done | bytes 221216 | tf_op jit(solution)/shard_map/ppermute | solution.py:312
  23.6 0.1 add_convert_fusion
  23.7 0.4 collective-permute-start.7
  24.1 9.0 %collective-permute-done.7 = bf16[64,1728]{1,0:T(8,128)(2,1)S(1)} collective-permute-done((bf16[64,1728]{1,0:T(8,128)(2,1)S(1)}, bf16[64,1728]{1,0:T(8,128)(2,1)S(1)}, u32[]{:S(2)}, u32[]{:S(2)}) %collective-permute-start.7) | collective-permute-done | bytes 221216 | tf_op jit(solution)/shard_map/ppermute | solution.py:312
  33.1 0.1 add_multiply_fusion.total_ref
  33.2 0.1 collective-permute-start.8
  33.2 0.5 %collective-permute-start.2 = (bf16[128,128]{1,0:T(8,128)(2,1)S(1)}, bf16[128,128]{1,0:T(8,128)(2,1)S(1)}, u32[]{:S(2)}, u32[]{:S(2)}) collective-permute-start(bf16[128,128]{1,0:T(8,128)(2,1)S(1)} %get-tuple-element.42), channel_id=1, source_target_pairs={{0,1},{1,0},{2,3},{3,2},{4,5},{5,4},{6,7},{7,6},{8,9},{9,8},{10,11... | collective-permute-start | bytes 98312 | tf_op jit(solution)/shard_map/ppermute | solution.py:405
  33.7 1.9 %collective-permute-start.3 = (bf16[128,128]{1,0:T(8,128)(2,1)S(1)}, bf16[128,128]{1,0:T(8,128)(2,1)S(1)}, u32[]{:S(2)}, u32[]{:S(2)}) collective-permute-start(bf16[128,128]{1,0:T(8,128)(2,1)S(1)} %get-tuple-element.43), channel_id=1, source_target_pairs={{1,2},{2,1},{3,4},{4,3},{5,6},{6,5},{7,8},{8,7},{9,10},{10,9},{11,... | collective-permute-start | bytes 98312 | tf_op jit(solution)/shard_map/ppermute | solution.py:406
  35.6 0.0 collective-permute-done.2.near_ref
  35.7 4.2 %collective-permute-done.3.far_ref = bf16[128,128]{1,0:T(8,128)(2,1)S(1)} collective-permute-done((bf16[128,128]{1,0:T(8,128)(2,1)S(1)}, bf16[128,128]{1,0:T(8,128)(2,1)S(1)}, u32[]{:S(2)}, u32[]{:S(2)}) %collective-permute-start.3) | collective-permute-done | bytes 32800 | tf_op jit(solution)/shard_map/ppermute | solution.py:406
  39.8 2.4 %shard_map.96 = (bf16[64,384]{1,0:T(8,128)(2,1)}, bf16[64,384]{1,0:T(8,128)(2,1)}) custom-call(bf16[128,128]{1,0:T(8,128)(2,1)S(1)} %collective-permute-done.2.near_ref, bf16[128,128]{1,0:T(8,128)(2,1)S(1)} %collective-permute-done.3.far_ref, bf16[3,128,128]{2,1,0:T(8,128)(2,1)S(1)} %get-tuple-element.44.state_ref, ...), custom_call_target="tpu_custom_call" | custom-call | flops 509607936 | bytes 2654208 | tf_op jit(solution)/shard_map/pallas_call | solution.py:421
  42.2 0.8 %shard_map.98 = (f32[64,1728]{1,0:T(8,128)}, f32[64,1728]{1,0:T(8,128)}) custom-call(f32[64,1728]{1,0:T(8,128)S(1)} %add_multiply_fusion.total_ref), custom_call_target="tpu_custom_call" | custom-call | tf_op jit(solution)/shard_map/pallas_call | solution.py:325
  43.0 0.0 collective-permute-done.8.other_ref
  43.0 0.8 %shard_map.99 = (f32[64,1728]{1,0:T(8,128)}, f32[64,1728]{1,0:T(8,128)}) custom-call(f32[64,1728]{1,0:T(8,128)S(1)} %collective-permute-done.8.other_ref, f32[64,1728]{1,0:T(8,128)} %get-tuple-element.50.first_in, f32[64,1728]{1,0:T(8,128)} %get-tuple-element.51.second_in), custom_call_target="tpu_custom_call", output_to_operand_aliasing={{0}: (1, {}), {1}: (2, {})} | custom-call | tf_op jit(solution)/shard_map/pallas_call | solution.py:326
  (1 shorter events, 0.0 us)
Async XLA Ops:
  1.8 5.3 %collective-permute-start = (bf16[128,128]{1,0:T(8,128)(2,1)S(1)}, bf16[128,128]{1,0:T(8,128)(2,1)S(1)}, u32[]{:S(2)}, u32[]{:S(2)}) collective-permute-start(bf16[128,128]{1,0:T(8,128)(2,1)S(1)} %get-tuple-element.30), channel_id=1, source_target_pairs={{0,1},{1,0},{2,3},{3,2},{4,5},{5,4},{6,7},{7,6},{8,9},{9,8},{10,11... | collective-permute-start | bytes 98312 | tf_op jit(solution)/shard_map/ppermute | solution.py:370
  1.9 6.2 %collective-permute-start.1 = (bf16[128,128]{1,0:T(8,128)(2,1)S(1)}, bf16[128,128]{1,0:T(8,128)(2,1)S(1)}, u32[]{:S(2)}, u32[]{:S(2)}) collective-permute-start(bf16[128,128]{1,0:T(8,128)(2,1)S(1)} %get-tuple-element.31), channel_id=1, source_target_pairs={{1,2},{2,1},{3,4},{4,3},{5,6},{6,5},{7,8},{8,7},{9,10},{10,9},{11,... | collective-permute-start | bytes 98312 | tf_op jit(solution)/shard_map/ppermute | solution.py:369
  9.8 1.6 %collective-permute-start.4 = (bf16[64,1728]{1,0:T(8,128)(2,1)S(1)}, bf16[64,1728]{1,0:T(8,128)(2,1)S(1)}, u32[]{:S(2)}, u32[]{:S(2)}) collective-permute-start(bf16[64,1728]{1,0:T(8,128)(2,1)S(1)} %get-tuple-element.49), channel_id=1, source_target_pairs={{0,1},{1,0},{2,3},{3,2},{4,5},{5,4},{6,7},{7,6},{8,9},{9,8},{10,11... | collective-permute-start | bytes 663560 | tf_op jit(solution)/shard_map/ppermute | solution.py:305
  11.4 6.1 %collective-permute-start.5 = (bf16[64,1728]{1,0:T(8,128)(2,1)S(1)}, bf16[64,1728]{1,0:T(8,128)(2,1)S(1)}, u32[]{:S(2)}, u32[]{:S(2)}) collective-permute-start(bf16[64,1728]{1,0:T(8,128)(2,1)S(1)} %add_convert_fusion.2), channel_id=1, source_target_pairs={{0,2},{1,9},{2,0},{3,11},{4,6},{5,13},{6,4},{7,15},{8,10},{9,1},{1... | collective-permute-start | bytes 663560 | tf_op jit(solution)/shard_map/ppermute | solution.py:312
  17.6 6.1 %collective-permute-start.6 = (bf16[64,1728]{1,0:T(8,128)(2,1)S(1)}, bf16[64,1728]{1,0:T(8,128)(2,1)S(1)}, u32[]{:S(2)}, u32[]{:S(2)}) collective-permute-start(bf16[64,1728]{1,0:T(8,128)(2,1)S(1)} %add_convert_fusion.1), channel_id=1, source_target_pairs={{0,4},{1,3},{2,6},{3,1},{4,0},{5,7},{6,2},{7,5},{8,12},{9,11},{10,... | collective-permute-start | bytes 663560 | tf_op jit(solution)/shard_map/ppermute | solution.py:312
  23.7 9.4 %collective-permute-start.7 = (bf16[64,1728]{1,0:T(8,128)(2,1)S(1)}, bf16[64,1728]{1,0:T(8,128)(2,1)S(1)}, u32[]{:S(2)}, u32[]{:S(2)}) collective-permute-start(bf16[64,1728]{1,0:T(8,128)(2,1)S(1)} %add_convert_fusion), channel_id=1, source_target_pairs={{0,8},{1,5},{2,10},{3,7},{4,12},{5,1},{6,14},{7,3},{8,0},{9,13},{1... | collective-permute-start | bytes 663560 | tf_op jit(solution)/shard_map/ppermute | solution.py:312
  33.2 9.9 %collective-permute-start.8 = (f32[64,1728]{1,0:T(8,128)S(1)}, f32[64,1728]{1,0:T(8,128)S(1)}, u32[]{:S(2)}, u32[]{:S(2)}) collective-permute-start(f32[64,1728]{1,0:T(8,128)S(1)} %add_multiply_fusion.total_ref), channel_id=1, source_target_pairs={{0,1},{1,0},{2,3},{3,2},{4,5},{5,4},{6,7},{7,6},{8,9},{9,8},{10,11... | collective-permute-start | bytes 1327112 | tf_op jit(solution)/shard_map/ppermute | solution.py:315
  33.2 2.4 %collective-permute-start.2 = (bf16[128,128]{1,0:T(8,128)(2,1)S(1)}, bf16[128,128]{1,0:T(8,128)(2,1)S(1)}, u32[]{:S(2)}, u32[]{:S(2)}) collective-permute-start(bf16[128,128]{1,0:T(8,128)(2,1)S(1)} %get-tuple-element.42), channel_id=1, source_target_pairs={{0,1},{1,0},{2,3},{3,2},{4,5},{5,4},{6,7},{7,6},{8,9},{9,8},{10,11... | collective-permute-start | bytes 98312 | tf_op jit(solution)/shard_map/ppermute | solution.py:405
  33.7 6.1 %collective-permute-start.3 = (bf16[128,128]{1,0:T(8,128)(2,1)S(1)}, bf16[128,128]{1,0:T(8,128)(2,1)S(1)}, u32[]{:S(2)}, u32[]{:S(2)}) collective-permute-start(bf16[128,128]{1,0:T(8,128)(2,1)S(1)} %get-tuple-element.43), channel_id=1, source_target_pairs={{1,2},{2,1},{3,4},{4,3},{5,6},{6,5},{7,8},{8,7},{9,10},{10,9},{11,... | collective-permute-start | bytes 98312 | tf_op jit(solution)/shard_map/ppermute | solution.py:406

commit v5 on v4

--- a/solution.py
+++ b/solution.py
@@ -293,10 +293,16 @@
     dx_ref[...] = (d_input + g_ref[...].astype(F32)).astype(BF16)
 
 
-def neighbour_pairs(count):
-    near = [(i, i ^ 1) for i in range(count) if i ^ 1 < count]
-    far = [(i, i + 1 if i % 2 else i - 1) for i in range(count)]
-    return near, [(i, j) for i, j in far if 0 <= j < count]
+def neighbour_pairs(groups, count):
+    near = [(i, i ^ 1) for i in range(groups * count)]
+    far = []
+    for group in range(groups):
+        for i in range(count):
+            other, tile = group, i + 1 if i % 2 else i - 1
+            if not 0 <= tile < count:
+                other, tile = (group + 1) % groups, i
+            far.append((group * count + i, other * count + tile))
+    return near, far
 
 
 def total_over_tiles(keep, send, scale):
@@ -339,7 +345,8 @@
     offsets = rulebook.shape[0]
     blocks = rows // BLOCK
     count = lax.axis_size("tile")
-    near_pairs, far_pairs = neighbour_pairs(count)
+    near_pairs, far_pairs = neighbour_pairs(lax.axis_size("groups"), count)
+    axes = ("groups", "tile")
     send_lists = send_lists.reshape(2)
     features, cotangent, rulebook, weight_first, weight_second, send_lists = (
         pltpu.with_memory_space_constraint(array, pltpu.HBM)
@@ -366,8 +373,8 @@
         scratch_shapes=[pltpu.SMEM((2,), jnp.int32), pltpu.SemaphoreType.DMA((6,))],
         compiler_params=MEDIUM,
     )(send_lists, features, cotangent, rulebook, weight_second, weight_first)
-    far = lax.ppermute(far, "tile", far_pairs)
-    near = lax.ppermute(near, "tile", near_pairs)
+    far = lax.ppermute(far, axes, far_pairs)
+    near = lax.ppermute(near, axes, near_pairs)
 
     work = pl.CostEstimate(
         flops=2 * 2 * width * offsets * rows * (width + BLOCK),
@@ -402,8 +409,8 @@
     )
     keep = keep_terms(state, xs, gs)
 
-    near = lax.ppermute(near, "tile", near_pairs)
-    far = lax.ppermute(far, "tile", far_pairs)
+    near = lax.ppermute(near, axes, near_pairs)
+    far = lax.ppermute(far, axes, far_pairs)
     second_phase = pl.pallas_call(
         second_kernel,
         out_shape=(values, values),

time: 44 us -> 40.2 us (0.914)
  starting transfers between devices: 7.48 us -> 3.7 us
    ppermute x4, starting transfers between devices: 5.85 us -> 2.05 us  [the longest x2 1.48 us: body(): far = lax.ppermute(far, axes, far_pairs)]
  transfers between devices with their start and end apart: 9 -> 9, of which waited for: 6 -> 7; matrix products, arithmetic and copies ran while one was open for 0% -> 0% of each run, Pallas kernels for 13% -> 14%
where the time goes in v5:
time: 40.2 us; the launch traced here: 40.1 us
  waiting for transfers between devices  26.3 us (65%)
  Pallas kernels  9.18 us (23%)
  starting transfers between devices  3.7 us (9%)
  between operations  0.72 us (2%)
    ppermute x3, waiting for transfers between devices, total_over_tiles(): received = lax.ppermute(sent, 'tile', pairs)  20 us
    ppermute x2, waiting for transfers between devices, body(): far = lax.ppermute(far, axes, far_pairs)  3.97 us
    pallas_call x1, Pallas kernels, body(): second_phase(near, far, state, rule, x, g, w1, w2)  2.4 us
    pallas_call x1, Pallas kernels, body(): xs, gs, pre, d_hidden, turned = own_phase(rule, x, g, w1, w2)  1.79 us
    pallas_call x1, Pallas kernels, body(): pl.pallas_call(rim_kernel, out_shape=(state_shape, rim, rim, weight, gath...  1.67 us
    ppermute x3, starting transfers between devices, total_over_tiles(): received = lax.ppermute(sent, 'tile', pairs)  1.51 us
    ppermute x2, starting transfers between devices, body(): far = lax.ppermute(far, axes, far_pairs)  1.48 us
    ppermute x2, waiting for transfers between devices, body(): near = lax.ppermute(near, axes, near_pairs)  1.35 us
  transfers between devices with their start and end apart: 9, of which 7 were waited for; matrix products, arithmetic and copies ran while one was open for 0% of the time, Pallas kernels for 14%

profile of v5, /device:TPU:28, one launch (start us, length us, event | category | flops | bytes accessed | tf_op | source)
XLA Modules:
  0.0 40.1 jit_solution(13058417512657436452)
XLA Ops:
  0.6 1.2 %shard_map.93 = (bf16[128,128]{1,0:T(8,128)(2,1)S(1)}, bf16[128,128]{1,0:T(8,128)(2,1)S(1)}, s32[2,8,128]{2,1,0:T(8,128)S(1)}, bf16[64,384]{1,0:T(8,128)(2,1)S(1...) custom-call(s32[2]{0:T(128)} %bitcast.1, ...), custom_call_target="tpu_custom_call" | custom-call | tf_op jit(solution)/shard_map/pallas_call | solution.py:365
  1.8 0.1 collective-permute-start
  1.9 1.5 %collective-permute-start.1 = (bf16[128,128]{1,0:T(8,128)(2,1)S(1)}, bf16[128,128]{1,0:T(8,128)(2,1)S(1)}, u32[]{:S(2)}, u32[]{:S(2)}) collective-permute-start(bf16[128,128]{1,0:T(8,128)(2,1)S(1)} %get-tuple-element.31), channel_id=1, source_target_pairs={{0,16},{1,2},{2,1},{3,4},{4,3},{5,6},{6,5},{7,8},{8,7},{9,10},{10,... | collective-permute-start | bytes 98312 | tf_op jit(solution)/shard_map/ppermute | solution.py:376
  3.4 1.8 %shard_map.94 = (bf16[1728,384]{1,0:T(8,128)(2,1)S(1)}, bf16[1728,384]{1,0:T(8,128)(2,1)S(1)}, f32[64,384]{1,0:T(8,128)S(1)}, f32[64,384]{1,0:T(8,128)S(1)}, bf16[64,1728]{1,0:T(8,128)(2,1)S(1)}) custom-call(s32[27,384]{1,0:T(8,128)S(1)} %get-tuple-element.32.rule_ref, bf16[64,384]{1,0:T(8,128)(2,1)S(1)} %get-tuple-element.33.x_ref, ...), custom_call_target="tpu_custom_call" | custom-call | flops 509607936 | bytes 2654208 | tf_op jit(solution)/shard_map/pallas_call | solution.py:393
  5.2 0.0 collective-permute-done.near_ref
  5.2 1.1 %collective-permute-done.1.far_ref = bf16[128,128]{1,0:T(8,128)(2,1)S(1)} collective-permute-done((bf16[128,128]{1,0:T(8,128)(2,1)S(1)}, bf16[128,128]{1,0:T(8,128)(2,1)S(1)}, u32[]{:S(2)}, u32[]{:S(2)}) %collective-permute-start.1) | collective-permute-done | bytes 32800 | tf_op jit(solution)/shard_map/ppermute | solution.py:376
  6.3 1.7 %shard_map.95 = (bf16[3,128,128]{2,1,0:T(8,128)(2,1)S(1)}, bf16[128,128]{1,0:T(8,128)(2,1)S(1)}, bf16[128,128]{1,0:T(8,128)(2,1)S(1)}, bf16[64,1728]{1,0:T(8,128...) custom-call(s32[2,8,128]{2,1,0:T(8,128)S(1)} %get-tuple-element.29.l, ...), custom_call_target="tpu_custom_call", output_to_operand_aliasing={{4}: (8, {}), {5}: (9, {})} | custom-call | tf_op jit(solution)/shard_map/pallas_call | solution.py:394
  7.9 0.1 collective-permute-start.4
  8.0 0.6 %shard_map.97 = f32[64,1728]{1,0:T(8,128)S(1)} custom-call(bf16[3,128,128]{2,1,0:T(8,128)(2,1)S(1)} %get-tuple-element.44.state_ref, bf16[1728,384]{1,0:T(8,128)(2,1)S(1)} %get-tuple-element.47.xs_ref, bf16[1728,384]{1,0:T(8,128)(2,1)S(1)} %get-tuple-element.48.gs_ref), custom_call_target="tpu_custom_call" | custom-call | tf_op jit(solution)/shard_map/pallas_call | solution.py:410
  8.6 0.9 %collective-permute-done.4 = bf16[64,1728]{1,0:T(8,128)(2,1)S(1)} collective-permute-done((bf16[64,1728]{1,0:T(8,128)(2,1)S(1)}, bf16[64,1728]{1,0:T(8,128)(2,1)S(1)}, u32[]{:S(2)}, u32[]{:S(2)}) %collective-permute-start.4) | collective-permute-done | bytes 221216 | tf_op jit(solution)/shard_map/ppermute | solution.py:311
  9.5 0.6 %collective-permute-start.5 = (bf16[64,1728]{1,0:T(8,128)(2,1)S(1)}, bf16[64,1728]{1,0:T(8,128)(2,1)S(1)}, u32[]{:S(2)}, u32[]{:S(2)}) collective-permute-start(bf16[64,1728]{1,0:T(8,128)(2,1)S(1)} %add_convert_fusion.2), channel_id=1, source_target_pairs={{0,2},{1,9},{2,0},{3,11},{4,6},{5,13},{6,4},{7,15},{8,10},{9,1},{1... | collective-permute-start | bytes 663560 | tf_op jit(solution)/shard_map/ppermute | solution.py:318
  10.1 5.5 %collective-permute-done.5 = bf16[64,1728]{1,0:T(8,128)(2,1)S(1)} collective-permute-done((bf16[64,1728]{1,0:T(8,128)(2,1)S(1)}, bf16[64,1728]{1,0:T(8,128)(2,1)S(1)}, u32[]{:S(2)}, u32[]{:S(2)}) %collective-permute-start.5) | collective-permute-done | bytes 221216 | tf_op jit(solution)/shard_map/ppermute | solution.py:318
  15.6 0.1 add_convert_fusion.1
  15.7 0.5 %collective-permute-start.6 = (bf16[64,1728]{1,0:T(8,128)(2,1)S(1)}, bf16[64,1728]{1,0:T(8,128)(2,1)S(1)}, u32[]{:S(2)}, u32[]{:S(2)}) collective-permute-start(bf16[64,1728]{1,0:T(8,128)(2,1)S(1)} %add_convert_fusion.1), channel_id=1, source_target_pairs={{0,4},{1,3},{2,6},{3,1},{4,0},{5,7},{6,2},{7,5},{8,12},{9,11},{10,... | collective-permute-start | bytes 663560 | tf_op jit(solution)/shard_map/ppermute | solution.py:318
  16.2 5.6 %collective-permute-done.6 = bf16[64,1728]{1,0:T(8,128)(2,1)S(1)} collective-permute-done((bf16[64,1728]{1,0:T(8,128)(2,1)S(1)}, bf16[64,1728]{1,0:T(8,128)(2,1)S(1)}, u32[]{:S(2)}, u32[]{:S(2)}) %collective-permute-start.6) | collective-permute-done | bytes 221216 | tf_op jit(solution)/shard_map/ppermute | solution.py:318
  21.8 0.1 add_convert_fusion
  21.8 0.4 collective-permute-start.7
  22.2 9.0 %collective-permute-done.7 = bf16[64,1728]{1,0:T(8,128)(2,1)S(1)} collective-permute-done((bf16[64,1728]{1,0:T(8,128)(2,1)S(1)}, bf16[64,1728]{1,0:T(8,128)(2,1)S(1)}, u32[]{:S(2)}, u32[]{:S(2)}) %collective-permute-start.7) | collective-permute-done | bytes 221216 | tf_op jit(solution)/shard_map/ppermute | solution.py:318
  31.2 0.1 add_multiply_fusion.total_ref
  31.3 0.1 collective-permute-start.8
  31.4 0.5 %collective-permute-start.2 = (bf16[128,128]{1,0:T(8,128)(2,1)S(1)}, bf16[128,128]{1,0:T(8,128)(2,1)S(1)}, u32[]{:S(2)}, u32[]{:S(2)}) collective-permute-start(bf16[128,128]{1,0:T(8,128)(2,1)S(1)} %get-tuple-element.42), channel_id=1, source_target_pairs={{0,1},{1,0},{2,3},{3,2},{4,5},{5,4},{6,7},{7,6},{8,9},{9,8},{10,11... | collective-permute-start | bytes 98312 | tf_op jit(solution)/shard_map/ppermute | solution.py:412
  31.9 0.0 collective-permute-start.3
  31.9 1.3 %collective-permute-done.2.near_ref = bf16[128,128]{1,0:T(8,128)(2,1)S(1)} collective-permute-done((bf16[128,128]{1,0:T(8,128)(2,1)S(1)}, bf16[128,128]{1,0:T(8,128)(2,1)S(1)}, u32[]{:S(2)}, u32[]{:S(2)}) %collective-permute-start.2) | collective-permute-done | bytes 32800 | tf_op jit(solution)/shard_map/ppermute | solution.py:412
  33.2 2.9 %collective-permute-done.3.far_ref = bf16[128,128]{1,0:T(8,128)(2,1)S(1)} collective-permute-done((bf16[128,128]{1,0:T(8,128)(2,1)S(1)}, bf16[128,128]{1,0:T(8,128)(2,1)S(1)}, u32[]{:S(2)}, u32[]{:S(2)}) %collective-permute-start.3) | collective-permute-done | bytes 32800 | tf_op jit(solution)/shard_map/ppermute | solution.py:413
  36.1 2.4 %shard_map.96 = (bf16[64,384]{1,0:T(8,128)(2,1)}, bf16[64,384]{1,0:T(8,128)(2,1)}) custom-call(bf16[128,128]{1,0:T(8,128)(2,1)S(1)} %collective-permute-done.2.near_ref, bf16[128,128]{1,0:T(8,128)(2,1)S(1)} %collective-permute-done.3.far_ref, bf16[3,128,128]{2,1,0:T(8,128)(2,1)S(1)} %get-tuple-element.44.state_ref, ...), custom_call_target="tpu_custom_call" | custom-call | flops 509607936 | bytes 2654208 | tf_op jit(solution)/shard_map/pallas_call | solution.py:428
  38.5 0.8 %shard_map.98 = (f32[64,1728]{1,0:T(8,128)}, f32[64,1728]{1,0:T(8,128)}) custom-call(f32[64,1728]{1,0:T(8,128)S(1)} %add_multiply_fusion.total_ref), custom_call_target="tpu_custom_call" | custom-call | tf_op jit(solution)/shard_map/pallas_call | solution.py:331
  39.3 0.0 collective-permute-done.8.other_ref
  39.3 0.8 %shard_map.99 = (f32[64,1728]{1,0:T(8,128)}, f32[64,1728]{1,0:T(8,128)}) custom-call(f32[64,1728]{1,0:T(8,128)S(1)} %collective-permute-done.8.other_ref, f32[64,1728]{1,0:T(8,128)} %get-tuple-element.50.first_in, f32[64,1728]{1,0:T(8,128)} %get-tuple-element.51.second_in), custom_call_target="tpu_custom_call", output_to_operand_aliasing={{0}: (1, {}), {1}: (2, {})} | custom-call | tf_op jit(solution)/shard_map/pallas_call | solution.py:332
  (1 shorter events, 0.0 us)
Async XLA Ops:
  1.8 3.4 %collective-permute-start = (bf16[128,128]{1,0:T(8,128)(2,1)S(1)}, bf16[128,128]{1,0:T(8,128)(2,1)S(1)}, u32[]{:S(2)}, u32[]{:S(2)}) collective-permute-start(bf16[128,128]{1,0:T(8,128)(2,1)S(1)} %get-tuple-element.30), channel_id=1, source_target_pairs={{0,1},{1,0},{2,3},{3,2},{4,5},{5,4},{6,7},{7,6},{8,9},{9,8},{10,11... | collective-permute-start | bytes 98312 | tf_op jit(solution)/shard_map/ppermute | solution.py:377
  1.9 4.4 %collective-permute-start.1 = (bf16[128,128]{1,0:T(8,128)(2,1)S(1)}, bf16[128,128]{1,0:T(8,128)(2,1)S(1)}, u32[]{:S(2)}, u32[]{:S(2)}) collective-permute-start(bf16[128,128]{1,0:T(8,128)(2,1)S(1)} %get-tuple-element.31), channel_id=1, source_target_pairs={{0,16},{1,2},{2,1},{3,4},{4,3},{5,6},{6,5},{7,8},{8,7},{9,10},{10,... | collective-permute-start | bytes 98312 | tf_op jit(solution)/shard_map/ppermute | solution.py:376
  7.9 1.6 %collective-permute-start.4 = (bf16[64,1728]{1,0:T(8,128)(2,1)S(1)}, bf16[64,1728]{1,0:T(8,128)(2,1)S(1)}, u32[]{:S(2)}, u32[]{:S(2)}) collective-permute-start(bf16[64,1728]{1,0:T(8,128)(2,1)S(1)} %get-tuple-element.49), channel_id=1, source_target_pairs={{0,1},{1,0},{2,3},{3,2},{4,5},{5,4},{6,7},{7,6},{8,9},{9,8},{10,11... | collective-permute-start | bytes 663560 | tf_op jit(solution)/shard_map/ppermute | solution.py:311
  9.5 6.1 %collective-permute-start.5 = (bf16[64,1728]{1,0:T(8,128)(2,1)S(1)}, bf16[64,1728]{1,0:T(8,128)(2,1)S(1)}, u32[]{:S(2)}, u32[]{:S(2)}) collective-permute-start(bf16[64,1728]{1,0:T(8,128)(2,1)S(1)} %add_convert_fusion.2), channel_id=1, source_target_pairs={{0,2},{1,9},{2,0},{3,11},{4,6},{5,13},{6,4},{7,15},{8,10},{9,1},{1... | collective-permute-start | bytes 663560 | tf_op jit(solution)/shard_map/ppermute | solution.py:318
  15.7 6.1 %collective-permute-start.6 = (bf16[64,1728]{1,0:T(8,128)(2,1)S(1)}, bf16[64,1728]{1,0:T(8,128)(2,1)S(1)}, u32[]{:S(2)}, u32[]{:S(2)}) collective-permute-start(bf16[64,1728]{1,0:T(8,128)(2,1)S(1)} %add_convert_fusion.1), channel_id=1, source_target_pairs={{0,4},{1,3},{2,6},{3,1},{4,0},{5,7},{6,2},{7,5},{8,12},{9,11},{10,... | collective-permute-start | bytes 663560 | tf_op jit(solution)/shard_map/ppermute | solution.py:318
  21.8 9.4 %collective-permute-start.7 = (bf16[64,1728]{1,0:T(8,128)(2,1)S(1)}, bf16[64,1728]{1,0:T(8,128)(2,1)S(1)}, u32[]{:S(2)}, u32[]{:S(2)}) collective-permute-start(bf16[64,1728]{1,0:T(8,128)(2,1)S(1)} %add_convert_fusion), channel_id=1, source_target_pairs={{0,8},{1,5},{2,10},{3,7},{4,12},{5,1},{6,14},{7,3},{8,0},{9,13},{1... | collective-permute-start | bytes 663560 | tf_op jit(solution)/shard_map/ppermute | solution.py:318
  31.3 8.0 %collective-permute-start.8 = (f32[64,1728]{1,0:T(8,128)S(1)}, f32[64,1728]{1,0:T(8,128)S(1)}, u32[]{:S(2)}, u32[]{:S(2)}) collective-permute-start(f32[64,1728]{1,0:T(8,128)S(1)} %add_multiply_fusion.total_ref), channel_id=1, source_target_pairs={{0,1},{1,0},{2,3},{3,2},{4,5},{5,4},{6,7},{7,6},{8,9},{9,8},{10,11... | collective-permute-start | bytes 1327112 | tf_op jit(solution)/shard_map/ppermute | solution.py:321
  31.4 1.9 %collective-permute-start.2 = (bf16[128,128]{1,0:T(8,128)(2,1)S(1)}, bf16[128,128]{1,0:T(8,128)(2,1)S(1)}, u32[]{:S(2)}, u32[]{:S(2)}) collective-permute-start(bf16[128,128]{1,0:T(8,128)(2,1)S(1)} %get-tuple-element.42), channel_id=1, source_target_pairs={{0,1},{1,0},{2,3},{3,2},{4,5},{5,4},{6,7},{7,6},{8,9},{9,8},{10,11... | collective-permute-start | bytes 98312 | tf_op jit(solution)/shard_map/ppermute | solution.py:412
  31.9 4.2 %collective-permute-start.3 = (bf16[128,128]{1,0:T(8,128)(2,1)S(1)}, bf16[128,128]{1,0:T(8,128)(2,1)S(1)}, u32[]{:S(2)}, u32[]{:S(2)}) collective-permute-start(bf16[128,128]{1,0:T(8,128)(2,1)S(1)} %get-tuple-element.43), channel_id=1, source_target_pairs={{0,16},{1,2},{2,1},{3,4},{4,3},{5,6},{6,5},{7,8},{8,7},{9,10},{10,... | collective-permute-start | bytes 98312 | tf_op jit(solution)/shard_map/ppermute | solution.py:413

commit v6 on v5

--- a/solution.py
+++ b/solution.py
@@ -11,7 +11,6 @@
 BLOCK = 128
 F32, BF16 = jnp.float32, jnp.bfloat16
 HBM = pl.BlockSpec(memory_space=pltpu.HBM)
-SMALL = pltpu.CompilerParams(vmem_limit_bytes=1 << 20)
 MEDIUM = pltpu.CompilerParams(vmem_limit_bytes=20 << 20)
 VMEM = pl.BlockSpec(memory_space=pltpu.VMEM)
 NT = (((1,), (1,)), ((), ()))
@@ -184,7 +183,7 @@
 def rim_kernel(
     lists_ref, near_ref, far_ref, pre_in, d_hidden_in, rule_ref, w1_ref, turned_ref, xs_in, gs_in,
     state_ref, near_out, far_out, send_ref, xs_ref, gs_ref,
-    pre_ref, d_hidden_ref,
+    pre_ref, d_hidden_ref, rim_ref,
 ):
     width, rows = pre_in.shape
     blocks = rows // BLOCK
@@ -197,32 +196,30 @@
     pre_ref[...] = pre_in[...]
     d_hidden_ref[...] = d_hidden_in[...]
     source_rows = lax.broadcasted_iota(jnp.int32, (BLOCK, BLOCK), 0)
+    sides = []
     for side in range(2):
         columns = pl.ds(pl.multiple_of(jnp.minimum(listed[side], blocks - 1) * BLOCK, BLOCK), BLOCK)
         start = 2 * side * group
         mirrored = offsets - group - start
+        span = slice(start * width, (start + group) * width)
+        mirror_span = slice(mirrored * width, (mirrored + group) * width)
+        sides.append((listed[side] < blocks, columns, span, mirror_span))
         local = rule_ref[start : start + group, columns] - (blocks + side) * BLOCK
-        rim_x, rim_g = [], []
         for j in range(group):
             found = jnp.dot(
                 tables[side], one_hot(source_rows, local[j : j + 1]), preferred_element_type=F32
-            )
-            rim_x.append(found[:width].astype(BF16))
-            rim_g.append(found[width:].astype(BF16))
-        rim_x = jnp.concatenate(rim_x, axis=0)
-        rim_g = jnp.concatenate(rim_g[::-1], axis=0)
-        span = slice(start * width, (start + group) * width)
-        mirror_span = slice(mirrored * width, (mirrored + group) * width)
+            ).astype(BF16)
+            rim_ref[2 * side, j * width : (j + 1) * width] = found[:width]
+            place = (group - 1 - j) * width
+            rim_ref[2 * side + 1, place : place + width] = found[width:]
+    for side, (named, columns, span, mirror_span) in enumerate(sides):
+        rim_x, rim_g = rim_ref[2 * side], rim_ref[2 * side + 1]
         pre_ref[:, columns] += jnp.dot(w1_ref[:, span], rim_x, preferred_element_type=F32)
         d_hidden_ref[:, columns] += jnp.dot(
             turned_ref[:, mirror_span], rim_g, preferred_element_type=F32
         )
-
-        @pl.when(listed[side] < blocks)
-        def _():
-            xs_ref[span, columns] = rim_x
-            gs_ref[mirror_span, columns] = rim_g
-
+        xs_ref[span, columns] = jnp.where(named, rim_x, xs_ref[span, columns])
+        gs_ref[mirror_span, columns] = jnp.where(named, rim_g, gs_ref[mirror_span, columns])
     pre = pre_ref[...]
     sigma = jax.nn.sigmoid(pre)
     hidden = (pre * sigma).astype(BF16)
@@ -255,23 +252,34 @@
         first_terms(state_ref, xs_ref, keep_ref)
 
 
-def put(source, for_odd, for_even, sem):
+def put(pieces, first_hbm, second_hbm, staging_ref, sems):
+    places = []
+    for i, (ref, row, own) in enumerate(pieces):
+        staging_ref[i] = ref[...].astype(F32)
+        places.append((i, slice(row, row + ref.shape[0]), own))
     odd = is_odd()
-    for chosen, target in ((odd, for_odd), (jnp.logical_not(odd), for_even)):
+    for chosen, mine, theirs in (
+        (odd, second_hbm, first_hbm),
+        (jnp.logical_not(odd), first_hbm, second_hbm),
+    ):
 
         @pl.when(chosen)
         def _():
-            copy = pltpu.make_async_copy(source, target, sem)
-            copy.start()
-            copy.wait()
-
-
-def put_own_kernel(total_ref, first_hbm, second_hbm, sem):
-    put(total_ref, second_hbm, first_hbm, sem)
-
-
-def put_other_kernel(other_ref, first_in, second_in, first_hbm, second_hbm, sem):
-    put(other_ref, first_hbm, second_hbm, sem)
+            copies = fetch(
+                [staging_ref.at[i] for i, _, _ in places],
+                [(mine if own else theirs).at[rows] for _, rows, own in places],
+                sems,
+            )
+            for copy in copies:
+                copy.wait()
+
+
+def put_own_kernel(own_ref, first_hbm, second_hbm, staging_ref, sems):
+    put(((own_ref, 0, True),), first_hbm, second_hbm, staging_ref, sems)
+
+
+def put_other_kernel(other_ref, first_in, second_in, first_hbm, second_hbm, staging_ref, sems):
+    put(((other_ref, 0, False),), first_hbm, second_hbm, staging_ref, sems)
 
 
 def second_kernel(
@@ -317,16 +325,17 @@
         sent = total.astype(wire)
         received = lax.ppermute(sent, "tile", pairs)
         total = sent.astype(F32) + received.astype(F32)
-    total = total * scale
+    total = (total * scale).astype(BF16)
     other = lax.ppermute(total, "tile", cores)
     result = jax.ShapeDtypeStruct(total.shape, F32)
+    staging = [pltpu.VMEM((1, *total.shape), F32), pltpu.SemaphoreType.DMA((1,))]
     put_own = pl.pallas_call(
         put_own_kernel,
         out_shape=(result, result),
         in_specs=[VMEM],
         out_specs=(HBM, HBM),
-        scratch_shapes=[pltpu.SemaphoreType.DMA],
-        compiler_params=SMALL,
+        scratch_shapes=staging,
+        compiler_params=MEDIUM,
     )
     half = put_own(total)
     return pl.pallas_call(
@@ -334,9 +343,9 @@
         out_shape=(result, result),
         in_specs=[VMEM, HBM, HBM],
         out_specs=(HBM, HBM),
-        scratch_shapes=[pltpu.SemaphoreType.DMA],
+        scratch_shapes=staging,
         input_output_aliases={1: 0, 2: 1},
-        compiler_params=SMALL,
+        compiler_params=MEDIUM,
     )(other, *half)
 
 
@@ -396,7 +405,11 @@
         out_shape=(state_shape, rim, rim, weight, gathered, gathered),
         in_specs=[VMEM] * 10,
         out_specs=(VMEM,) * 6,
-        scratch_shapes=[pltpu.VMEM((width, rows), F32), pltpu.VMEM((width, rows), F32)],
+        scratch_shapes=[
+            pltpu.VMEM((width, rows), F32),
+            pltpu.VMEM((width, rows), F32),
+            pltpu.VMEM((4, offsets // 3 * width, BLOCK), BF16),
+        ],
         input_output_aliases={8: 4, 9: 5},
         compiler_params=MEDIUM,
     )(lists, near, far, pre, d_hidden, rule, w1, turned, xs, gs)

time: 40.2 us -> 39.9 us (level)
  no operation moved by 1% of the time
where the time goes in v6:
time: 39.9 us; the launch traced here: 39.8 us
  waiting for transfers between devices  26.3 us (66%)
  Pallas kernels  8.85 us (22%)
  starting transfers between devices  3.69 us (9%)
  between operations  0.72 us (2%)
    ppermute x3, waiting for transfers between devices, total_over_tiles(): received = lax.ppermute(sent, 'tile', pairs)  20.1 us
    ppermute x2, waiting for transfers between devices, body(): far = lax.ppermute(far, axes, far_pairs)  4.3 us
    pallas_call x1, Pallas kernels, body(): second_phase(near, far, state, rule, x, g, w1, w2)  2.39 us
    pallas_call x1, Pallas kernels, body(): xs, gs, pre, d_hidden, turned = own_phase(rule, x, g, w1, w2)  1.79 us
    ppermute x3, starting transfers between devices, total_over_tiles(): received = lax.ppermute(sent, 'tile', pairs)  1.5 us
    ppermute x2, starting transfers between devices, body(): far = lax.ppermute(far, axes, far_pairs)  1.48 us
    pallas_call x1, Pallas kernels, body(): pl.pallas_call(rim_kernel, out_shape=(state_shape, rim, rim, weight, gath...  1.29 us
    pallas_call x1, Pallas kernels, body(): pl.pallas_call(load_kernel, out_shape=(rim, rim, shape((2, 8, BLOCK), jnp...  1.19 us
  transfers between devices with their start and end apart: 9, of which 7 were waited for; matrix products, arithmetic and copies ran while one was open for 0% of the time, Pallas kernels for 14%

profile of v6, /device:TPU:28, one launch (start us, length us, event | category | flops | bytes accessed | tf_op | source)
XLA Modules:
  0.0 39.8 jit_solution(9785402989522260589)
XLA Ops:
  0.6 1.2 %shard_map.93 = (bf16[128,128]{1,0:T(8,128)(2,1)S(1)}, bf16[128,128]{1,0:T(8,128)(2,1)S(1)}, s32[2,8,128]{2,1,0:T(8,128)S(1)}, bf16[64,384]{1,0:T(8,128)(2,1)S(1...) custom-call(s32[2]{0:T(128)} %bitcast.1, ...), custom_call_target="tpu_custom_call" | custom-call | tf_op jit(solution)/shard_map/pallas_call | solution.py:374
  1.8 0.1 collective-permute-start
  1.9 1.5 %collective-permute-start.1 = (bf16[128,128]{1,0:T(8,128)(2,1)S(1)}, bf16[128,128]{1,0:T(8,128)(2,1)S(1)}, u32[]{:S(2)}, u32[]{:S(2)}) collective-permute-start(bf16[128,128]{1,0:T(8,128)(2,1)S(1)} %get-tuple-element.31), channel_id=1, source_target_pairs={{0,16},{1,2},{2,1},{3,4},{4,3},{5,6},{6,5},{7,8},{8,7},{9,10},{10,... | collective-permute-start | bytes 98312 | tf_op jit(solution)/shard_map/ppermute | solution.py:385
  3.4 1.8 %shard_map.94 = (bf16[1728,384]{1,0:T(8,128)(2,1)S(1)}, bf16[1728,384]{1,0:T(8,128)(2,1)S(1)}, f32[64,384]{1,0:T(8,128)S(1)}, f32[64,384]{1,0:T(8,128)S(1)}, bf16[64,1728]{1,0:T(8,128)(2,1)S(1)}) custom-call(s32[27,384]{1,0:T(8,128)S(1)} %get-tuple-element.32.rule_ref, bf16[64,384]{1,0:T(8,128)(2,1)S(1)} %get-tuple-element.33.x_ref, ...), custom_call_target="tpu_custom_call" | custom-call | flops 509607936 | bytes 2654208 | tf_op jit(solution)/shard_map/pallas_call | solution.py:402
  5.2 0.0 collective-permute-done.near_ref
  5.2 1.1 %collective-permute-done.1.far_ref = bf16[128,128]{1,0:T(8,128)(2,1)S(1)} collective-permute-done((bf16[128,128]{1,0:T(8,128)(2,1)S(1)}, bf16[128,128]{1,0:T(8,128)(2,1)S(1)}, u32[]{:S(2)}, u32[]{:S(2)}) %collective-permute-start.1) | collective-permute-done | bytes 32800 | tf_op jit(solution)/shard_map/ppermute | solution.py:385
  6.3 1.3 %shard_map.95 = (bf16[3,128,128]{2,1,0:T(8,128)(2,1)S(1)}, bf16[128,128]{1,0:T(8,128)(2,1)S(1)}, bf16[128,128]{1,0:T(8,128)(2,1)S(1)}, bf16[64,1728]{1,0:T(8,128...) custom-call(s32[2,8,128]{2,1,0:T(8,128)S(1)} %get-tuple-element.29.l, ...), custom_call_target="tpu_custom_call", output_to_operand_aliasing={{4}: (8, {}), {5}: (9, {})} | custom-call | tf_op jit(solution)/shard_map/pallas_call | solution.py:403
  7.6 0.1 collective-permute-start.4
  7.7 0.6 %shard_map.97 = f32[64,1728]{1,0:T(8,128)S(1)} custom-call(bf16[3,128,128]{2,1,0:T(8,128)(2,1)S(1)} %get-tuple-element.44.state_ref, bf16[1728,384]{1,0:T(8,128)(2,1)S(1)} %get-tuple-element.47.xs_ref, bf16[1728,384]{1,0:T(8,128)(2,1)S(1)} %get-tuple-element.48.gs_ref), custom_call_target="tpu_custom_call" | custom-call | tf_op jit(solution)/shard_map/pallas_call | solution.py:423
  8.2 0.9 %collective-permute-done.4 = bf16[64,1728]{1,0:T(8,128)(2,1)S(1)} collective-permute-done((bf16[64,1728]{1,0:T(8,128)(2,1)S(1)}, bf16[64,1728]{1,0:T(8,128)(2,1)S(1)}, u32[]{:S(2)}, u32[]{:S(2)}) %collective-permute-start.4) | collective-permute-done | bytes 221216 | tf_op jit(solution)/shard_map/ppermute | solution.py:319
  9.2 0.6 %collective-permute-start.5 = (bf16[64,1728]{1,0:T(8,128)(2,1)S(1)}, bf16[64,1728]{1,0:T(8,128)(2,1)S(1)}, u32[]{:S(2)}, u32[]{:S(2)}) collective-permute-start(bf16[64,1728]{1,0:T(8,128)(2,1)S(1)} %add_convert_fusion.2), channel_id=1, source_target_pairs={{0,2},{1,9},{2,0},{3,11},{4,6},{5,13},{6,4},{7,15},{8,10},{9,1},{1... | collective-permute-start | bytes 663560 | tf_op jit(solution)/shard_map/ppermute | solution.py:326
  9.8 5.5 %collective-permute-done.5 = bf16[64,1728]{1,0:T(8,128)(2,1)S(1)} collective-permute-done((bf16[64,1728]{1,0:T(8,128)(2,1)S(1)}, bf16[64,1728]{1,0:T(8,128)(2,1)S(1)}, u32[]{:S(2)}, u32[]{:S(2)}) %collective-permute-start.5) | collective-permute-done | bytes 221216 | tf_op jit(solution)/shard_map/ppermute | solution.py:326
  15.3 0.1 add_convert_fusion.1
  15.3 0.5 %collective-permute-start.6 = (bf16[64,1728]{1,0:T(8,128)(2,1)S(1)}, bf16[64,1728]{1,0:T(8,128)(2,1)S(1)}, u32[]{:S(2)}, u32[]{:S(2)}) collective-permute-start(bf16[64,1728]{1,0:T(8,128)(2,1)S(1)} %add_convert_fusion.1), channel_id=1, source_target_pairs={{0,4},{1,3},{2,6},{3,1},{4,0},{5,7},{6,2},{7,5},{8,12},{9,11},{10,... | collective-permute-start | bytes 663560 | tf_op jit(solution)/shard_map/ppermute | solution.py:326
  15.8 5.6 %collective-permute-done.6 = bf16[64,1728]{1,0:T(8,128)(2,1)S(1)} collective-permute-done((bf16[64,1728]{1,0:T(8,128)(2,1)S(1)}, bf16[64,1728]{1,0:T(8,128)(2,1)S(1)}, u32[]{:S(2)}, u32[]{:S(2)}) %collective-permute-start.6) | collective-permute-done | bytes 221216 | tf_op jit(solution)/shard_map/ppermute | solution.py:326
  21.4 0.1 add_convert_fusion
  21.5 0.4 collective-permute-start.7
  21.9 9.0 %collective-permute-done.7 = bf16[64,1728]{1,0:T(8,128)(2,1)S(1)} collective-permute-done((bf16[64,1728]{1,0:T(8,128)(2,1)S(1)}, bf16[64,1728]{1,0:T(8,128)(2,1)S(1)}, u32[]{:S(2)}, u32[]{:S(2)}) %collective-permute-start.7) | collective-permute-done | bytes 221216 | tf_op jit(solution)/shard_map/ppermute | solution.py:326
  30.8 0.1 multiply_convert_fusion.own_ref
  30.9 0.1 collective-permute-start.8
  31.0 0.5 %collective-permute-start.2 = (bf16[128,128]{1,0:T(8,128)(2,1)S(1)}, bf16[128,128]{1,0:T(8,128)(2,1)S(1)}, u32[]{:S(2)}, u32[]{:S(2)}) collective-permute-start(bf16[128,128]{1,0:T(8,128)(2,1)S(1)} %get-tuple-element.42), channel_id=1, source_target_pairs={{0,1},{1,0},{2,3},{3,2},{4,5},{5,4},{6,7},{7,6},{8,9},{9,8},{10,11... | collective-permute-start | bytes 98312 | tf_op jit(solution)/shard_map/ppermute | solution.py:425
  31.5 0.0 collective-permute-start.3
  31.5 1.0 %collective-permute-done.2.near_ref = bf16[128,128]{1,0:T(8,128)(2,1)S(1)} collective-permute-done((bf16[128,128]{1,0:T(8,128)(2,1)S(1)}, bf16[128,128]{1,0:T(8,128)(2,1)S(1)}, u32[]{:S(2)}, u32[]{:S(2)}) %collective-permute-start.2) | collective-permute-done | bytes 32800 | tf_op jit(solution)/shard_map/ppermute | solution.py:425
  32.5 3.2 %collective-permute-done.3.far_ref = bf16[128,128]{1,0:T(8,128)(2,1)S(1)} collective-permute-done((bf16[128,128]{1,0:T(8,128)(2,1)S(1)}, bf16[128,128]{1,0:T(8,128)(2,1)S(1)}, u32[]{:S(2)}, u32[]{:S(2)}) %collective-permute-start.3) | collective-permute-done | bytes 32800 | tf_op jit(solution)/shard_map/ppermute | solution.py:426
  35.7 2.4 %shard_map.96 = (bf16[64,384]{1,0:T(8,128)(2,1)}, bf16[64,384]{1,0:T(8,128)(2,1)}) custom-call(bf16[128,128]{1,0:T(8,128)(2,1)S(1)} %collective-permute-done.2.near_ref, bf16[128,128]{1,0:T(8,128)(2,1)S(1)} %collective-permute-done.3.far_ref, bf16[3,128,128]{2,1,0:T(8,128)(2,1)S(1)} %get-tuple-element.44.state_ref, ...), custom_call_target="tpu_custom_call" | custom-call | flops 509607936 | bytes 2654208 | tf_op jit(solution)/shard_map/pallas_call | solution.py:441
  38.1 0.8 %shard_map.98 = (f32[64,1728]{1,0:T(8,128)}, f32[64,1728]{1,0:T(8,128)}) custom-call(bf16[64,1728]{1,0:T(8,128)(2,1)S(1)} %multiply_convert_fusion.own_ref), custom_call_target="tpu_custom_call" | custom-call | tf_op jit(solution)/shard_map/pallas_call | solution.py:340
  38.9 0.0 collective-permute-done.8.other_ref
  39.0 0.8 %shard_map.99 = (f32[64,1728]{1,0:T(8,128)}, f32[64,1728]{1,0:T(8,128)}) custom-call(bf16[64,1728]{1,0:T(8,128)(2,1)S(1)} %collective-permute-done.8.other_ref, f32[64,1728]{1,0:T(8,128)} %get-tuple-element.50.first_in, f32[64,1728]{1,0:T(8,128)} %get-tuple-element.51.second_in), custom_call_target="tpu_custom_call", output_to_operand_aliasing={{0}: (1, {}), {1}: (2, {})} | custom-call | tf_op jit(solution)/shard_map/pallas_call | solution.py:341
  (1 shorter events, 0.0 us)
Async XLA Ops:
  1.8 3.4 %collective-permute-start = (bf16[128,128]{1,0:T(8,128)(2,1)S(1)}, bf16[128,128]{1,0:T(8,128)(2,1)S(1)}, u32[]{:S(2)}, u32[]{:S(2)}) collective-permute-start(bf16[128,128]{1,0:T(8,128)(2,1)S(1)} %get-tuple-element.30), channel_id=1, source_target_pairs={{0,1},{1,0},{2,3},{3,2},{4,5},{5,4},{6,7},{7,6},{8,9},{9,8},{10,11... | collective-permute-start | bytes 98312 | tf_op jit(solution)/shard_map/ppermute | solution.py:386
  1.9 4.4 %collective-permute-start.1 = (bf16[128,128]{1,0:T(8,128)(2,1)S(1)}, bf16[128,128]{1,0:T(8,128)(2,1)S(1)}, u32[]{:S(2)}, u32[]{:S(2)}) collective-permute-start(bf16[128,128]{1,0:T(8,128)(2,1)S(1)} %get-tuple-element.31), channel_id=1, source_target_pairs={{0,16},{1,2},{2,1},{3,4},{4,3},{5,6},{6,5},{7,8},{8,7},{9,10},{10,... | collective-permute-start | bytes 98312 | tf_op jit(solution)/shard_map/ppermute | solution.py:385
  7.6 1.6 %collective-permute-start.4 = (bf16[64,1728]{1,0:T(8,128)(2,1)S(1)}, bf16[64,1728]{1,0:T(8,128)(2,1)S(1)}, u32[]{:S(2)}, u32[]{:S(2)}) collective-permute-start(bf16[64,1728]{1,0:T(8,128)(2,1)S(1)} %get-tuple-element.49), channel_id=1, source_target_pairs={{0,1},{1,0},{2,3},{3,2},{4,5},{5,4},{6,7},{7,6},{8,9},{9,8},{10,11... | collective-permute-start | bytes 663560 | tf_op jit(solution)/shard_map/ppermute | solution.py:319
  9.2 6.1 %collective-permute-start.5 = (bf16[64,1728]{1,0:T(8,128)(2,1)S(1)}, bf16[64,1728]{1,0:T(8,128)(2,1)S(1)}, u32[]{:S(2)}, u32[]{:S(2)}) collective-permute-start(bf16[64,1728]{1,0:T(8,128)(2,1)S(1)} %add_convert_fusion.2), channel_id=1, source_target_pairs={{0,2},{1,9},{2,0},{3,11},{4,6},{5,13},{6,4},{7,15},{8,10},{9,1},{1... | collective-permute-start | bytes 663560 | tf_op jit(solution)/shard_map/ppermute | solution.py:326
  15.3 6.1 %collective-permute-start.6 = (bf16[64,1728]{1,0:T(8,128)(2,1)S(1)}, bf16[64,1728]{1,0:T(8,128)(2,1)S(1)}, u32[]{:S(2)}, u32[]{:S(2)}) collective-permute-start(bf16[64,1728]{1,0:T(8,128)(2,1)S(1)} %add_convert_fusion.1), channel_id=1, source_target_pairs={{0,4},{1,3},{2,6},{3,1},{4,0},{5,7},{6,2},{7,5},{8,12},{9,11},{10,... | collective-permute-start | bytes 663560 | tf_op jit(solution)/shard_map/ppermute | solution.py:326
  21.5 9.4 %collective-permute-start.7 = (bf16[64,1728]{1,0:T(8,128)(2,1)S(1)}, bf16[64,1728]{1,0:T(8,128)(2,1)S(1)}, u32[]{:S(2)}, u32[]{:S(2)}) collective-permute-start(bf16[64,1728]{1,0:T(8,128)(2,1)S(1)} %add_convert_fusion), channel_id=1, source_target_pairs={{0,8},{1,5},{2,10},{3,7},{4,12},{5,1},{6,14},{7,3},{8,0},{9,13},{1... | collective-permute-start | bytes 663560 | tf_op jit(solution)/shard_map/ppermute | solution.py:326
  30.9 8.0 %collective-permute-start.8 = (bf16[64,1728]{1,0:T(8,128)(2,1)S(1)}, bf16[64,1728]{1,0:T(8,128)(2,1)S(1)}, u32[]{:S(2)}, u32[]{:S(2)}) collective-permute-start(bf16[64,1728]{1,0:T(8,128)(2,1)S(1)} %multiply_convert_fusion.own_ref), channel_id=1, source_target_pairs={{0,1},{1,0},{2,3},{3,2},{4,5},{5,4},{6,7},{7,6},{8,9},{9,8},{10,11... | collective-permute-start | bytes 663560 | tf_op jit(solution)/shard_map/ppermute | solution.py:329
  31.0 1.5 %collective-permute-start.2 = (bf16[128,128]{1,0:T(8,128)(2,1)S(1)}, bf16[128,128]{1,0:T(8,128)(2,1)S(1)}, u32[]{:S(2)}, u32[]{:S(2)}) collective-permute-start(bf16[128,128]{1,0:T(8,128)(2,1)S(1)} %get-tuple-element.42), channel_id=1, source_target_pairs={{0,1},{1,0},{2,3},{3,2},{4,5},{5,4},{6,7},{7,6},{8,9},{9,8},{10,11... | collective-permute-start | bytes 98312 | tf_op jit(solution)/shard_map/ppermute | solution.py:425
  31.5 4.2 %collective-permute-start.3 = (bf16[128,128]{1,0:T(8,128)(2,1)S(1)}, bf16[128,128]{1,0:T(8,128)(2,1)S(1)}, u32[]{:S(2)}, u32[]{:S(2)}) collective-permute-start(bf16[128,128]{1,0:T(8,128)(2,1)S(1)} %get-tuple-element.43), channel_id=1, source_target_pairs={{0,16},{1,2},{2,1},{3,4},{4,3},{5,6},{6,5},{7,8},{8,7},{9,10},{10,... | collective-permute-start | bytes 98312 | tf_op jit(solution)/shard_map/ppermute | solution.py:426

commit v7 on v6

--- a/solution.py
+++ b/solution.py
@@ -14,6 +14,11 @@
 MEDIUM = pltpu.CompilerParams(vmem_limit_bytes=20 << 20)
 VMEM = pl.BlockSpec(memory_space=pltpu.VMEM)
 NT = (((1,), (1,)), ((), ()))
+
+
+def in_chunks(ref, count=4):
+    rows = ref.shape[0] // count
+    return [ref.at[i * rows : (i + 1) * rows] for i in range(count)]
 
 
 def is_odd():
@@ -42,8 +47,8 @@
 ):
     width, rows = x_ref.shape
     copies = fetch(
-        (lists_hbm, x_hbm, g_hbm, rule_hbm, w2_hbm, w1_hbm),
-        (lists_ref, x_ref, g_ref, rule_ref, w2_ref, w1_ref),
+        (lists_hbm, x_hbm, g_hbm, rule_hbm, *in_chunks(w2_hbm), *in_chunks(w1_hbm)),
+        (lists_ref, x_ref, g_ref, rule_ref, *in_chunks(w2_ref), *in_chunks(w1_ref)),
         sems,
     )
     for copy in copies[:3]:
@@ -69,6 +74,16 @@
     return (rows == line).astype(F32).astype(BF16)
 
 
+def select_rows(table, rows, local):
+    found = []
+    for j in range(0, local.shape[0], 2):
+        lines = [local[i : i + 1] for i in range(j, min(j + 2, local.shape[0]))]
+        choice = jnp.concatenate([one_hot(rows, line) for line in lines], axis=1)
+        both = jnp.dot(table, choice, preferred_element_type=F32).astype(BF16)
+        found += [both[:, i * BLOCK : (i + 1) * BLOCK] for i in range(len(lines))]
+    return found
+
+
 def gather(table_ref, rule_ref, first_ref, second_ref, blocks):
     offsets = rule_ref.shape[0]
     group = offsets // 3
@@ -77,10 +92,8 @@
     source_rows = lax.broadcasted_iota(jnp.int32, (BLOCK, BLOCK), 0)
 
     def store(k, low, high, found, mirrored):
-        first_ref[k * width : (k + 1) * width, low:high] = found[:width].astype(BF16)
-        second_ref[mirrored * width : (mirrored + 1) * width, low:high] = found[
-            width:
-        ].astype(BF16)
+        first_ref[k * width : (k + 1) * width, low:high] = found[:width]
+        second_ref[mirrored * width : (mirrored + 1) * width, low:high] = found[width:]
 
     strays = jnp.zeros((group, BLOCK), jnp.int32)
     for block in range(blocks):
@@ -97,11 +110,8 @@
             strays = strays | (
                 named & ((local < 0) | (local >= BLOCK))
             ).astype(jnp.int32)
-            table = table_ref[source]
-            for j in range(group):
+            for j, found in enumerate(select_rows(table_ref[source], source_rows, local)):
                 k = side * group + j
-                choice = one_hot(source_rows, local[j : j + 1])
-                found = jnp.dot(table, choice, preferred_element_type=F32)
                 store(k, low, high, found, offsets - 1 - k)
 
     @pl.when(jnp.max(strays.astype(F32)) > 0)
@@ -205,10 +215,7 @@
         mirror_span = slice(mirrored * width, (mirrored + group) * width)
         sides.append((listed[side] < blocks, columns, span, mirror_span))
         local = rule_ref[start : start + group, columns] - (blocks + side) * BLOCK
-        for j in range(group):
-            found = jnp.dot(
-                tables[side], one_hot(source_rows, local[j : j + 1]), preferred_element_type=F32
-            ).astype(BF16)
+        for j, found in enumerate(select_rows(tables[side], source_rows, local)):
             rim_ref[2 * side, j * width : (j + 1) * width] = found[:width]
             place = (group - 1 - j) * width
             rim_ref[2 * side + 1, place : place + width] = found[width:]
@@ -252,34 +259,28 @@
         first_terms(state_ref, xs_ref, keep_ref)
 
 
-def put(pieces, first_hbm, second_hbm, staging_ref, sems):
-    places = []
-    for i, (ref, row, own) in enumerate(pieces):
-        staging_ref[i] = ref[...].astype(F32)
-        places.append((i, slice(row, row + ref.shape[0]), own))
+def put(source_ref, for_odd, for_even, staging_ref, sems):
     odd = is_odd()
-    for chosen, mine, theirs in (
-        (odd, second_hbm, first_hbm),
-        (jnp.logical_not(odd), first_hbm, second_hbm),
-    ):
+    for chosen, target in ((odd, for_odd), (jnp.logical_not(odd), for_even)):
 
         @pl.when(chosen)
         def _():
-            copies = fetch(
-                [staging_ref.at[i] for i, _, _ in places],
-                [(mine if own else theirs).at[rows] for _, rows, own in places],
-                sems,
-            )
+            copies = []
+            chunks = zip(in_chunks(source_ref), in_chunks(staging_ref), in_chunks(target))
+            for i, (source, staging, place) in enumerate(chunks):
+                staging[...] = source[...].astype(F32)
+                copies.append(pltpu.make_async_copy(staging, place, sems.at[i]))
+                copies[-1].start()
             for copy in copies:
                 copy.wait()
 
 
 def put_own_kernel(own_ref, first_hbm, second_hbm, staging_ref, sems):
-    put(((own_ref, 0, True),), first_hbm, second_hbm, staging_ref, sems)
+    put(own_ref, second_hbm, first_hbm, staging_ref, sems)
 
 
 def put_other_kernel(other_ref, first_in, second_in, first_hbm, second_hbm, staging_ref, sems):
-    put(((other_ref, 0, False),), first_hbm, second_hbm, staging_ref, sems)
+    put(other_ref, first_hbm, second_hbm, staging_ref, sems)
 
 
 def second_kernel(
@@ -328,7 +329,7 @@
     total = (total * scale).astype(BF16)
     other = lax.ppermute(total, "tile", cores)
     result = jax.ShapeDtypeStruct(total.shape, F32)
-    staging = [pltpu.VMEM((1, *total.shape), F32), pltpu.SemaphoreType.DMA((1,))]
+    staging = [pltpu.VMEM(total.shape, F32), pltpu.SemaphoreType.DMA((4,))]
     put_own = pl.pallas_call(
         put_own_kernel,
         out_shape=(result, result),
@@ -379,7 +380,7 @@
         ),
         in_specs=[HBM] * 6,
         out_specs=(VMEM,) * 8,
-        scratch_shapes=[pltpu.SMEM((2,), jnp.int32), pltpu.SemaphoreType.DMA((6,))],
+        scratch_shapes=[pltpu.SMEM((2,), jnp.int32), pltpu.SemaphoreType.DMA((12,))],
         compiler_params=MEDIUM,
     )(send_lists, features, cotangent, rulebook, weight_second, weight_first)
     far = lax.ppermute(far, axes, far_pairs)

time: 39.9 us -> 39.9 us (level)
  no operation moved by 1% of the time
where the time goes in v7:
time: 39.9 us; the launch traced here: 39.7 us
  waiting for transfers between devices  26.3 us (66%)
  Pallas kernels  8.75 us (22%)
  starting transfers between devices  3.72 us (9%)
  between operations  0.72 us (2%)
    ppermute x3, waiting for transfers between devices, total_over_tiles(): received = lax.ppermute(sent, 'tile', pairs)  20 us
    ppermute x2, waiting for transfers between devices, body(): far = lax.ppermute(far, axes, far_pairs)  4.33 us
    pallas_call x1, Pallas kernels, body(): second_phase(near, far, state, rule, x, g, w1, w2)  2.35 us
    pallas_call x1, Pallas kernels, body(): xs, gs, pre, d_hidden, turned = own_phase(rule, x, g, w1, w2)  1.75 us
    ppermute x3, starting transfers between devices, total_over_tiles(): received = lax.ppermute(sent, 'tile', pairs)  1.53 us
    ppermute x2, starting transfers between devices, body(): far = lax.ppermute(far, axes, far_pairs)  1.48 us
    pallas_call x1, Pallas kernels, body(): pl.pallas_call(rim_kernel, out_shape=(state_shape, rim, rim, weight, gath...  1.26 us
    pallas_call x1, Pallas kernels, body(): pl.pallas_call(load_kernel, out_shape=(rim, rim, shape((2, 8, BLOCK), jnp...  1.2 us
  transfers between devices with their start and end apart: 9, of which 7 were waited for; matrix products, arithmetic and copies ran while one was open for 0% of the time, Pallas kernels for 14%

profile of v7, /device:TPU:28, one launch (start us, length us, event | category | flops | bytes accessed | tf_op | source)
XLA Modules:
  0.0 39.7 jit_solution(6021339156620045486)
XLA Ops:
  0.6 1.2 %shard_map.93 = (bf16[128,128]{1,0:T(8,128)(2,1)S(1)}, bf16[128,128]{1,0:T(8,128)(2,1)S(1)}, s32[2,8,128]{2,1,0:T(8,128)S(1)}, bf16[64,384]{1,0:T(8,128)(2,1)S(1...) custom-call(s32[2]{0:T(128)} %bitcast.1, ...), custom_call_target="tpu_custom_call" | custom-call | tf_op jit(solution)/shard_map/pallas_call | solution.py:375
  1.8 0.1 collective-permute-start
  1.9 1.5 %collective-permute-start.1 = (bf16[128,128]{1,0:T(8,128)(2,1)S(1)}, bf16[128,128]{1,0:T(8,128)(2,1)S(1)}, u32[]{:S(2)}, u32[]{:S(2)}) collective-permute-start(bf16[128,128]{1,0:T(8,128)(2,1)S(1)} %get-tuple-element.31), channel_id=1, source_target_pairs={{0,16},{1,2},{2,1},{3,4},{4,3},{5,6},{6,5},{7,8},{8,7},{9,10},{10,... | collective-permute-start | bytes 98312 | tf_op jit(solution)/shard_map/ppermute | solution.py:386
  3.4 1.7 %shard_map.94 = (bf16[1728,384]{1,0:T(8,128)(2,1)S(1)}, bf16[1728,384]{1,0:T(8,128)(2,1)S(1)}, f32[64,384]{1,0:T(8,128)S(1)}, f32[64,384]{1,0:T(8,128)S(1)}, bf16[64,1728]{1,0:T(8,128)(2,1)S(1)}) custom-call(s32[27,384]{1,0:T(8,128)S(1)} %get-tuple-element.32.rule_ref, bf16[64,384]{1,0:T(8,128)(2,1)S(1)} %get-tuple-element.33.x_ref, ...), custom_call_target="tpu_custom_call" | custom-call | flops 509607936 | bytes 2654208 | tf_op jit(solution)/shard_map/pallas_call | solution.py:403
  5.2 0.0 collective-permute-done.near_ref
  5.2 1.1 %collective-permute-done.1.far_ref = bf16[128,128]{1,0:T(8,128)(2,1)S(1)} collective-permute-done((bf16[128,128]{1,0:T(8,128)(2,1)S(1)}, bf16[128,128]{1,0:T(8,128)(2,1)S(1)}, u32[]{:S(2)}, u32[]{:S(2)}) %collective-permute-start.1) | collective-permute-done | bytes 32800 | tf_op jit(solution)/shard_map/ppermute | solution.py:386
  6.3 1.3 %shard_map.95 = (bf16[3,128,128]{2,1,0:T(8,128)(2,1)S(1)}, bf16[128,128]{1,0:T(8,128)(2,1)S(1)}, bf16[128,128]{1,0:T(8,128)(2,1)S(1)}, bf16[64,1728]{1,0:T(8,128...) custom-call(s32[2,8,128]{2,1,0:T(8,128)S(1)} %get-tuple-element.29.l, ...), custom_call_target="tpu_custom_call", output_to_operand_aliasing={{4}: (8, {}), {5}: (9, {})} | custom-call | tf_op jit(solution)/shard_map/pallas_call | solution.py:404
  7.5 0.1 collective-permute-start.4
  7.6 0.6 %shard_map.97 = f32[64,1728]{1,0:T(8,128)S(1)} custom-call(bf16[3,128,128]{2,1,0:T(8,128)(2,1)S(1)} %get-tuple-element.44.state_ref, bf16[1728,384]{1,0:T(8,128)(2,1)S(1)} %get-tuple-element.47.xs_ref, bf16[1728,384]{1,0:T(8,128)(2,1)S(1)} %get-tuple-element.48.gs_ref), custom_call_target="tpu_custom_call" | custom-call | tf_op jit(solution)/shard_map/pallas_call | solution.py:424
  8.2 0.9 %collective-permute-done.4 = bf16[64,1728]{1,0:T(8,128)(2,1)S(1)} collective-permute-done((bf16[64,1728]{1,0:T(8,128)(2,1)S(1)}, bf16[64,1728]{1,0:T(8,128)(2,1)S(1)}, u32[]{:S(2)}, u32[]{:S(2)}) %collective-permute-start.4) | collective-permute-done | bytes 221216 | tf_op jit(solution)/shard_map/ppermute | solution.py:320
  9.1 0.6 %collective-permute-start.5 = (bf16[64,1728]{1,0:T(8,128)(2,1)S(1)}, bf16[64,1728]{1,0:T(8,128)(2,1)S(1)}, u32[]{:S(2)}, u32[]{:S(2)}) collective-permute-start(bf16[64,1728]{1,0:T(8,128)(2,1)S(1)} %add_convert_fusion.2), channel_id=1, source_target_pairs={{0,2},{1,9},{2,0},{3,11},{4,6},{5,13},{6,4},{7,15},{8,10},{9,1},{1... | collective-permute-start | bytes 663560 | tf_op jit(solution)/shard_map/ppermute | solution.py:327
  9.7 5.5 %collective-permute-done.5 = bf16[64,1728]{1,0:T(8,128)(2,1)S(1)} collective-permute-done((bf16[64,1728]{1,0:T(8,128)(2,1)S(1)}, bf16[64,1728]{1,0:T(8,128)(2,1)S(1)}, u32[]{:S(2)}, u32[]{:S(2)}) %collective-permute-start.5) | collective-permute-done | bytes 221216 | tf_op jit(solution)/shard_map/ppermute | solution.py:327
  15.2 0.1 add_convert_fusion.1
  15.3 0.5 %collective-permute-start.6 = (bf16[64,1728]{1,0:T(8,128)(2,1)S(1)}, bf16[64,1728]{1,0:T(8,128)(2,1)S(1)}, u32[]{:S(2)}, u32[]{:S(2)}) collective-permute-start(bf16[64,1728]{1,0:T(8,128)(2,1)S(1)} %add_convert_fusion.1), channel_id=1, source_target_pairs={{0,4},{1,3},{2,6},{3,1},{4,0},{5,7},{6,2},{7,5},{8,12},{9,11},{10,... | collective-permute-start | bytes 663560 | tf_op jit(solution)/shard_map/ppermute | solution.py:327
  15.8 5.6 %collective-permute-done.6 = bf16[64,1728]{1,0:T(8,128)(2,1)S(1)} collective-permute-done((bf16[64,1728]{1,0:T(8,128)(2,1)S(1)}, bf16[64,1728]{1,0:T(8,128)(2,1)S(1)}, u32[]{:S(2)}, u32[]{:S(2)}) %collective-permute-start.6) | collective-permute-done | bytes 221216 | tf_op jit(solution)/shard_map/ppermute | solution.py:327
  21.4 0.1 add_convert_fusion
  21.4 0.4 %collective-permute-start.7 = (bf16[64,1728]{1,0:T(8,128)(2,1)S(1)}, bf16[64,1728]{1,0:T(8,128)(2,1)S(1)}, u32[]{:S(2)}, u32[]{:S(2)}) collective-permute-start(bf16[64,1728]{1,0:T(8,128)(2,1)S(1)} %add_convert_fusion), channel_id=1, source_target_pairs={{0,8},{1,5},{2,10},{3,7},{4,12},{5,1},{6,14},{7,3},{8,0},{9,13},{1... | collective-permute-start | bytes 663560 | tf_op jit(solution)/shard_map/ppermute | solution.py:327
  21.8 9.0 %collective-permute-done.7 = bf16[64,1728]{1,0:T(8,128)(2,1)S(1)} collective-permute-done((bf16[64,1728]{1,0:T(8,128)(2,1)S(1)}, bf16[64,1728]{1,0:T(8,128)(2,1)S(1)}, u32[]{:S(2)}, u32[]{:S(2)}) %collective-permute-start.7) | collective-permute-done | bytes 221216 | tf_op jit(solution)/shard_map/ppermute | solution.py:327
  30.8 0.1 multiply_convert_fusion.own_ref
  30.9 0.1 collective-permute-start.8
  31.0 0.5 %collective-permute-start.2 = (bf16[128,128]{1,0:T(8,128)(2,1)S(1)}, bf16[128,128]{1,0:T(8,128)(2,1)S(1)}, u32[]{:S(2)}, u32[]{:S(2)}) collective-permute-start(bf16[128,128]{1,0:T(8,128)(2,1)S(1)} %get-tuple-element.42), channel_id=1, source_target_pairs={{0,1},{1,0},{2,3},{3,2},{4,5},{5,4},{6,7},{7,6},{8,9},{9,8},{10,11... | collective-permute-start | bytes 98312 | tf_op jit(solution)/shard_map/ppermute | solution.py:426
  31.5 0.0 collective-permute-start.3
  31.5 1.0 %collective-permute-done.2.near_ref = bf16[128,128]{1,0:T(8,128)(2,1)S(1)} collective-permute-done((bf16[128,128]{1,0:T(8,128)(2,1)S(1)}, bf16[128,128]{1,0:T(8,128)(2,1)S(1)}, u32[]{:S(2)}, u32[]{:S(2)}) %collective-permute-start.2) | collective-permute-done | bytes 32800 | tf_op jit(solution)/shard_map/ppermute | solution.py:426
  32.5 3.2 %collective-permute-done.3.far_ref = bf16[128,128]{1,0:T(8,128)(2,1)S(1)} collective-permute-done((bf16[128,128]{1,0:T(8,128)(2,1)S(1)}, bf16[128,128]{1,0:T(8,128)(2,1)S(1)}, u32[]{:S(2)}, u32[]{:S(2)}) %collective-permute-start.3) | collective-permute-done | bytes 32800 | tf_op jit(solution)/shard_map/ppermute | solution.py:427
  35.7 2.4 %shard_map.96 = (bf16[64,384]{1,0:T(8,128)(2,1)}, bf16[64,384]{1,0:T(8,128)(2,1)}) custom-call(bf16[128,128]{1,0:T(8,128)(2,1)S(1)} %collective-permute-done.2.near_ref, bf16[128,128]{1,0:T(8,128)(2,1)S(1)} %collective-permute-done.3.far_ref, bf16[3,128,128]{2,1,0:T(8,128)(2,1)S(1)} %get-tuple-element.44.state_ref, ...), custom_call_target="tpu_custom_call" | custom-call | flops 509607936 | bytes 2654208 | tf_op jit(solution)/shard_map/pallas_call | solution.py:442
  38.1 0.8 %shard_map.98 = (f32[64,1728]{1,0:T(8,128)}, f32[64,1728]{1,0:T(8,128)}) custom-call(bf16[64,1728]{1,0:T(8,128)(2,1)S(1)} %multiply_convert_fusion.own_ref), custom_call_target="tpu_custom_call" | custom-call | tf_op jit(solution)/shard_map/pallas_call | solution.py:341
  38.9 0.0 collective-permute-done.8.other_ref
  38.9 0.8 %shard_map.99 = (f32[64,1728]{1,0:T(8,128)}, f32[64,1728]{1,0:T(8,128)}) custom-call(bf16[64,1728]{1,0:T(8,128)(2,1)S(1)} %collective-permute-done.8.other_ref, f32[64,1728]{1,0:T(8,128)} %get-tuple-element.50.first_in, f32[64,1728]{1,0:T(8,128)} %get-tuple-element.51.second_in), custom_call_target="tpu_custom_call", output_to_operand_aliasing={{0}: (1, {}), {1}: (2, {})} | custom-call | tf_op jit(solution)/shard_map/pallas_call | solution.py:342
  (1 shorter events, 0.0 us)
Async XLA Ops:
  1.8 3.3 %collective-permute-start = (bf16[128,128]{1,0:T(8,128)(2,1)S(1)}, bf16[128,128]{1,0:T(8,128)(2,1)S(1)}, u32[]{:S(2)}, u32[]{:S(2)}) collective-permute-start(bf16[128,128]{1,0:T(8,128)(2,1)S(1)} %get-tuple-element.30), channel_id=1, source_target_pairs={{0,1},{1,0},{2,3},{3,2},{4,5},{5,4},{6,7},{7,6},{8,9},{9,8},{10,11... | collective-permute-start | bytes 98312 | tf_op jit(solution)/shard_map/ppermute | solution.py:387
  1.9 4.4 %collective-permute-start.1 = (bf16[128,128]{1,0:T(8,128)(2,1)S(1)}, bf16[128,128]{1,0:T(8,128)(2,1)S(1)}, u32[]{:S(2)}, u32[]{:S(2)}) collective-permute-start(bf16[128,128]{1,0:T(8,128)(2,1)S(1)} %get-tuple-element.31), channel_id=1, source_target_pairs={{0,16},{1,2},{2,1},{3,4},{4,3},{5,6},{6,5},{7,8},{8,7},{9,10},{10,... | collective-permute-start | bytes 98312 | tf_op jit(solution)/shard_map/ppermute | solution.py:386
  7.5 1.6 %collective-permute-start.4 = (bf16[64,1728]{1,0:T(8,128)(2,1)S(1)}, bf16[64,1728]{1,0:T(8,128)(2,1)S(1)}, u32[]{:S(2)}, u32[]{:S(2)}) collective-permute-start(bf16[64,1728]{1,0:T(8,128)(2,1)S(1)} %get-tuple-element.49), channel_id=1, source_target_pairs={{0,1},{1,0},{2,3},{3,2},{4,5},{5,4},{6,7},{7,6},{8,9},{9,8},{10,11... | collective-permute-start | bytes 663560 | tf_op jit(solution)/shard_map/ppermute | solution.py:320
  9.1 6.1 %collective-permute-start.5 = (bf16[64,1728]{1,0:T(8,128)(2,1)S(1)}, bf16[64,1728]{1,0:T(8,128)(2,1)S(1)}, u32[]{:S(2)}, u32[]{:S(2)}) collective-permute-start(bf16[64,1728]{1,0:T(8,128)(2,1)S(1)} %add_convert_fusion.2), channel_id=1, source_target_pairs={{0,2},{1,9},{2,0},{3,11},{4,6},{5,13},{6,4},{7,15},{8,10},{9,1},{1... | collective-permute-start | bytes 663560 | tf_op jit(solution)/shard_map/ppermute | solution.py:327
  15.3 6.1 %collective-permute-start.6 = (bf16[64,1728]{1,0:T(8,128)(2,1)S(1)}, bf16[64,1728]{1,0:T(8,128)(2,1)S(1)}, u32[]{:S(2)}, u32[]{:S(2)}) collective-permute-start(bf16[64,1728]{1,0:T(8,128)(2,1)S(1)} %add_convert_fusion.1), channel_id=1, source_target_pairs={{0,4},{1,3},{2,6},{3,1},{4,0},{5,7},{6,2},{7,5},{8,12},{9,11},{10,... | collective-permute-start | bytes 663560 | tf_op jit(solution)/shard_map/ppermute | solution.py:327
  21.4 9.4 %collective-permute-start.7 = (bf16[64,1728]{1,0:T(8,128)(2,1)S(1)}, bf16[64,1728]{1,0:T(8,128)(2,1)S(1)}, u32[]{:S(2)}, u32[]{:S(2)}) collective-permute-start(bf16[64,1728]{1,0:T(8,128)(2,1)S(1)} %add_convert_fusion), channel_id=1, source_target_pairs={{0,8},{1,5},{2,10},{3,7},{4,12},{5,1},{6,14},{7,3},{8,0},{9,13},{1... | collective-permute-start | bytes 663560 | tf_op jit(solution)/shard_map/ppermute | solution.py:327
  30.9 8.0 %collective-permute-start.8 = (bf16[64,1728]{1,0:T(8,128)(2,1)S(1)}, bf16[64,1728]{1,0:T(8,128)(2,1)S(1)}, u32[]{:S(2)}, u32[]{:S(2)}) collective-permute-start(bf16[64,1728]{1,0:T(8,128)(2,1)S(1)} %multiply_convert_fusion.own_ref), channel_id=1, source_target_pairs={{0,1},{1,0},{2,3},{3,2},{4,5},{5,4},{6,7},{7,6},{8,9},{9,8},{10,11... | collective-permute-start | bytes 663560 | tf_op jit(solution)/shard_map/ppermute | solution.py:330
  31.0 1.5 %collective-permute-start.2 = (bf16[128,128]{1,0:T(8,128)(2,1)S(1)}, bf16[128,128]{1,0:T(8,128)(2,1)S(1)}, u32[]{:S(2)}, u32[]{:S(2)}) collective-permute-start(bf16[128,128]{1,0:T(8,128)(2,1)S(1)} %get-tuple-element.42), channel_id=1, source_target_pairs={{0,1},{1,0},{2,3},{3,2},{4,5},{5,4},{6,7},{7,6},{8,9},{9,8},{10,11... | collective-permute-start | bytes 98312 | tf_op jit(solution)/shard_map/ppermute | solution.py:426
  31.5 4.2 %collective-permute-start.3 = (bf16[128,128]{1,0:T(8,128)(2,1)S(1)}, bf16[128,128]{1,0:T(8,128)(2,1)S(1)}, u32[]{:S(2)}, u32[]{:S(2)}) collective-permute-start(bf16[128,128]{1,0:T(8,128)(2,1)S(1)} %get-tuple-element.43), channel_id=1, source_target_pairs={{0,16},{1,2},{2,1},{3,4},{4,3},{5,6},{6,5},{7,8},{8,7},{9,10},{10,... | collective-permute-start | bytes 98312 | tf_op jit(solution)/shard_map/ppermute | solution.py:427

commit v8 on v7

--- a/solution.py
+++ b/solution.py
@@ -163,6 +163,19 @@
     d_hidden_ref[...] = jnp.dot(turned_ref[...], gs_ref[...], preferred_element_type=F32)
 
 
+def packed_rows(offsets, width):
+    return offsets * width * width // BLOCK
+
+
+def pack(out_ref, pair, pieces):
+    width = pieces[0].shape[0]
+    if len(pieces) == 1:
+        pieces = [pieces[0][: width // 2], pieces[0][width // 2 :]]
+    joined = jnp.concatenate(pieces, axis=1)
+    row = pair * width
+    out_ref[row : row + joined.shape[0]] = joined.astype(out_ref.dtype)
+
+
 def first_terms(state_ref, xs_ref, out_ref):
     blocks = state_ref.shape[0]
     width = state_ref.shape[1] // 2
@@ -171,7 +184,14 @@
     for low in range(0, depth, 8 * width):
         high = min(depth, low + 8 * width)
         terms = lax.dot_general(d_pre, xs_ref[low:high], NT, preferred_element_type=F32)
-        out_ref[:, low:high] = terms.astype(out_ref.dtype)
+        for at in range(low, high, 2 * width):
+            end = min(high, at + 2 * width)
+            pair = terms[:, at - low : end - low]
+            if end - at == BLOCK:
+                row = at // BLOCK * width
+                out_ref[row : row + width] = pair.astype(out_ref.dtype)
+            else:
+                pack(out_ref, at // BLOCK, [pair])
 
 
 def second_terms(state_ref, gs_ref, out_ref):
@@ -186,8 +206,7 @@
             pieces = [
                 terms[i - low : i - low + width] for i in range(at, min(high, at + 2 * width), width)
             ]
-            joined = pieces[0] if len(pieces) == 1 else jnp.concatenate(pieces, axis=1)
-            out_ref[:, at : at + joined.shape[1]] = joined.astype(out_ref.dtype)
+            pack(out_ref, at // BLOCK, pieces)
 
 
 def rim_kernel(
@@ -260,18 +279,21 @@
 
 
 def put(source_ref, for_odd, for_even, staging_ref, sems):
+    width, depth = staging_ref.shape
+    for pair in range(depth // BLOCK):
+        block = source_ref[pair * width : (pair + 1) * width]
+        staging_ref[:, pair * BLOCK : (pair + 1) * BLOCK] = block.astype(F32)
+    if depth % BLOCK:
+        low, half = depth - width, width // 2
+        block = source_ref[depth // BLOCK * width :].astype(F32)
+        staging_ref[:half, low:] = block[:, :width]
+        staging_ref[half:, low:] = block[:, width:]
     odd = is_odd()
     for chosen, target in ((odd, for_odd), (jnp.logical_not(odd), for_even)):
 
         @pl.when(chosen)
         def _():
-            copies = []
-            chunks = zip(in_chunks(source_ref), in_chunks(staging_ref), in_chunks(target))
-            for i, (source, staging, place) in enumerate(chunks):
-                staging[...] = source[...].astype(F32)
-                copies.append(pltpu.make_async_copy(staging, place, sems.at[i]))
-                copies[-1].start()
-            for copy in copies:
+            for copy in fetch((staging_ref,), (target,), sems):
                 copy.wait()
 
 
@@ -314,7 +336,7 @@
     return near, far
 
 
-def total_over_tiles(keep, send, scale):
+def total_over_tiles(keep, send, scale, shape):
     count = lax.axis_size("tile")
     cores = [(i, i ^ 1) for i in range(count)]
     received = lax.ppermute(send, "tile", cores)
@@ -328,8 +350,8 @@
         total = sent.astype(F32) + received.astype(F32)
     total = (total * scale).astype(BF16)
     other = lax.ppermute(total, "tile", cores)
-    result = jax.ShapeDtypeStruct(total.shape, F32)
-    staging = [pltpu.VMEM(total.shape, F32), pltpu.SemaphoreType.DMA((4,))]
+    result = jax.ShapeDtypeStruct(shape, F32)
+    staging = [pltpu.VMEM(shape, F32), pltpu.SemaphoreType.DMA((1,))]
     put_own = pl.pallas_call(
         put_own_kernel,
         out_shape=(result, result),
@@ -368,7 +390,7 @@
     sums = shape((width, rows), F32)
     gathered = shape((offsets * width, rows), BF16)
     weight = shape((width, offsets * width), BF16)
-    terms = shape((width, offsets * width), F32)
+    packed = (packed_rows(offsets, width), BLOCK)
     state_shape = shape((blocks, 2 * width, BLOCK), BF16)
     table = pltpu.VMEM((blocks + 2, 2 * width, BLOCK), BF16)
 
@@ -403,7 +425,7 @@
     xs, gs, pre, d_hidden, turned = own_phase(rule, x, g, w1, w2)
     state, near, far, send, xs, gs = pl.pallas_call(
         rim_kernel,
-        out_shape=(state_shape, rim, rim, weight, gathered, gathered),
+        out_shape=(state_shape, rim, rim, shape(packed, BF16), gathered, gathered),
         in_specs=[VMEM] * 10,
         out_specs=(VMEM,) * 6,
         scratch_shapes=[
@@ -416,7 +438,7 @@
     )(lists, near, far, pre, d_hidden, rule, w1, turned, xs, gs)
     keep_terms = pl.pallas_call(
         keep_kernel,
-        out_shape=terms,
+        out_shape=shape(packed, F32),
         in_specs=[VMEM] * 3,
         out_specs=VMEM,
         compiler_params=MEDIUM,
@@ -442,7 +464,7 @@
     out_features, d_features = second_phase(near, far, state, rule, x, g, w1, w2)
 
     scale = 1.0 / math.sqrt(rows * count)
-    grad_first, grad_second = total_over_tiles(keep, send, scale)
+    grad_first, grad_second = total_over_tiles(keep, send, scale, weight.shape)
     return out_features, d_features, grad_first, grad_second
 
 

time: 39.9 us -> 39.7 us (level)
  waiting for transfers between devices: 26.3 us -> 25.9 us
where the time goes in v8:
time: 39.7 us; the launch traced here: 39.5 us
  waiting for transfers between devices  25.9 us (65%)
  Pallas kernels  8.93 us (22%)
  starting transfers between devices  3.7 us (9%)
  between operations  0.72 us (2%)
    ppermute x3, waiting for transfers between devices, total_over_tiles(): received = lax.ppermute(sent, 'tile', pairs)  19.7 us
    ppermute x2, waiting for transfers between devices, body(): far = lax.ppermute(far, axes, far_pairs)  4.35 us
    pallas_call x1, Pallas kernels, body(): second_phase(near, far, state, rule, x, g, w1, w2)  2.37 us
    pallas_call x1, Pallas kernels, body(): xs, gs, pre, d_hidden, turned = own_phase(rule, x, g, w1, w2)  1.74 us
    ppermute x3, starting transfers between devices, total_over_tiles(): received = lax.ppermute(sent, 'tile', pairs)  1.5 us
    ppermute x2, starting transfers between devices, body(): far = lax.ppermute(far, axes, far_pairs)  1.48 us
    pallas_call x1, Pallas kernels, body(): pl.pallas_call(rim_kernel, out_shape=(state_shape, rim, rim, shape(packed...  1.28 us
    pallas_call x1, Pallas kernels, body(): pl.pallas_call(load_kernel, out_shape=(rim, rim, shape((2, 8, BLOCK), jnp...  1.2 us
  transfers between devices with their start and end apart: 9, of which 7 were waited for; matrix products, arithmetic and copies ran while one was open for 0% of the time, Pallas kernels for 14%

profile of v8, /device:TPU:28, one launch (start us, length us, event | category | flops | bytes accessed | tf_op | source)
XLA Modules:
  0.0 39.5 jit_solution(17413149015767321477)
XLA Ops:
  0.6 1.2 %shard_map.93 = (bf16[128,128]{1,0:T(8,128)(2,1)S(1)}, bf16[128,128]{1,0:T(8,128)(2,1)S(1)}, s32[2,8,128]{2,1,0:T(8,128)S(1)}, bf16[64,384]{1,0:T(8,128)(2,1)S(1...) custom-call(s32[2]{0:T(128)} %bitcast.1, ...), custom_call_target="tpu_custom_call" | custom-call | tf_op jit(solution)/shard_map/pallas_call | solution.py:397
  1.8 0.1 collective-permute-start
  1.9 1.5 %collective-permute-start.1 = (bf16[128,128]{1,0:T(8,128)(2,1)S(1)}, bf16[128,128]{1,0:T(8,128)(2,1)S(1)}, u32[]{:S(2)}, u32[]{:S(2)}) collective-permute-start(bf16[128,128]{1,0:T(8,128)(2,1)S(1)} %get-tuple-element.31), channel_id=1, source_target_pairs={{0,16},{1,2},{2,1},{3,4},{4,3},{5,6},{6,5},{7,8},{8,7},{9,10},{10,... | collective-permute-start | bytes 98312 | tf_op jit(solution)/shard_map/ppermute | solution.py:408
  3.4 1.7 %shard_map.94 = (bf16[1728,384]{1,0:T(8,128)(2,1)S(1)}, bf16[1728,384]{1,0:T(8,128)(2,1)S(1)}, f32[64,384]{1,0:T(8,128)S(1)}, f32[64,384]{1,0:T(8,128)S(1)}, bf16[64,1728]{1,0:T(8,128)(2,1)S(1)}) custom-call(s32[27,384]{1,0:T(8,128)S(1)} %get-tuple-element.32.rule_ref, bf16[64,384]{1,0:T(8,128)(2,1)S(1)} %get-tuple-element.33.x_ref, ...), custom_call_target="tpu_custom_call" | custom-call | flops 509607936 | bytes 2654208 | tf_op jit(solution)/shard_map/pallas_call | solution.py:425
  5.1 0.0 collective-permute-done.near_ref
  5.2 1.1 %collective-permute-done.1.far_ref = bf16[128,128]{1,0:T(8,128)(2,1)S(1)} collective-permute-done((bf16[128,128]{1,0:T(8,128)(2,1)S(1)}, bf16[128,128]{1,0:T(8,128)(2,1)S(1)}, u32[]{:S(2)}, u32[]{:S(2)}) %collective-permute-start.1) | collective-permute-done | bytes 32800 | tf_op jit(solution)/shard_map/ppermute | solution.py:408
  6.3 1.3 %shard_map.95 = (bf16[3,128,128]{2,1,0:T(8,128)(2,1)S(1)}, bf16[128,128]{1,0:T(8,128)(2,1)S(1)}, bf16[128,128]{1,0:T(8,128)(2,1)S(1)}, bf16[864,128]{1,0:T(8,128...) custom-call(s32[2,8,128]{2,1,0:T(8,128)S(1)} %get-tuple-element.29.l, ...), custom_call_target="tpu_custom_call", output_to_operand_aliasing={{4}: (8, {}), {5}: (9, {})} | custom-call | tf_op jit(solution)/shard_map/pallas_call | solution.py:426
  7.6 0.1 collective-permute-start.4
  7.6 0.6 %shard_map.97 = f32[864,128]{1,0:T(8,128)S(1)} custom-call(bf16[3,128,128]{2,1,0:T(8,128)(2,1)S(1)} %get-tuple-element.44.state_ref, bf16[1728,384]{1,0:T(8,128)(2,1)S(1)} %get-tuple-element.47.xs_ref, bf16[1728,384]{1,0:T(8,128)(2,1)S(1)} %get-tuple-element.48.gs_ref), custom_call_target="tpu_custom_call" | custom-call | tf_op jit(solution)/shard_map/pallas_call | solution.py:446
  8.3 0.8 %collective-permute-done.4 = bf16[864,128]{1,0:T(8,128)(2,1)S(1)} collective-permute-done((bf16[864,128]{1,0:T(8,128)(2,1)S(1)}, bf16[864,128]{1,0:T(8,128)(2,1)S(1)}, u32[]{:S(2)}, u32[]{:S(2)}) %collective-permute-start.4) | collective-permute-done | bytes 221216 | tf_op jit(solution)/shard_map/ppermute | solution.py:342
  9.2 0.6 %collective-permute-start.5 = (bf16[864,128]{1,0:T(8,128)(2,1)S(1)}, bf16[864,128]{1,0:T(8,128)(2,1)S(1)}, u32[]{:S(2)}, u32[]{:S(2)}) collective-permute-start(bf16[864,128]{1,0:T(8,128)(2,1)S(1)} %add_convert_fusion.2), channel_id=1, source_target_pairs={{0,2},{1,9},{2,0},{3,11},{4,6},{5,13},{6,4},{7,15},{8,10},{9,1},{1... | collective-permute-start | bytes 663560 | tf_op jit(solution)/shard_map/ppermute | solution.py:349
  9.8 5.4 %collective-permute-done.5 = bf16[864,128]{1,0:T(8,128)(2,1)S(1)} collective-permute-done((bf16[864,128]{1,0:T(8,128)(2,1)S(1)}, bf16[864,128]{1,0:T(8,128)(2,1)S(1)}, u32[]{:S(2)}, u32[]{:S(2)}) %collective-permute-start.5) | collective-permute-done | bytes 221216 | tf_op jit(solution)/shard_map/ppermute | solution.py:349
  15.2 0.1 add_convert_fusion.1
  15.2 0.5 %collective-permute-start.6 = (bf16[864,128]{1,0:T(8,128)(2,1)S(1)}, bf16[864,128]{1,0:T(8,128)(2,1)S(1)}, u32[]{:S(2)}, u32[]{:S(2)}) collective-permute-start(bf16[864,128]{1,0:T(8,128)(2,1)S(1)} %add_convert_fusion.1), channel_id=1, source_target_pairs={{0,4},{1,3},{2,6},{3,1},{4,0},{5,7},{6,2},{7,5},{8,12},{9,11},{10,... | collective-permute-start | bytes 663560 | tf_op jit(solution)/shard_map/ppermute | solution.py:349
  15.7 5.5 %collective-permute-done.6 = bf16[864,128]{1,0:T(8,128)(2,1)S(1)} collective-permute-done((bf16[864,128]{1,0:T(8,128)(2,1)S(1)}, bf16[864,128]{1,0:T(8,128)(2,1)S(1)}, u32[]{:S(2)}, u32[]{:S(2)}) %collective-permute-start.6) | collective-permute-done | bytes 221216 | tf_op jit(solution)/shard_map/ppermute | solution.py:349
  21.2 0.1 add_convert_fusion
  21.3 0.4 collective-permute-start.7
  21.7 8.8 %collective-permute-done.7 = bf16[864,128]{1,0:T(8,128)(2,1)S(1)} collective-permute-done((bf16[864,128]{1,0:T(8,128)(2,1)S(1)}, bf16[864,128]{1,0:T(8,128)(2,1)S(1)}, u32[]{:S(2)}, u32[]{:S(2)}) %collective-permute-start.7) | collective-permute-done | bytes 221216 | tf_op jit(solution)/shard_map/ppermute | solution.py:349
  30.5 0.1 multiply_convert_fusion.own_ref
  30.6 0.1 collective-permute-start.8
  30.7 0.5 %collective-permute-start.2 = (bf16[128,128]{1,0:T(8,128)(2,1)S(1)}, bf16[128,128]{1,0:T(8,128)(2,1)S(1)}, u32[]{:S(2)}, u32[]{:S(2)}) collective-permute-start(bf16[128,128]{1,0:T(8,128)(2,1)S(1)} %get-tuple-element.42), channel_id=1, source_target_pairs={{0,1},{1,0},{2,3},{3,2},{4,5},{5,4},{6,7},{7,6},{8,9},{9,8},{10,11... | collective-permute-start | bytes 98312 | tf_op jit(solution)/shard_map/ppermute | solution.py:448
  31.2 0.0 collective-permute-start.3
  31.2 1.0 %collective-permute-done.2.near_ref = bf16[128,128]{1,0:T(8,128)(2,1)S(1)} collective-permute-done((bf16[128,128]{1,0:T(8,128)(2,1)S(1)}, bf16[128,128]{1,0:T(8,128)(2,1)S(1)}, u32[]{:S(2)}, u32[]{:S(2)}) %collective-permute-start.2) | collective-permute-done | bytes 32800 | tf_op jit(solution)/shard_map/ppermute | solution.py:448
  32.2 3.2 %collective-permute-done.3.far_ref = bf16[128,128]{1,0:T(8,128)(2,1)S(1)} collective-permute-done((bf16[128,128]{1,0:T(8,128)(2,1)S(1)}, bf16[128,128]{1,0:T(8,128)(2,1)S(1)}, u32[]{:S(2)}, u32[]{:S(2)}) %collective-permute-start.3) | collective-permute-done | bytes 32800 | tf_op jit(solution)/shard_map/ppermute | solution.py:449
  35.4 2.4 %shard_map.96 = (bf16[64,384]{1,0:T(8,128)(2,1)}, bf16[64,384]{1,0:T(8,128)(2,1)}) custom-call(bf16[128,128]{1,0:T(8,128)(2,1)S(1)} %collective-permute-done.2.near_ref, bf16[128,128]{1,0:T(8,128)(2,1)S(1)} %collective-permute-done.3.far_ref, bf16[3,128,128]{2,1,0:T(8,128)(2,1)S(1)} %get-tuple-element.44.state_ref, ...), custom_call_target="tpu_custom_call" | custom-call | flops 509607936 | bytes 2654208 | tf_op jit(solution)/shard_map/pallas_call | solution.py:464
  37.8 0.8 %shard_map.98 = (f32[64,1728]{1,0:T(8,128)}, f32[64,1728]{1,0:T(8,128)}) custom-call(bf16[864,128]{1,0:T(8,128)(2,1)S(1)} %multiply_convert_fusion.own_ref), custom_call_target="tpu_custom_call" | custom-call | tf_op jit(solution)/shard_map/pallas_call | solution.py:363
  38.6 0.0 collective-permute-done.8.other_ref
  38.6 0.9 %shard_map.99 = (f32[64,1728]{1,0:T(8,128)}, f32[64,1728]{1,0:T(8,128)}) custom-call(bf16[864,128]{1,0:T(8,128)(2,1)S(1)} %collective-permute-done.8.other_ref, f32[64,1728]{1,0:T(8,128)} %get-tuple-element.50.first_in, f32[64,1728]{1,0:T(8,128)} %get-tuple-element.51.second_in), custom_call_target="tpu_custom_call", output_to_operand_aliasing={{0}: (1, {}), {1}: (2, {})} | custom-call | tf_op jit(solution)/shard_map/pallas_call | solution.py:364
  (1 shorter events, 0.0 us)
Async XLA Ops:
  1.8 3.3 %collective-permute-start = (bf16[128,128]{1,0:T(8,128)(2,1)S(1)}, bf16[128,128]{1,0:T(8,128)(2,1)S(1)}, u32[]{:S(2)}, u32[]{:S(2)}) collective-permute-start(bf16[128,128]{1,0:T(8,128)(2,1)S(1)} %get-tuple-element.30), channel_id=1, source_target_pairs={{0,1},{1,0},{2,3},{3,2},{4,5},{5,4},{6,7},{7,6},{8,9},{9,8},{10,11... | collective-permute-start | bytes 98312 | tf_op jit(solution)/shard_map/ppermute | solution.py:409
  1.9 4.4 %collective-permute-start.1 = (bf16[128,128]{1,0:T(8,128)(2,1)S(1)}, bf16[128,128]{1,0:T(8,128)(2,1)S(1)}, u32[]{:S(2)}, u32[]{:S(2)}) collective-permute-start(bf16[128,128]{1,0:T(8,128)(2,1)S(1)} %get-tuple-element.31), channel_id=1, source_target_pairs={{0,16},{1,2},{2,1},{3,4},{4,3},{5,6},{6,5},{7,8},{8,7},{9,10},{10,... | collective-permute-start | bytes 98312 | tf_op jit(solution)/shard_map/ppermute | solution.py:408
  7.6 1.5 %collective-permute-start.4 = (bf16[864,128]{1,0:T(8,128)(2,1)S(1)}, bf16[864,128]{1,0:T(8,128)(2,1)S(1)}, u32[]{:S(2)}, u32[]{:S(2)}) collective-permute-start(bf16[864,128]{1,0:T(8,128)(2,1)S(1)} %get-tuple-element.49), channel_id=1, source_target_pairs={{0,1},{1,0},{2,3},{3,2},{4,5},{5,4},{6,7},{7,6},{8,9},{9,8},{10,11... | collective-permute-start | bytes 663560 | tf_op jit(solution)/shard_map/ppermute | solution.py:342
  9.2 6.0 %collective-permute-start.5 = (bf16[864,128]{1,0:T(8,128)(2,1)S(1)}, bf16[864,128]{1,0:T(8,128)(2,1)S(1)}, u32[]{:S(2)}, u32[]{:S(2)}) collective-permute-start(bf16[864,128]{1,0:T(8,128)(2,1)S(1)} %add_convert_fusion.2), channel_id=1, source_target_pairs={{0,2},{1,9},{2,0},{3,11},{4,6},{5,13},{6,4},{7,15},{8,10},{9,1},{1... | collective-permute-start | bytes 663560 | tf_op jit(solution)/shard_map/ppermute | solution.py:349
  15.2 6.0 %collective-permute-start.6 = (bf16[864,128]{1,0:T(8,128)(2,1)S(1)}, bf16[864,128]{1,0:T(8,128)(2,1)S(1)}, u32[]{:S(2)}, u32[]{:S(2)}) collective-permute-start(bf16[864,128]{1,0:T(8,128)(2,1)S(1)} %add_convert_fusion.1), channel_id=1, source_target_pairs={{0,4},{1,3},{2,6},{3,1},{4,0},{5,7},{6,2},{7,5},{8,12},{9,11},{10,... | collective-permute-start | bytes 663560 | tf_op jit(solution)/shard_map/ppermute | solution.py:349
  21.3 9.2 %collective-permute-start.7 = (bf16[864,128]{1,0:T(8,128)(2,1)S(1)}, bf16[864,128]{1,0:T(8,128)(2,1)S(1)}, u32[]{:S(2)}, u32[]{:S(2)}) collective-permute-start(bf16[864,128]{1,0:T(8,128)(2,1)S(1)} %add_convert_fusion), channel_id=1, source_target_pairs={{0,8},{1,5},{2,10},{3,7},{4,12},{5,1},{6,14},{7,3},{8,0},{9,13},{1... | collective-permute-start | bytes 663560 | tf_op jit(solution)/shard_map/ppermute | solution.py:349
  30.6 8.0 %collective-permute-start.8 = (bf16[864,128]{1,0:T(8,128)(2,1)S(1)}, bf16[864,128]{1,0:T(8,128)(2,1)S(1)}, u32[]{:S(2)}, u32[]{:S(2)}) collective-permute-start(bf16[864,128]{1,0:T(8,128)(2,1)S(1)} %multiply_convert_fusion.own_ref), channel_id=1, source_target_pairs={{0,1},{1,0},{2,3},{3,2},{4,5},{5,4},{6,7},{7,6},{8,9},{9,8},{10,11... | collective-permute-start | bytes 663560 | tf_op jit(solution)/shard_map/ppermute | solution.py:352
  30.7 1.5 %collective-permute-start.2 = (bf16[128,128]{1,0:T(8,128)(2,1)S(1)}, bf16[128,128]{1,0:T(8,128)(2,1)S(1)}, u32[]{:S(2)}, u32[]{:S(2)}) collective-permute-start(bf16[128,128]{1,0:T(8,128)(2,1)S(1)} %get-tuple-element.42), channel_id=1, source_target_pairs={{0,1},{1,0},{2,3},{3,2},{4,5},{5,4},{6,7},{7,6},{8,9},{9,8},{10,11... | collective-permute-start | bytes 98312 | tf_op jit(solution)/shard_map/ppermute | solution.py:448
  31.2 4.2 %collective-permute-start.3 = (bf16[128,128]{1,0:T(8,128)(2,1)S(1)}, bf16[128,128]{1,0:T(8,128)(2,1)S(1)}, u32[]{:S(2)}, u32[]{:S(2)}) collective-permute-start(bf16[128,128]{1,0:T(8,128)(2,1)S(1)} %get-tuple-element.43), channel_id=1, source_target_pairs={{0,16},{1,2},{2,1},{3,4},{4,3},{5,6},{6,5},{7,8},{8,7},{9,10},{10,... | collective-permute-start | bytes 98312 | tf_op jit(solution)/shard_map/ppermute | solution.py:449

commit v9 on v8

--- a/solution.py
+++ b/solution.py
@@ -14,11 +14,6 @@
 MEDIUM = pltpu.CompilerParams(vmem_limit_bytes=20 << 20)
 VMEM = pl.BlockSpec(memory_space=pltpu.VMEM)
 NT = (((1,), (1,)), ((), ()))
-
-
-def in_chunks(ref, count=4):
-    rows = ref.shape[0] // count
-    return [ref.at[i * rows : (i + 1) * rows] for i in range(count)]
 
 
 def is_odd():
@@ -41,14 +36,14 @@
 
 
 def load_kernel(
-    lists_hbm, x_hbm, g_hbm, rule_hbm, w2_hbm, w1_hbm,
-    near_ref, far_ref, lists_out, x_ref, g_ref, rule_ref, w2_ref, w1_ref,
+    lists_hbm, x_hbm, g_hbm, rule_hbm, w2_hbm,
+    near_ref, far_ref, lists_out, x_ref, g_ref, rule_ref, w2_ref,
     lists_ref, sems,
 ):
     width, rows = x_ref.shape
     copies = fetch(
-        (lists_hbm, x_hbm, g_hbm, rule_hbm, *in_chunks(w2_hbm), *in_chunks(w1_hbm)),
-        (lists_ref, x_ref, g_ref, rule_ref, *in_chunks(w2_ref), *in_chunks(w1_ref)),
+        (lists_hbm, x_hbm, g_hbm, rule_hbm, w2_hbm),
+        (lists_ref, x_ref, g_ref, rule_ref, w2_ref),
         sems,
     )
     for copy in copies[:3]:
@@ -146,10 +141,11 @@
 
 
 def own_kernel(
-    rule_ref, x_ref, g_ref, w1_ref, w2_ref,
-    xs_ref, gs_ref, pre_ref, d_hidden_ref, turned_ref,
-    table_ref,
+    rule_ref, x_ref, g_ref, w2_ref, w1_hbm,
+    xs_ref, gs_ref, pre_ref, d_hidden_ref, turned_ref, w1_ref,
+    table_ref, sems,
 ):
+    copies = fetch((w1_hbm,), (w1_ref,), sems)
     width, rows = x_ref.shape
     blocks = rows // BLOCK
     for block in range(blocks):
@@ -159,8 +155,10 @@
     table_ref[blocks:] = jnp.zeros_like(table_ref[blocks:])
     gather(table_ref, rule_ref, xs_ref, gs_ref, blocks)
     turn(w2_ref, turned_ref)
+    d_hidden_ref[...] = jnp.dot(turned_ref[...], gs_ref[...], preferred_element_type=F32)
+    for copy in copies:
+        copy.wait()
     pre_ref[...] = jnp.dot(w1_ref[...], xs_ref[...], preferred_element_type=F32)
-    d_hidden_ref[...] = jnp.dot(turned_ref[...], gs_ref[...], preferred_element_type=F32)
 
 
 def packed_rows(offsets, width):
@@ -280,20 +278,34 @@
 
 def put(source_ref, for_odd, for_even, staging_ref, sems):
     width, depth = staging_ref.shape
-    for pair in range(depth // BLOCK):
-        block = source_ref[pair * width : (pair + 1) * width]
-        staging_ref[:, pair * BLOCK : (pair + 1) * BLOCK] = block.astype(F32)
-    if depth % BLOCK:
-        low, half = depth - width, width // 2
-        block = source_ref[depth // BLOCK * width :].astype(F32)
-        staging_ref[:half, low:] = block[:, :width]
-        staging_ref[half:, low:] = block[:, width:]
+    pairs = depth // BLOCK
+    cuts = [0, pairs // 3 * BLOCK, 2 * pairs // 3 * BLOCK, depth]
+
+    def unpack(low, high):
+        for at in range(low, high, BLOCK):
+            row = at // BLOCK * width
+            if at + BLOCK <= high:
+                staging_ref[:, at : at + BLOCK] = source_ref[row : row + width].astype(F32)
+            else:
+                half = width // 2
+                block = source_ref[row : row + half].astype(F32)
+                staging_ref[:half, at:high] = block[:, :width]
+                staging_ref[half:, at:high] = block[:, width:]
+
     odd = is_odd()
     for chosen, target in ((odd, for_odd), (jnp.logical_not(odd), for_even)):
 
         @pl.when(chosen)
         def _():
-            for copy in fetch((staging_ref,), (target,), sems):
+            copies = []
+            for i, (low, high) in enumerate(zip(cuts, cuts[1:])):
+                unpack(low, high)
+                place = pl.ds(low, high - low)
+                copies.append(
+                    pltpu.make_async_copy(staging_ref.at[:, place], target.at[:, place], sems.at[i])
+                )
+                copies[-1].start()
+            for copy in copies:
                 copy.wait()
 
 
@@ -351,7 +363,7 @@
     total = (total * scale).astype(BF16)
     other = lax.ppermute(total, "tile", cores)
     result = jax.ShapeDtypeStruct(shape, F32)
-    staging = [pltpu.VMEM(shape, F32), pltpu.SemaphoreType.DMA((1,))]
+    staging = [pltpu.VMEM(shape, F32), pltpu.SemaphoreType.DMA((3,))]
     put_own = pl.pallas_call(
         put_own_kernel,
         out_shape=(result, result),
@@ -394,17 +406,17 @@
     state_shape = shape((blocks, 2 * width, BLOCK), BF16)
     table = pltpu.VMEM((blocks + 2, 2 * width, BLOCK), BF16)
 
-    near, far, lists, x, g, rule, w2, w1 = pl.pallas_call(
+    near, far, lists, x, g, rule, w2 = pl.pallas_call(
         load_kernel,
         out_shape=(
             rim, rim, shape((2, 8, BLOCK), jnp.int32), values, values,
-            shape(rulebook.shape, jnp.int32), weight, weight,
+            shape(rulebook.shape, jnp.int32), weight,
         ),
-        in_specs=[HBM] * 6,
-        out_specs=(VMEM,) * 8,
-        scratch_shapes=[pltpu.SMEM((2,), jnp.int32), pltpu.SemaphoreType.DMA((12,))],
-        compiler_params=MEDIUM,
-    )(send_lists, features, cotangent, rulebook, weight_second, weight_first)
+        in_specs=[HBM] * 5,
+        out_specs=(VMEM,) * 7,
+        scratch_shapes=[pltpu.SMEM((2,), jnp.int32), pltpu.SemaphoreType.DMA((5,))],
+        compiler_params=MEDIUM,
+    )(send_lists, features, cotangent, rulebook, weight_second)
     far = lax.ppermute(far, axes, far_pairs)
     near = lax.ppermute(near, axes, near_pairs)
 
@@ -415,14 +427,14 @@
     )
     own_phase = pl.pallas_call(
         own_kernel,
-        out_shape=(gathered, gathered, sums, sums, weight),
-        in_specs=[VMEM] * 5,
-        out_specs=(VMEM,) * 5,
-        scratch_shapes=[table],
+        out_shape=(gathered, gathered, sums, sums, weight, weight),
+        in_specs=[VMEM] * 4 + [HBM],
+        out_specs=(VMEM,) * 6,
+        scratch_shapes=[table, pltpu.SemaphoreType.DMA((1,))],
         compiler_params=MEDIUM,
         cost_estimate=work,
     )
-    xs, gs, pre, d_hidden, turned = own_phase(rule, x, g, w1, w2)
+    xs, gs, pre, d_hidden, turned, w1 = own_phase(rule, x, g, w2, weight_first)
     state, near, far, send, xs, gs = pl.pallas_call(
         rim_kernel,
         out_shape=(state_shape, rim, rim, shape(packed, BF16), gathered, gathered),

time: 39.7 us -> 39.5 us (level)
  waiting for transfers between devices: 25.9 us -> 25.5 us
  transfers between devices with their start and end apart: 9 -> 9, of which waited for: 7 -> 7; matrix products, arithmetic and copies ran while one was open for 0% -> 0% of each run, Pallas kernels for 14% -> 15%
where the time goes in v9:
time: 39.5 us; the launch traced here: 39.3 us
  waiting for transfers between devices  25.5 us (65%)
  Pallas kernels  9.07 us (23%)
  starting transfers between devices  3.7 us (9%)
  between operations  0.72 us (2%)
    ppermute x3, waiting for transfers between devices, total_over_tiles(): received = lax.ppermute(sent, 'tile', pairs)  19.7 us
    ppermute x2, waiting for transfers between devices, body(): far = lax.ppermute(far, axes, far_pairs)  4 us
    pallas_call x1, Pallas kernels, body(): second_phase(near, far, state, rule, x, g, w1, w2)  2.37 us
    pallas_call x1, Pallas kernels, body(): xs, gs, pre, d_hidden, turned, w1 = own_phase(rule, x, g, w2, weight_first)  2.1 us
    ppermute x3, starting transfers between devices, total_over_tiles(): received = lax.ppermute(sent, 'tile', pairs)  1.51 us
    ppermute x2, starting transfers between devices, body(): far = lax.ppermute(far, axes, far_pairs)  1.48 us
    pallas_call x1, Pallas kernels, body(): pl.pallas_call(rim_kernel, out_shape=(state_shape, rim, rim, shape(packed...  1.27 us
    pallas_call x1, Pallas kernels, body(): pl.pallas_call(load_kernel, out_shape=(rim, rim, shape((2, 8, BLOCK), jnp...  1.07 us
  transfers between devices with their start and end apart: 9, of which 7 were waited for; matrix products, arithmetic and copies ran while one was open for 0% of the time, Pallas kernels for 15%

profile of v9, /device:TPU:28, one launch (start us, length us, event | category | flops | bytes accessed | tf_op | source)
XLA Modules:
  0.0 39.3 jit_solution(4682457550849896887)
XLA Ops:
  0.6 1.1 %shard_map.93 = (bf16[128,128]{1,0:T(8,128)(2,1)S(1)}, bf16[128,128]{1,0:T(8,128)(2,1)S(1)}, s32[2,8,128]{2,1,0:T(8,128)S(1)}, bf16[64,384]{1,0:T(8,128)(2,1)S(1...) custom-call(s32[2]{0:T(128)} %bitcast.1, bf16[64,384]{1,0:T(8,128)(2,1)} %x_hbm.1, ...), custom_call_target="tpu_custom_call" | custom-call | tf_op jit(solution)/shard_map/pallas_call | solution.py:409
  1.7 0.1 collective-permute-start
  1.8 1.5 %collective-permute-start.1 = (bf16[128,128]{1,0:T(8,128)(2,1)S(1)}, bf16[128,128]{1,0:T(8,128)(2,1)S(1)}, u32[]{:S(2)}, u32[]{:S(2)}) collective-permute-start(bf16[128,128]{1,0:T(8,128)(2,1)S(1)} %get-tuple-element.31), channel_id=1, source_target_pairs={{0,16},{1,2},{2,1},{3,4},{4,3},{5,6},{6,5},{7,8},{8,7},{9,10},{10,... | collective-permute-start | bytes 98312 | tf_op jit(solution)/shard_map/ppermute | solution.py:420
  3.3 2.1 %shard_map.94 = (bf16[1728,384]{1,0:T(8,128)(2,1)S(1)}, bf16[1728,384]{1,0:T(8,128)(2,1)S(1)}, f32[64,384]{1,0:T(8,128)S(1)}, f32[64,384]{1,0:T(8,128)S(1)}, bf1...) custom-call(s32[27,384]{1,0:T(8,128)S(1)} %get-tuple-element.32.rule_ref, ...), custom_call_target="tpu_custom_call" | custom-call | flops 509607936 | bytes 2654208 | tf_op jit(solution)/shard_map/pallas_call | solution.py:437
  5.4 0.0 collective-permute-done.near_ref
  5.4 0.8 %collective-permute-done.1.far_ref = bf16[128,128]{1,0:T(8,128)(2,1)S(1)} collective-permute-done((bf16[128,128]{1,0:T(8,128)(2,1)S(1)}, bf16[128,128]{1,0:T(8,128)(2,1)S(1)}, u32[]{:S(2)}, u32[]{:S(2)}) %collective-permute-start.1) | collective-permute-done | bytes 32800 | tf_op jit(solution)/shard_map/ppermute | solution.py:420
  6.2 1.3 %shard_map.95 = (bf16[3,128,128]{2,1,0:T(8,128)(2,1)S(1)}, bf16[128,128]{1,0:T(8,128)(2,1)S(1)}, bf16[128,128]{1,0:T(8,128)(2,1)S(1)}, bf16[864,128]{1,0:T(8,128...) custom-call(s32[2,8,128]{2,1,0:T(8,128)S(1)} %get-tuple-element.29.l, ...), custom_call_target="tpu_custom_call", output_to_operand_aliasing={{4}: (8, {}), {5}: (9, {})} | custom-call | tf_op jit(solution)/shard_map/pallas_call | solution.py:438
  7.4 0.1 collective-permute-start.4
  7.5 0.6 %shard_map.97 = f32[864,128]{1,0:T(8,128)S(1)} custom-call(bf16[3,128,128]{2,1,0:T(8,128)(2,1)S(1)} %get-tuple-element.44.state_ref, bf16[1728,384]{1,0:T(8,128)(2,1)S(1)} %get-tuple-element.47.xs_ref, bf16[1728,384]{1,0:T(8,128)(2,1)S(1)} %get-tuple-element.48.gs_ref), custom_call_target="tpu_custom_call" | custom-call | tf_op jit(solution)/shard_map/pallas_call | solution.py:458
  8.2 0.8 %collective-permute-done.4 = bf16[864,128]{1,0:T(8,128)(2,1)S(1)} collective-permute-done((bf16[864,128]{1,0:T(8,128)(2,1)S(1)}, bf16[864,128]{1,0:T(8,128)(2,1)S(1)}, u32[]{:S(2)}, u32[]{:S(2)}) %collective-permute-start.4) | collective-permute-done | bytes 221216 | tf_op jit(solution)/shard_map/ppermute | solution.py:354
  9.0 0.6 %collective-permute-start.5 = (bf16[864,128]{1,0:T(8,128)(2,1)S(1)}, bf16[864,128]{1,0:T(8,128)(2,1)S(1)}, u32[]{:S(2)}, u32[]{:S(2)}) collective-permute-start(bf16[864,128]{1,0:T(8,128)(2,1)S(1)} %add_convert_fusion.2), channel_id=1, source_target_pairs={{0,2},{1,9},{2,0},{3,11},{4,6},{5,13},{6,4},{7,15},{8,10},{9,1},{1... | collective-permute-start | bytes 663560 | tf_op jit(solution)/shard_map/ppermute | solution.py:361
  9.6 5.4 %collective-permute-done.5 = bf16[864,128]{1,0:T(8,128)(2,1)S(1)} collective-permute-done((bf16[864,128]{1,0:T(8,128)(2,1)S(1)}, bf16[864,128]{1,0:T(8,128)(2,1)S(1)}, u32[]{:S(2)}, u32[]{:S(2)}) %collective-permute-start.5) | collective-permute-done | bytes 221216 | tf_op jit(solution)/shard_map/ppermute | solution.py:361
  15.0 0.1 add_convert_fusion.1
  15.1 0.5 %collective-permute-start.6 = (bf16[864,128]{1,0:T(8,128)(2,1)S(1)}, bf16[864,128]{1,0:T(8,128)(2,1)S(1)}, u32[]{:S(2)}, u32[]{:S(2)}) collective-permute-start(bf16[864,128]{1,0:T(8,128)(2,1)S(1)} %add_convert_fusion.1), channel_id=1, source_target_pairs={{0,4},{1,3},{2,6},{3,1},{4,0},{5,7},{6,2},{7,5},{8,12},{9,11},{10,... | collective-permute-start | bytes 663560 | tf_op jit(solution)/shard_map/ppermute | solution.py:361
  15.6 5.5 %collective-permute-done.6 = bf16[864,128]{1,0:T(8,128)(2,1)S(1)} collective-permute-done((bf16[864,128]{1,0:T(8,128)(2,1)S(1)}, bf16[864,128]{1,0:T(8,128)(2,1)S(1)}, u32[]{:S(2)}, u32[]{:S(2)}) %collective-permute-start.6) | collective-permute-done | bytes 221216 | tf_op jit(solution)/shard_map/ppermute | solution.py:361
  21.1 0.1 add_convert_fusion
  21.2 0.4 %collective-permute-start.7 = (bf16[864,128]{1,0:T(8,128)(2,1)S(1)}, bf16[864,128]{1,0:T(8,128)(2,1)S(1)}, u32[]{:S(2)}, u32[]{:S(2)}) collective-permute-start(bf16[864,128]{1,0:T(8,128)(2,1)S(1)} %add_convert_fusion), channel_id=1, source_target_pairs={{0,8},{1,5},{2,10},{3,7},{4,12},{5,1},{6,14},{7,3},{8,0},{9,13},{1... | collective-permute-start | bytes 663560 | tf_op jit(solution)/shard_map/ppermute | solution.py:361
  21.6 8.8 %collective-permute-done.7 = bf16[864,128]{1,0:T(8,128)(2,1)S(1)} collective-permute-done((bf16[864,128]{1,0:T(8,128)(2,1)S(1)}, bf16[864,128]{1,0:T(8,128)(2,1)S(1)}, u32[]{:S(2)}, u32[]{:S(2)}) %collective-permute-start.7) | collective-permute-done | bytes 221216 | tf_op jit(solution)/shard_map/ppermute | solution.py:361
  30.4 0.1 multiply_convert_fusion.own_ref
  30.4 0.1 collective-permute-start.8
  30.5 0.5 %collective-permute-start.2 = (bf16[128,128]{1,0:T(8,128)(2,1)S(1)}, bf16[128,128]{1,0:T(8,128)(2,1)S(1)}, u32[]{:S(2)}, u32[]{:S(2)}) collective-permute-start(bf16[128,128]{1,0:T(8,128)(2,1)S(1)} %get-tuple-element.42), channel_id=1, source_target_pairs={{0,1},{1,0},{2,3},{3,2},{4,5},{5,4},{6,7},{7,6},{8,9},{9,8},{10,11... | collective-permute-start | bytes 98312 | tf_op jit(solution)/shard_map/ppermute | solution.py:460
  31.0 0.0 collective-permute-start.3
  31.0 1.0 %collective-permute-done.2.near_ref = bf16[128,128]{1,0:T(8,128)(2,1)S(1)} collective-permute-done((bf16[128,128]{1,0:T(8,128)(2,1)S(1)}, bf16[128,128]{1,0:T(8,128)(2,1)S(1)}, u32[]{:S(2)}, u32[]{:S(2)}) %collective-permute-start.2) | collective-permute-done | bytes 32800 | tf_op jit(solution)/shard_map/ppermute | solution.py:460
  32.0 3.2 %collective-permute-done.3.far_ref = bf16[128,128]{1,0:T(8,128)(2,1)S(1)} collective-permute-done((bf16[128,128]{1,0:T(8,128)(2,1)S(1)}, bf16[128,128]{1,0:T(8,128)(2,1)S(1)}, u32[]{:S(2)}, u32[]{:S(2)}) %collective-permute-start.3) | collective-permute-done | bytes 32800 | tf_op jit(solution)/shard_map/ppermute | solution.py:461
  35.3 2.4 %shard_map.96 = (bf16[64,384]{1,0:T(8,128)(2,1)}, bf16[64,384]{1,0:T(8,128)(2,1)}) custom-call(bf16[128,128]{1,0:T(8,128)(2,1)S(1)} %collective-permute-done.2.near_ref, bf16[128,128]{1,0:T(8,128)(2,1)S(1)} %collective-permute-done.3.far_ref, bf16[3,128,128]{2,1,0:T(8,128)(2,1)S(1)} %get-tuple-element.44.state_ref, ...), custom_call_target="tpu_custom_call" | custom-call | flops 509607936 | bytes 2654208 | tf_op jit(solution)/shard_map/pallas_call | solution.py:476
  37.6 0.8 %shard_map.98 = (f32[64,1728]{1,0:T(8,128)}, f32[64,1728]{1,0:T(8,128)}) custom-call(bf16[864,128]{1,0:T(8,128)(2,1)S(1)} %multiply_convert_fusion.own_ref), custom_call_target="tpu_custom_call" | custom-call | tf_op jit(solution)/shard_map/pallas_call | solution.py:375
  38.4 0.0 collective-permute-done.8.other_ref
  38.4 0.8 %shard_map.99 = (f32[64,1728]{1,0:T(8,128)}, f32[64,1728]{1,0:T(8,128)}) custom-call(bf16[864,128]{1,0:T(8,128)(2,1)S(1)} %collective-permute-done.8.other_ref, f32[64,1728]{1,0:T(8,128)} %get-tuple-element.50.first_in, f32[64,1728]{1,0:T(8,128)} %get-tuple-element.51.second_in), custom_call_target="tpu_custom_call", output_to_operand_aliasing={{0}: (1, {}), {1}: (2, {})} | custom-call | tf_op jit(solution)/shard_map/pallas_call | solution.py:376
  (1 shorter events, 0.0 us)
Async XLA Ops:
  1.7 3.7 %collective-permute-start = (bf16[128,128]{1,0:T(8,128)(2,1)S(1)}, bf16[128,128]{1,0:T(8,128)(2,1)S(1)}, u32[]{:S(2)}, u32[]{:S(2)}) collective-permute-start(bf16[128,128]{1,0:T(8,128)(2,1)S(1)} %get-tuple-element.30), channel_id=1, source_target_pairs={{0,1},{1,0},{2,3},{3,2},{4,5},{5,4},{6,7},{7,6},{8,9},{9,8},{10,11... | collective-permute-start | bytes 98312 | tf_op jit(solution)/shard_map/ppermute | solution.py:421
  1.8 4.4 %collective-permute-start.1 = (bf16[128,128]{1,0:T(8,128)(2,1)S(1)}, bf16[128,128]{1,0:T(8,128)(2,1)S(1)}, u32[]{:S(2)}, u32[]{:S(2)}) collective-permute-start(bf16[128,128]{1,0:T(8,128)(2,1)S(1)} %get-tuple-element.31), channel_id=1, source_target_pairs={{0,16},{1,2},{2,1},{3,4},{4,3},{5,6},{6,5},{7,8},{8,7},{9,10},{10,... | collective-permute-start | bytes 98312 | tf_op jit(solution)/shard_map/ppermute | solution.py:420
  7.4 1.5 %collective-permute-start.4 = (bf16[864,128]{1,0:T(8,128)(2,1)S(1)}, bf16[864,128]{1,0:T(8,128)(2,1)S(1)}, u32[]{:S(2)}, u32[]{:S(2)}) collective-permute-start(bf16[864,128]{1,0:T(8,128)(2,1)S(1)} %get-tuple-element.49), channel_id=1, source_target_pairs={{0,1},{1,0},{2,3},{3,2},{4,5},{5,4},{6,7},{7,6},{8,9},{9,8},{10,11... | collective-permute-start | bytes 663560 | tf_op jit(solution)/shard_map/ppermute | solution.py:354
  9.0 6.0 %collective-permute-start.5 = (bf16[864,128]{1,0:T(8,128)(2,1)S(1)}, bf16[864,128]{1,0:T(8,128)(2,1)S(1)}, u32[]{:S(2)}, u32[]{:S(2)}) collective-permute-start(bf16[864,128]{1,0:T(8,128)(2,1)S(1)} %add_convert_fusion.2), channel_id=1, source_target_pairs={{0,2},{1,9},{2,0},{3,11},{4,6},{5,13},{6,4},{7,15},{8,10},{9,1},{1... | collective-permute-start | bytes 663560 | tf_op jit(solution)/shard_map/ppermute | solution.py:361
  15.1 6.0 %collective-permute-start.6 = (bf16[864,128]{1,0:T(8,128)(2,1)S(1)}, bf16[864,128]{1,0:T(8,128)(2,1)S(1)}, u32[]{:S(2)}, u32[]{:S(2)}) collective-permute-start(bf16[864,128]{1,0:T(8,128)(2,1)S(1)} %add_convert_fusion.1), channel_id=1, source_target_pairs={{0,4},{1,3},{2,6},{3,1},{4,0},{5,7},{6,2},{7,5},{8,12},{9,11},{10,... | collective-permute-start | bytes 663560 | tf_op jit(solution)/shard_map/ppermute | solution.py:361
  21.2 9.2 %collective-permute-start.7 = (bf16[864,128]{1,0:T(8,128)(2,1)S(1)}, bf16[864,128]{1,0:T(8,128)(2,1)S(1)}, u32[]{:S(2)}, u32[]{:S(2)}) collective-permute-start(bf16[864,128]{1,0:T(8,128)(2,1)S(1)} %add_convert_fusion), channel_id=1, source_target_pairs={{0,8},{1,5},{2,10},{3,7},{4,12},{5,1},{6,14},{7,3},{8,0},{9,13},{1... | collective-permute-start | bytes 663560 | tf_op jit(solution)/shard_map/ppermute | solution.py:361
  30.4 8.0 %collective-permute-start.8 = (bf16[864,128]{1,0:T(8,128)(2,1)S(1)}, bf16[864,128]{1,0:T(8,128)(2,1)S(1)}, u32[]{:S(2)}, u32[]{:S(2)}) collective-permute-start(bf16[864,128]{1,0:T(8,128)(2,1)S(1)} %multiply_convert_fusion.own_ref), channel_id=1, source_target_pairs={{0,1},{1,0},{2,3},{3,2},{4,5},{5,4},{6,7},{7,6},{8,9},{9,8},{10,11... | collective-permute-start | bytes 663560 | tf_op jit(solution)/shard_map/ppermute | solution.py:364
  30.5 1.5 %collective-permute-start.2 = (bf16[128,128]{1,0:T(8,128)(2,1)S(1)}, bf16[128,128]{1,0:T(8,128)(2,1)S(1)}, u32[]{:S(2)}, u32[]{:S(2)}) collective-permute-start(bf16[128,128]{1,0:T(8,128)(2,1)S(1)} %get-tuple-element.42), channel_id=1, source_target_pairs={{0,1},{1,0},{2,3},{3,2},{4,5},{5,4},{6,7},{7,6},{8,9},{9,8},{10,11... | collective-permute-start | bytes 98312 | tf_op jit(solution)/shard_map/ppermute | solution.py:460
  31.0 4.2 %collective-permute-start.3 = (bf16[128,128]{1,0:T(8,128)(2,1)S(1)}, bf16[128,128]{1,0:T(8,128)(2,1)S(1)}, u32[]{:S(2)}, u32[]{:S(2)}) collective-permute-start(bf16[128,128]{1,0:T(8,128)(2,1)S(1)} %get-tuple-element.43), channel_id=1, source_target_pairs={{0,16},{1,2},{2,1},{3,4},{4,3},{5,6},{6,5},{7,8},{8,7},{9,10},{10,... | collective-permute-start | bytes 98312 | tf_op jit(solution)/shard_map/ppermute | solution.py:461

commit v10 on v9

--- a/solution.py
+++ b/solution.py
@@ -353,14 +353,25 @@
     cores = [(i, i ^ 1) for i in range(count)]
     received = lax.ppermute(send, "tile", cores)
     total = keep + received.astype(F32)
+    index = lax.axis_index("tile")
     bits = [1 << b for b in range(1, count.bit_length() - 1)]
-    for step, (even_bit, odd_bit) in enumerate(zip(bits, bits[-1:] + bits[:-1])):
+    routes = list(zip(bits, bits[-1:] + bits[:-1]))
+    exchanges = [[(i, i ^ route[i % 2]) for i in range(count)] for route in routes]
+    high = jnp.where(index % 2 == 1, index // routes[0][1], index // routes[0][0]) % 2 == 1
+    half = total.shape[0] // 2
+    for step, pairs in enumerate(exchanges):
         wire = BF16 if step >= len(bits) - 3 else F32
-        pairs = [(i, i ^ (odd_bit if i % 2 else even_bit)) for i in range(count)]
-        sent = total.astype(wire)
+        if step == 0:
+            sent = jnp.where(high, total[:half], total[half:]).astype(wire)
+            total = jnp.where(high, total[half:], total[:half])
+        else:
+            sent = total.astype(wire)
+            total = sent.astype(F32)
         received = lax.ppermute(sent, "tile", pairs)
-        total = sent.astype(F32) + received.astype(F32)
+        total = total + received.astype(F32)
     total = (total * scale).astype(BF16)
+    rest = lax.ppermute(total, "tile", exchanges[0])
+    total = jnp.where(high, jnp.concatenate([rest, total]), jnp.concatenate([total, rest]))
     other = lax.ppermute(total, "tile", cores)
     result = jax.ShapeDtypeStruct(shape, F32)
     staging = [pltpu.VMEM(shape, F32), pltpu.SemaphoreType.DMA((3,))]

time: 39.5 us -> 42.5 us (1.076)
  the two profiles are of different devices: /device:TPU:28 before, /device:TPU:0 now
where the time goes in v10:
time: 42.5 us; the launch traced here: 42.4 us
  starting transfers between devices  15.9 us (37%)
  waiting for transfers between devices  14.2 us (33%)
  Pallas kernels  9.04 us (21%)
  local copies, waits for them, and re-layouts  1.25 us (3%)
  other arithmetic  1.18 us (3%)
  between operations  0.78 us (2%)
    ppermute x3, waiting for transfers between devices, total_over_tiles(): received = lax.ppermute(sent, 'tile', pairs)  8.18 us
    ppermute x3, starting transfers between devices, total_over_tiles(): received = lax.ppermute(sent, 'tile', pairs)  7.48 us
    ppermute x2, starting transfers between devices, body(): far = lax.ppermute(far, axes, far_pairs)  4.09 us
    ppermute x1, starting transfers between devices, total_over_tiles(): rest = lax.ppermute(total, 'tile', exchanges[0])  3.11 us
    ppermute x1, waiting for transfers between devices, total_over_tiles(): rest = lax.ppermute(total, 'tile', exchanges[0])  2.73 us
    ppermute x2, waiting for transfers between devices, body(): far = lax.ppermute(far, axes, far_pairs)  2.4 us
    pallas_call x1, Pallas kernels, body(): second_phase(near, far, state, rule, x, g, w1, w2)  2.36 us
    pallas_call x1, Pallas kernels, body(): xs, gs, pre, d_hidden, turned, w1 = own_phase(rule, x, g, w2, weight_first)  2.1 us
  transfers between devices with their start and end apart: 10, of which 6 were waited for; matrix products, arithmetic and copies ran while one was open for 0% of the time, Pallas kernels for 14%

profile of v10, /device:TPU:0, one launch (start us, length us, event | category | flops | bytes accessed | tf_op | source)
XLA Modules:
  0.0 42.4 jit_solution(13357308756529671317)
XLA Ops:
  0.6 1.1 %shard_map.93 = (bf16[128,128]{1,0:T(8,128)(2,1)S(1)}, bf16[128,128]{1,0:T(8,128)(2,1)S(1)}, s32[2,8,128]{2,1,0:T(8,128)S(1)}, bf16[64,384]{1,0:T(8,128)(2,1)S(1...) custom-call(s32[2]{0:T(128)} %bitcast.1, bf16[64,384]{1,0:T(8,128)(2,1)} %x_hbm.1, ...), custom_call_target="tpu_custom_call" | custom-call | tf_op jit(solution)/shard_map/pallas_call | solution.py:420
  1.7 0.0 copy-start
  1.7 0.6 %collective-permute-start = (bf16[128,128]{1,0:T(8,128)(2,1)S(1)}, bf16[128,128]{1,0:T(8,128)(2,1)S(1)}, u32[]{:S(2)}, u32[]{:S(2)}) collective-permute-start(bf16[128,128]{1,0:T(8,128)(2,1)S(1)} %get-tuple-element.30), channel_id=1, source_target_pairs={{0,1},{1,0},{2,3},{3,2},{4,5},{5,4},{6,7},{7,6},{8,9},{9,8},{10,11... | collective-permute-start | bytes 98312 | tf_op jit(solution)/shard_map/ppermute | solution.py:432
  2.3 2.6 %collective-permute-start.1 = (bf16[128,128]{1,0:T(8,128)(2,1)S(1)}, bf16[128,128]{1,0:T(8,128)(2,1)S(1)}, u32[]{:S(2)}, u32[]{:S(2)}) collective-permute-start(bf16[128,128]{1,0:T(8,128)(2,1)S(1)} %get-tuple-element.31), channel_id=1, source_target_pairs={{0,16},{1,2},{2,1},{3,4},{4,3},{5,6},{6,5},{7,8},{8,7},{9,10},{10,... | collective-permute-start | bytes 98312 | tf_op jit(solution)/shard_map/ppermute | solution.py:431
  4.9 2.1 %shard_map.94 = (bf16[1728,384]{1,0:T(8,128)(2,1)S(1)}, bf16[1728,384]{1,0:T(8,128)(2,1)S(1)}, f32[64,384]{1,0:T(8,128)S(1)}, f32[64,384]{1,0:T(8,128)S(1)}, bf1...) custom-call(s32[27,384]{1,0:T(8,128)S(1)} %get-tuple-element.32.rule_ref, ...), custom_call_target="tpu_custom_call" | custom-call | flops 509607936 | bytes 2654208 | tf_op jit(solution)/shard_map/pallas_call | solution.py:448
  7.0 1.3 %shard_map.95 = (bf16[3,128,128]{2,1,0:T(8,128)(2,1)S(1)}, bf16[128,128]{1,0:T(8,128)(2,1)S(1)}, bf16[128,128]{1,0:T(8,128)(2,1)S(1)}, bf16[864,128]{1,0:T(8,128...) custom-call(s32[2,8,128]{2,1,0:T(8,128)S(1)} %get-tuple-element.29.l, ...), custom_call_target="tpu_custom_call", output_to_operand_aliasing={{4}: (8, {}), {5}: (9, {})} | custom-call | tf_op jit(solution)/shard_map/pallas_call | solution.py:449
  8.3 0.0 copy-start.2
  8.3 0.6 %copy-done.2 = bf16[128,128]{1,0:T(8,128)(2,1)} copy-done((bf16[128,128]{1,0:T(8,128)(2,1)}, bf16[128,128]{1,0:T(8,128)(2,1)S(1)}, u32[]{:S(2)}) %copy-start.2) | copy-done | bytes 32792
  8.9 0.6 %copy-done.4 = bf16[128,128]{1,0:T(8,128)(2,1)} copy-done((bf16[128,128]{1,0:T(8,128)(2,1)}, bf16[128,128]{1,0:T(8,128)(2,1)S(1)}, u32[]{:S(2)}) %copy-start.4) | copy-done | bytes 32792
  9.5 0.1 collective-permute-start.4
  9.6 0.6 %shard_map.97 = f32[864,128]{1,0:T(8,128)S(1)} custom-call(bf16[3,128,128]{2,1,0:T(8,128)(2,1)S(1)} %get-tuple-element.44.state_ref, bf16[1728,384]{1,0:T(8,128)(2,1)S(1)} %get-tuple-element.47.xs_ref, bf16[1728,384]{1,0:T(8,128)(2,1)S(1)} %get-tuple-element.48.gs_ref), custom_call_target="tpu_custom_call" | custom-call | tf_op jit(solution)/shard_map/pallas_call | solution.py:469
  10.3 0.9 %collective-permute-done.4 = bf16[864,128]{1,0:T(8,128)(2,1)} collective-permute-done((bf16[864,128]{1,0:T(8,128)(2,1)S(1)}, bf16[864,128]{1,0:T(8,128)(2,1)}, u32[]{:S(2)}, u32[]{:S(2)}) %collective-permute-start.4) | collective-permute-done | bytes 221216 | tf_op jit(solution)/shard_map/ppermute | solution.py:354
  11.1 1.0 %convert_add_fusion = f32[864,128]{1,0:T(8,128)S(1)} fusion(f32[864,128]{1,0:T(8,128)S(1)} %shard_map.97, bf16[864,128]{1,0:T(8,128)(2,1)} %collective-permute-done.4), kind=kLoop, calls=%fused_computation | loop fusion | flops 221184 | bytes 1105920 | tf_op jit(solution)/shard_map/add | solution.py:355
  12.1 0.0 copy-start.5
  12.1 0.0 copy-start.3
  12.1 0.0 copy-start.1
  12.2 2.3 %collective-permute-start.5 = (bf16[432,128]{1,0:T(8,128)(2,1)S(1)}, bf16[432,128]{1,0:T(8,128)(2,1)S(1)}, u32[]{:S(2)}, u32[]{:S(2)}) collective-permute-start(bf16[432,128]{1,0:T(8,128)(2,1)S(1)} %select_convert_fusion), channel_id=1, source_target_pairs={{0,2},{1,9},{2,0},{3,11},{4,6},{5,13},{6,4},{7,15},{8,10},{9,1},{1... | collective-permute-start | bytes 331784 | tf_op jit(solution)/shard_map/ppermute | solution.py:370
  14.4 2.7 %collective-permute-done.5 = bf16[432,128]{1,0:T(8,128)(2,1)S(1)} collective-permute-done((bf16[432,128]{1,0:T(8,128)(2,1)S(1)}, bf16[432,128]{1,0:T(8,128)(2,1)S(1)}, u32[]{:S(2)}, u32[]{:S(2)}) %collective-permute-start.5) | collective-permute-done | bytes 110624 | tf_op jit(solution)/shard_map/ppermute | solution.py:370
  17.2 2.1 %collective-permute-start.6 = (bf16[432,128]{1,0:T(8,128)(2,1)S(1)}, bf16[432,128]{1,0:T(8,128)(2,1)S(1)}, u32[]{:S(2)}, u32[]{:S(2)}) collective-permute-start(bf16[432,128]{1,0:T(8,128)(2,1)S(1)} %add_convert_fusion.1), channel_id=1, source_target_pairs={{0,4},{1,3},{2,6},{3,1},{4,0},{5,7},{6,2},{7,5},{8,12},{9,11},{10,... | collective-permute-start | bytes 331784 | tf_op jit(solution)/shard_map/ppermute | solution.py:370
  19.3 2.7 %collective-permute-done.6 = bf16[432,128]{1,0:T(8,128)(2,1)S(1)} collective-permute-done((bf16[432,128]{1,0:T(8,128)(2,1)S(1)}, bf16[432,128]{1,0:T(8,128)(2,1)S(1)}, u32[]{:S(2)}, u32[]{:S(2)}) %collective-permute-start.6) | collective-permute-done | bytes 110624 | tf_op jit(solution)/shard_map/ppermute | solution.py:370
  22.1 3.1 %collective-permute-start.7 = (bf16[432,128]{1,0:T(8,128)(2,1)S(1)}, bf16[432,128]{1,0:T(8,128)(2,1)S(1)}, u32[]{:S(2)}, u32[]{:S(2)}) collective-permute-start(bf16[432,128]{1,0:T(8,128)(2,1)S(1)} %add_convert_fusion), channel_id=1, source_target_pairs={{0,8},{1,5},{2,10},{3,7},{4,12},{5,1},{6,14},{7,3},{8,0},{9,13},{1... | collective-permute-start | bytes 331784 | tf_op jit(solution)/shard_map/ppermute | solution.py:370
  25.2 2.7 %collective-permute-done.7 = bf16[432,128]{1,0:T(8,128)(2,1)S(1)} collective-permute-done((bf16[432,128]{1,0:T(8,128)(2,1)S(1)}, bf16[432,128]{1,0:T(8,128)(2,1)S(1)}, u32[]{:S(2)}, u32[]{:S(2)}) %collective-permute-start.7) | collective-permute-done | bytes 110624 | tf_op jit(solution)/shard_map/ppermute | solution.py:370
  28.0 3.1 %collective-permute-start.8 = (bf16[432,128]{1,0:T(8,128)(2,1)S(1)}, bf16[432,128]{1,0:T(8,128)(2,1)S(1)}, u32[]{:S(2)}, u32[]{:S(2)}) collective-permute-start(bf16[432,128]{1,0:T(8,128)(2,1)S(1)} %multiply_convert_fusion), channel_id=1, source_target_pairs={{0,2},{1,9},{2,0},{3,11},{4,6},{5,13},{6,4},{7,15},{8,10},{9,1},{1... | collective-permute-start | bytes 331784 | tf_op jit(solution)/shard_map/ppermute | solution.py:373
  31.1 2.7 %collective-permute-done.8 = bf16[432,128]{1,0:T(8,128)(2,1)S(1)} collective-permute-done((bf16[432,128]{1,0:T(8,128)(2,1)S(1)}, bf16[432,128]{1,0:T(8,128)(2,1)S(1)}, u32[]{:S(2)}, u32[]{:S(2)}) %collective-permute-start.8) | collective-permute-done | bytes 110624 | tf_op jit(solution)/shard_map/ppermute | solution.py:373
  33.8 0.1 maximum_select_fusion.own_ref
  33.9 0.1 collective-permute-start.9
  34.0 0.5 %collective-permute-start.2 = (bf16[128,128]{1,0:T(8,128)(2,1)S(1)}, bf16[128,128]{1,0:T(8,128)(2,1)S(1)}, u32[]{:S(2)}, u32[]{:S(2)}) collective-permute-start(bf16[128,128]{1,0:T(8,128)(2,1)S(1)} %copy-done.5), channel_id=1, source_target_pairs={{0,1},{1,0},{2,3},{3,2},{4,5},{5,4},{6,7},{7,6},{8,9},{9,8},{10,11... | collective-permute-start | bytes 98312 | tf_op jit(solution)/shard_map/ppermute | solution.py:471
  34.5 1.5 %collective-permute-start.3 = (bf16[128,128]{1,0:T(8,128)(2,1)S(1)}, bf16[128,128]{1,0:T(8,128)(2,1)S(1)}, u32[]{:S(2)}, u32[]{:S(2)}) collective-permute-start(bf16[128,128]{1,0:T(8,128)(2,1)S(1)} %copy-done.3), channel_id=1, source_target_pairs={{0,16},{1,2},{2,1},{3,4},{4,3},{5,6},{6,5},{7,8},{8,7},{9,10},{10,... | collective-permute-start | bytes 98312 | tf_op jit(solution)/shard_map/ppermute | solution.py:472
  36.0 2.4 %collective-permute-done.3.far_ref = bf16[128,128]{1,0:T(8,128)(2,1)S(1)} collective-permute-done((bf16[128,128]{1,0:T(8,128)(2,1)S(1)}, bf16[128,128]{1,0:T(8,128)(2,1)S(1)}, u32[]{:S(2)}, u32[]{:S(2)}) %collective-permute-start.3) | collective-permute-done | bytes 32800 | tf_op jit(solution)/shard_map/ppermute | solution.py:472
  38.4 2.4 %shard_map.96 = (bf16[64,384]{1,0:T(8,128)(2,1)}, bf16[64,384]{1,0:T(8,128)(2,1)}) custom-call(bf16[128,128]{1,0:T(8,128)(2,1)S(1)} %collective-permute-done.2.near_ref, bf16[128,128]{1,0:T(8,128)(2,1)S(1)} %collective-permute-done.3.far_ref, bf16[3,128,128]{2,1,0:T(8,128)(2,1)S(1)} %get-tuple-element.44.state_ref, ...), custom_call_target="tpu_custom_call" | custom-call | flops 509607936 | bytes 2654208 | tf_op jit(solution)/shard_map/pallas_call | solution.py:487
  40.7 0.8 %shard_map.98 = (f32[64,1728]{1,0:T(8,128)}, f32[64,1728]{1,0:T(8,128)}) custom-call(bf16[864,128]{1,0:T(8,128)(2,1)S(1)} %maximum_select_fusion.own_ref), custom_call_target="tpu_custom_call" | custom-call | tf_op jit(solution)/shard_map/pallas_call | solution.py:386
  41.5 0.8 %shard_map.99 = (f32[64,1728]{1,0:T(8,128)}, f32[64,1728]{1,0:T(8,128)}) custom-call(bf16[864,128]{1,0:T(8,128)(2,1)S(1)} %collective-permute-done.9.other_ref, f32[64,1728]{1,0:T(8,128)} %get-tuple-element.50.first_in, f32[64,1728]{1,0:T(8,128)} %get-tuple-element.51.second_in), custom_call_target="tpu_custom_call", output_to_operand_aliasing={{0}: (1, {}), {1}: (2, {})} | custom-call | tf_op jit(solution)/shard_map/pallas_call | solution.py:387
  (13 shorter events, 0.2 us)
Async XLA Ops:
  1.7 5.3 %copy-start = (bf16[64,384]{1,0:T(8,128)(2,1)}, bf16[64,384]{1,0:T(8,128)(2,1)S(1)}, u32[]{:S(2)}) copy-start(bf16[64,384]{1,0:T(8,128)(2,1)S(1)} %get-tuple-element.34.g_ref) | copy-start | bytes 147460
  1.7 5.2 %collective-permute-start = (bf16[128,128]{1,0:T(8,128)(2,1)S(1)}, bf16[128,128]{1,0:T(8,128)(2,1)S(1)}, u32[]{:S(2)}, u32[]{:S(2)}) collective-permute-start(bf16[128,128]{1,0:T(8,128)(2,1)S(1)} %get-tuple-element.30), channel_id=1, source_target_pairs={{0,1},{1,0},{2,3},{3,2},{4,5},{5,4},{6,7},{7,6},{8,9},{9,8},{10,11... | collective-permute-start | bytes 98312 | tf_op jit(solution)/shard_map/ppermute | solution.py:432
  2.3 4.7 %collective-permute-start.1 = (bf16[128,128]{1,0:T(8,128)(2,1)S(1)}, bf16[128,128]{1,0:T(8,128)(2,1)S(1)}, u32[]{:S(2)}, u32[]{:S(2)}) collective-permute-start(bf16[128,128]{1,0:T(8,128)(2,1)S(1)} %get-tuple-element.31), channel_id=1, source_target_pairs={{0,16},{1,2},{2,1},{3,4},{4,3},{5,6},{6,5},{7,8},{8,7},{9,10},{10,... | collective-permute-start | bytes 98312 | tf_op jit(solution)/shard_map/ppermute | solution.py:431
  8.3 0.6 %copy-start.2 = (bf16[128,128]{1,0:T(8,128)(2,1)}, bf16[128,128]{1,0:T(8,128)(2,1)S(1)}, u32[]{:S(2)}) copy-start(bf16[128,128]{1,0:T(8,128)(2,1)S(1)} %get-tuple-element.43) | copy-start | bytes 98308
  8.9 0.6 %copy-start.4 = (bf16[128,128]{1,0:T(8,128)(2,1)}, bf16[128,128]{1,0:T(8,128)(2,1)S(1)}, u32[]{:S(2)}) copy-start(bf16[128,128]{1,0:T(8,128)(2,1)S(1)} %get-tuple-element.42) | copy-start | bytes 98308
  9.5 1.6 %collective-permute-start.4 = (bf16[864,128]{1,0:T(8,128)(2,1)S(1)}, bf16[864,128]{1,0:T(8,128)(2,1)}, u32[]{:S(2)}, u32[]{:S(2)}) collective-permute-start(bf16[864,128]{1,0:T(8,128)(2,1)S(1)} %get-tuple-element.49), channel_id=1, source_target_pairs={{0,1},{1,0},{2,3},{3,2},{4,5},{5,4},{6,7},{7,6},{8,9},{9,8},{10,11... | collective-permute-start | bytes 663560 | tf_op jit(solution)/shard_map/ppermute | solution.py:354
  12.1 21.9 %copy-start.5 = (bf16[128,128]{1,0:T(8,128)(2,1)S(1)}, bf16[128,128]{1,0:T(8,128)(2,1)}, u32[]{:S(2)}) copy-start(bf16[128,128]{1,0:T(8,128)(2,1)} %copy-done.4) | copy-start | bytes 98308
  12.1 22.3 %copy-start.3 = (bf16[128,128]{1,0:T(8,128)(2,1)S(1)}, bf16[128,128]{1,0:T(8,128)(2,1)}, u32[]{:S(2)}) copy-start(bf16[128,128]{1,0:T(8,128)(2,1)} %copy-done.2) | copy-start | bytes 98308
  12.1 26.2 %copy-start.1 = (bf16[64,384]{1,0:T(8,128)(2,1)S(1)}, bf16[64,384]{1,0:T(8,128)(2,1)}, u32[]{:S(2)}) copy-start(bf16[64,384]{1,0:T(8,128)(2,1)} %copy-done) | copy-start | bytes 147460
  12.2 5.0 %collective-permute-start.5 = (bf16[432,128]{1,0:T(8,128)(2,1)S(1)}, bf16[432,128]{1,0:T(8,128)(2,1)S(1)}, u32[]{:S(2)}, u32[]{:S(2)}) collective-permute-start(bf16[432,128]{1,0:T(8,128)(2,1)S(1)} %select_convert_fusion), channel_id=1, source_target_pairs={{0,2},{1,9},{2,0},{3,11},{4,6},{5,13},{6,4},{7,15},{8,10},{9,1},{1... | collective-permute-start | bytes 331784 | tf_op jit(solution)/shard_map/ppermute | solution.py:370
  17.2 4.9 %collective-permute-start.6 = (bf16[432,128]{1,0:T(8,128)(2,1)S(1)}, bf16[432,128]{1,0:T(8,128)(2,1)S(1)}, u32[]{:S(2)}, u32[]{:S(2)}) collective-permute-start(bf16[432,128]{1,0:T(8,128)(2,1)S(1)} %add_convert_fusion.1), channel_id=1, source_target_pairs={{0,4},{1,3},{2,6},{3,1},{4,0},{5,7},{6,2},{7,5},{8,12},{9,11},{10,... | collective-permute-start | bytes 331784 | tf_op jit(solution)/shard_map/ppermute | solution.py:370
  22.1 5.8 %collective-permute-start.7 = (bf16[432,128]{1,0:T(8,128)(2,1)S(1)}, bf16[432,128]{1,0:T(8,128)(2,1)S(1)}, u32[]{:S(2)}, u32[]{:S(2)}) collective-permute-start(bf16[432,128]{1,0:T(8,128)(2,1)S(1)} %add_convert_fusion), channel_id=1, source_target_pairs={{0,8},{1,5},{2,10},{3,7},{4,12},{5,1},{6,14},{7,3},{8,0},{9,13},{1... | collective-permute-start | bytes 331784 | tf_op jit(solution)/shard_map/ppermute | solution.py:370
  28.0 5.8 %collective-permute-start.8 = (bf16[432,128]{1,0:T(8,128)(2,1)S(1)}, bf16[432,128]{1,0:T(8,128)(2,1)S(1)}, u32[]{:S(2)}, u32[]{:S(2)}) collective-permute-start(bf16[432,128]{1,0:T(8,128)(2,1)S(1)} %multiply_convert_fusion), channel_id=1, source_target_pairs={{0,2},{1,9},{2,0},{3,11},{4,6},{5,13},{6,4},{7,15},{8,10},{9,1},{1... | collective-permute-start | bytes 331784 | tf_op jit(solution)/shard_map/ppermute | solution.py:373
  33.9 7.7 %collective-permute-start.9 = (bf16[864,128]{1,0:T(8,128)(2,1)S(1)}, bf16[864,128]{1,0:T(8,128)(2,1)S(1)}, u32[]{:S(2)}, u32[]{:S(2)}) collective-permute-start(bf16[864,128]{1,0:T(8,128)(2,1)S(1)} %maximum_select_fusion.own_ref), channel_id=1, source_target_pairs={{0,1},{1,0},{2,3},{3,2},{4,5},{5,4},{6,7},{7,6},{8,9},{9,8},{10,11... | collective-permute-start | bytes 663560 | tf_op jit(solution)/shard_map/ppermute | solution.py:375
  34.0 2.0 %collective-permute-start.2 = (bf16[128,128]{1,0:T(8,128)(2,1)S(1)}, bf16[128,128]{1,0:T(8,128)(2,1)S(1)}, u32[]{:S(2)}, u32[]{:S(2)}) collective-permute-start(bf16[128,128]{1,0:T(8,128)(2,1)S(1)} %copy-done.5), channel_id=1, source_target_pairs={{0,1},{1,0},{2,3},{3,2},{4,5},{5,4},{6,7},{7,6},{8,9},{9,8},{10,11... | collective-permute-start | bytes 98312 | tf_op jit(solution)/shard_map/ppermute | solution.py:471
  34.5 3.9 %collective-permute-start.3 = (bf16[128,128]{1,0:T(8,128)(2,1)S(1)}, bf16[128,128]{1,0:T(8,128)(2,1)S(1)}, u32[]{:S(2)}, u32[]{:S(2)}) collective-permute-start(bf16[128,128]{1,0:T(8,128)(2,1)S(1)} %copy-done.3), channel_id=1, source_target_pairs={{0,16},{1,2},{2,1},{3,4},{4,3},{5,6},{6,5},{7,8},{8,7},{9,10},{10,... | collective-permute-start | bytes 98312 | tf_op jit(solution)/shard_map/ppermute | solution.py:472

commit v11 on v9

--- a/solution.py
+++ b/solution.py
@@ -140,10 +140,33 @@
         turned_ref[:, k * width : (k + count) * width] = joined.astype(BF16)
 
 
-def own_kernel(
-    rule_ref, x_ref, g_ref, w2_ref, w1_hbm,
-    xs_ref, gs_ref, pre_ref, d_hidden_ref, turned_ref, w1_ref,
-    table_ref, sems,
+def listed_blocks(lists_ref):
+    return [jnp.max(lists_ref[side].astype(F32)).astype(jnp.int32) for side in range(2)]
+
+
+def halo_rows(side, listed, table, rule_ref, blocks):
+    width = table.shape[0] // 2
+    offsets = rule_ref.shape[0]
+    group = offsets // 3
+    upper = side == 1
+    block = jnp.where(upper, listed[1], listed[0])
+    columns = pl.ds(pl.multiple_of(jnp.minimum(block, blocks - 1) * BLOCK, BLOCK), BLOCK)
+    far_start = (offsets - group) * width
+    start = pl.multiple_of(jnp.where(upper, far_start, 0), BLOCK)
+    mirrored = pl.multiple_of(jnp.where(upper, 0, far_start), BLOCK)
+    lines = jnp.where(
+        upper, rule_ref[offsets - group : offsets, columns], rule_ref[:group, columns]
+    )
+    local = lines - (blocks + side) * BLOCK
+    found = select_rows(table, lax.broadcasted_iota(jnp.int32, (BLOCK, BLOCK), 0), local)
+    first = [rows[:width] for rows in found]
+    second = [rows[width:] for rows in found[::-1]]
+    depth = group * width
+    return block < blocks, columns, pl.ds(start, depth), pl.ds(mirrored, depth), first, second
+
+
+def own_gather_kernel(
+    rule_ref, x_ref, g_ref, w1_hbm, xs_ref, gs_ref, w1_ref, table_ref, sems
 ):
     copies = fetch((w1_hbm,), (w1_ref,), sems)
     width, rows = x_ref.shape
@@ -154,10 +177,30 @@
         table_ref[block, width:] = g_ref[:, low:high]
     table_ref[blocks:] = jnp.zeros_like(table_ref[blocks:])
     gather(table_ref, rule_ref, xs_ref, gs_ref, blocks)
-    turn(w2_ref, turned_ref)
-    d_hidden_ref[...] = jnp.dot(turned_ref[...], gs_ref[...], preferred_element_type=F32)
     for copy in copies:
         copy.wait()
+
+
+def insert_rows(target_ref, span, columns, named, pieces):
+    width = pieces[0].shape[0]
+    for i, piece in enumerate(pieces):
+        place = pl.ds(pl.multiple_of(span.start + i * width, width), width)
+        target_ref[place, columns] = jnp.where(named, piece, target_ref[place, columns])
+
+
+def own_conv_kernel(
+    lists_ref, near_ref, rule_ref, w1_ref, w2_ref, xs_in, gs_in,
+    pre_ref, d_hidden_ref, turned_ref, xs_ref, gs_ref,
+):
+    blocks = pre_ref.shape[1] // BLOCK
+    turn(w2_ref, turned_ref)
+    side = jnp.where(is_odd(), 0, 1)
+    named, columns, span, mirror_span, first, second = halo_rows(
+        side, listed_blocks(lists_ref), near_ref[...], rule_ref, blocks
+    )
+    insert_rows(xs_ref, span, columns, named, first)
+    insert_rows(gs_ref, mirror_span, columns, named, second)
+    d_hidden_ref[...] = jnp.dot(turned_ref[...], gs_ref[...], preferred_element_type=F32)
     pre_ref[...] = jnp.dot(w1_ref[...], xs_ref[...], preferred_element_type=F32)
 
 
@@ -208,42 +251,28 @@
 
 
 def rim_kernel(
-    lists_ref, near_ref, far_ref, pre_in, d_hidden_in, rule_ref, w1_ref, turned_ref, xs_in, gs_in,
+    lists_ref, far_ref, pre_in, d_hidden_in, rule_ref, w1_ref, turned_ref, xs_in, gs_in,
     state_ref, near_out, far_out, send_ref, xs_ref, gs_ref,
     pre_ref, d_hidden_ref, rim_ref,
 ):
     width, rows = pre_in.shape
     blocks = rows // BLOCK
-    offsets = rule_ref.shape[0]
-    group = offsets // 3
     odd = is_odd()
-    listed = [jnp.max(lists_ref[side].astype(F32)).astype(jnp.int32) for side in range(2)]
-    near, far = near_ref[...], far_ref[...]
-    tables = (jnp.where(odd, near, far), jnp.where(odd, far, near))
+    listed = listed_blocks(lists_ref)
+    named, columns, span, mirror_span, first, second = halo_rows(
+        jnp.where(odd, 1, 0), listed, far_ref[...], rule_ref, blocks
+    )
     pre_ref[...] = pre_in[...]
     d_hidden_ref[...] = d_hidden_in[...]
-    source_rows = lax.broadcasted_iota(jnp.int32, (BLOCK, BLOCK), 0)
-    sides = []
-    for side in range(2):
-        columns = pl.ds(pl.multiple_of(jnp.minimum(listed[side], blocks - 1) * BLOCK, BLOCK), BLOCK)
-        start = 2 * side * group
-        mirrored = offsets - group - start
-        span = slice(start * width, (start + group) * width)
-        mirror_span = slice(mirrored * width, (mirrored + group) * width)
-        sides.append((listed[side] < blocks, columns, span, mirror_span))
-        local = rule_ref[start : start + group, columns] - (blocks + side) * BLOCK
-        for j, found in enumerate(select_rows(tables[side], source_rows, local)):
-            rim_ref[2 * side, j * width : (j + 1) * width] = found[:width]
-            place = (group - 1 - j) * width
-            rim_ref[2 * side + 1, place : place + width] = found[width:]
-    for side, (named, columns, span, mirror_span) in enumerate(sides):
-        rim_x, rim_g = rim_ref[2 * side], rim_ref[2 * side + 1]
-        pre_ref[:, columns] += jnp.dot(w1_ref[:, span], rim_x, preferred_element_type=F32)
-        d_hidden_ref[:, columns] += jnp.dot(
-            turned_ref[:, mirror_span], rim_g, preferred_element_type=F32
-        )
-        xs_ref[span, columns] = jnp.where(named, rim_x, xs_ref[span, columns])
-        gs_ref[mirror_span, columns] = jnp.where(named, rim_g, gs_ref[mirror_span, columns])
+    for i, (x_rows, g_rows) in enumerate(zip(first, second)):
+        rim_ref[0, i * width : (i + 1) * width] = x_rows
+        rim_ref[1, i * width : (i + 1) * width] = g_rows
+    pre_ref[:, columns] += jnp.dot(w1_ref[:, span], rim_ref[0], preferred_element_type=F32)
+    d_hidden_ref[:, columns] += jnp.dot(
+        turned_ref[:, mirror_span], rim_ref[1], preferred_element_type=F32
+    )
+    insert_rows(xs_ref, span, columns, named, first)
+    insert_rows(gs_ref, mirror_span, columns, named, second)
     pre = pre_ref[...]
     sigma = jax.nn.sigmoid(pre)
     hidden = (pre * sigma).astype(BF16)
@@ -425,29 +454,39 @@
         bytes_accessed=4 * offsets * width * rows,
         transcendentals=0,
     )
-    own_phase = pl.pallas_call(
-        own_kernel,
-        out_shape=(gathered, gathered, sums, sums, weight, weight),
-        in_specs=[VMEM] * 4 + [HBM],
-        out_specs=(VMEM,) * 6,
+    own_gather = pl.pallas_call(
+        own_gather_kernel,
+        out_shape=(gathered, gathered, weight),
+        in_specs=[VMEM] * 3 + [HBM],
+        out_specs=(VMEM,) * 3,
         scratch_shapes=[table, pltpu.SemaphoreType.DMA((1,))],
         compiler_params=MEDIUM,
         cost_estimate=work,
     )
-    xs, gs, pre, d_hidden, turned, w1 = own_phase(rule, x, g, w2, weight_first)
+    xs, gs, w1 = own_gather(rule, x, g, weight_first)
+    own_conv = pl.pallas_call(
+        own_conv_kernel,
+        out_shape=(sums, sums, weight, gathered, gathered),
+        in_specs=[VMEM] * 7,
+        out_specs=(VMEM,) * 5,
+        input_output_aliases={5: 3, 6: 4},
+        compiler_params=MEDIUM,
+        cost_estimate=work,
+    )
+    pre, d_hidden, turned, xs, gs = own_conv(lists, near, rule, w1, w2, xs, gs)
     state, near, far, send, xs, gs = pl.pallas_call(
         rim_kernel,
         out_shape=(state_shape, rim, rim, shape(packed, BF16), gathered, gathered),
-        in_specs=[VMEM] * 10,
+        in_specs=[VMEM] * 9,
         out_specs=(VMEM,) * 6,
         scratch_shapes=[
             pltpu.VMEM((width, rows), F32),
             pltpu.VMEM((width, rows), F32),
-            pltpu.VMEM((4, offsets // 3 * width, BLOCK), BF16),
+            pltpu.VMEM((2, offsets // 3 * width, BLOCK), BF16),
         ],
-        input_output_aliases={8: 4, 9: 5},
-        compiler_params=MEDIUM,
-    )(lists, near, far, pre, d_hidden, rule, w1, turned, xs, gs)
+        input_output_aliases={7: 4, 8: 5},
+        compiler_params=MEDIUM,
+    )(lists, far, pre, d_hidden, rule, w1, turned, xs, gs)
     keep_terms = pl.pallas_call(
         keep_kernel,
         out_shape=shape(packed, F32),

time: 39.5 us -> 39.2 us (level)
    ppermute x2, starting transfers between devices: 0.57 us -> 1.29 us  [body(): near = lax.ppermute(near, axes, near_pairs)]
    ppermute x2, starting transfers between devices: 1.48 us -> 0.88 us  [body(): far = lax.ppermute(far, axes, far_pairs)]
    pallas_call x1 -> x2, Pallas kernels: 2.1 us -> 2.11 us  [the longest x1 1.11 us: body(): xs, gs, w1 = own_gather(rule, x, g, weight_first)]
where the time goes in v11:
time: 39.2 us; the launch traced here: 39 us
  waiting for transfers between devices  25.2 us (64%)
  Pallas kernels  8.94 us (23%)
  starting transfers between devices  3.87 us (10%)
  between operations  0.72 us (2%)
    ppermute x3, waiting for transfers between devices, total_over_tiles(): received = lax.ppermute(sent, 'tile', pairs)  19.6 us
    ppermute x2, waiting for transfers between devices, body(): far = lax.ppermute(far, axes, far_pairs)  3.73 us
    pallas_call x1, Pallas kernels, body(): second_phase(near, far, state, rule, x, g, w1, w2)  2.36 us
    ppermute x3, starting transfers between devices, total_over_tiles(): received = lax.ppermute(sent, 'tile', pairs)  1.56 us
    ppermute x2, starting transfers between devices, body(): near = lax.ppermute(near, axes, near_pairs)  1.29 us
    pallas_call x1, Pallas kernels, body(): pl.pallas_call(rim_kernel, out_shape=(state_shape, rim, rim, shape(packed...  1.15 us
    pallas_call x1, Pallas kernels, body(): xs, gs, w1 = own_gather(rule, x, g, weight_first)  1.11 us
    pallas_call x1, Pallas kernels, body(): pl.pallas_call(load_kernel, out_shape=(rim, rim, shape((2, 8, BLOCK), jnp...  1.07 us
  transfers between devices with their start and end apart: 9, of which 7 were waited for; matrix products, arithmetic and copies ran while one was open for 0% of the time, Pallas kernels for 15%

profile of v11, /device:TPU:28, one launch (start us, length us, event | category | flops | bytes accessed | tf_op | source)
XLA Modules:
  0.0 39.0 jit_solution(8307887455513136702)
XLA Ops:
  0.6 1.1 %shard_map.93 = (bf16[128,128]{1,0:T(8,128)(2,1)S(1)}, bf16[128,128]{1,0:T(8,128)(2,1)S(1)}, s32[2,8,128]{2,1,0:T(8,128)S(1)}, bf16[64,384]{1,0:T(8,128)(2,1)S(1...) custom-call(s32[2]{0:T(128)} %bitcast.1, bf16[64,384]{1,0:T(8,128)(2,1)} %x_hbm.1, ...), custom_call_target="tpu_custom_call" | custom-call | tf_op jit(solution)/shard_map/pallas_call | solution.py:438
  1.7 0.9 %collective-permute-start = (bf16[128,128]{1,0:T(8,128)(2,1)S(1)}, bf16[128,128]{1,0:T(8,128)(2,1)S(1)}, u32[]{:S(2)}, u32[]{:S(2)}) collective-permute-start(bf16[128,128]{1,0:T(8,128)(2,1)S(1)} %get-tuple-element.32), channel_id=1, source_target_pairs={{0,16},{1,2},{2,1},{3,4},{4,3},{5,6},{6,5},{7,8},{8,7},{9,10},{10,... | collective-permute-start | bytes 98312 | tf_op jit(solution)/shard_map/ppermute | solution.py:449
  2.6 0.8 %collective-permute-start.1 = (bf16[128,128]{1,0:T(8,128)(2,1)S(1)}, bf16[128,128]{1,0:T(8,128)(2,1)S(1)}, u32[]{:S(2)}, u32[]{:S(2)}) collective-permute-start(bf16[128,128]{1,0:T(8,128)(2,1)S(1)} %get-tuple-element.33), channel_id=1, source_target_pairs={{0,1},{1,0},{2,3},{3,2},{4,5},{5,4},{6,7},{7,6},{8,9},{9,8},{10,11... | collective-permute-start | bytes 98312 | tf_op jit(solution)/shard_map/ppermute | solution.py:450
  3.4 1.1 %shard_map.94 = (bf16[1728,384]{1,0:T(8,128)(2,1)S(1)}, bf16[1728,384]{1,0:T(8,128)(2,1)S(1)}, bf16[64,1728]{1,0:T(8,128)(2,1)S(1)}) custom-call(s32[27,384]{1,0:T(8,128)S(1)} %get-tuple-element.34.rule_ref, bf16[64,384]{1,0:T(8,128)(2,1)S(1)} %get-tuple-element.35.x_ref, bf16[64,384]{1,0:T(8,128)(2,1)S(1)} %get-tuple-element.36.g_ref, bf16[64,1728]{1,0:T(8,128)(2,1)} %w1_hbm.1), custom_call_target="tpu_custom_call" | custom-call | flops 509607936 | bytes 2654208 | tf_op jit(solution)/shard_map/pallas_call | solution.py:466
  4.5 0.0 collective-permute-done.1.near_ref
  4.5 1.0 %shard_map.95 = (f32[64,384]{1,0:T(8,128)S(1)}, f32[64,384]{1,0:T(8,128)S(1)}, bf16[64,1728]{1,0:T(8,128)(2,1)S(1)}, bf16[1728,384]{1,0:T(8,128)(2,1)S(1)}, bf16[1728,384]{1,0:T(8,128)(2,1)S(1)}) custom-call(s32[2,8,128]{2,1,0:T(8,128)S(1)} %get-tuple-element.31.lists_ref, ...), custom_call_target="tpu_custom_call", output_to_operand_aliasing={{3}: (5, {}), {4}: (6, {})} | custom-call | flops 509607936 | bytes 2654208 | tf_op jit(solution)/shard_map/pallas_call | solution.py:476
  5.5 0.5 %collective-permute-done.far_ref = bf16[128,128]{1,0:T(8,128)(2,1)S(1)} collective-permute-done((bf16[128,128]{1,0:T(8,128)(2,1)S(1)}, bf16[128,128]{1,0:T(8,128)(2,1)S(1)}, u32[]{:S(2)}, u32[]{:S(2)}) %collective-permute-start) | collective-permute-done | bytes 32800 | tf_op jit(solution)/shard_map/ppermute | solution.py:449
  6.0 1.1 %shard_map.96 = (bf16[3,128,128]{2,1,0:T(8,128)(2,1)S(1)}, bf16[128,128]{1,0:T(8,128)(2,1)S(1)}, bf16[128,128]{1,0:T(8,128)(2,1)S(1)}, bf16[864,128]{1,0:T(8,128...) custom-call(s32[2,8,128]{2,1,0:T(8,128)S(1)} %get-tuple-element.31.l, ...), custom_call_target="tpu_custom_call", output_to_operand_aliasing={{4}: (7, {}), {5}: (8, {})} | custom-call | tf_op jit(solution)/shard_map/pallas_call | solution.py:477
  7.2 0.1 collective-permute-start.4
  7.2 0.6 %shard_map.98 = f32[864,128]{1,0:T(8,128)S(1)} custom-call(bf16[3,128,128]{2,1,0:T(8,128)(2,1)S(1)} %get-tuple-element.48.state_ref, bf16[1728,384]{1,0:T(8,128)(2,1)S(1)} %get-tuple-element.51.xs_ref, bf16[1728,384]{1,0:T(8,128)(2,1)S(1)} %get-tuple-element.52.gs_ref), custom_call_target="tpu_custom_call" | custom-call | tf_op jit(solution)/shard_map/pallas_call | solution.py:497
  7.9 0.8 %collective-permute-done.4 = bf16[864,128]{1,0:T(8,128)(2,1)S(1)} collective-permute-done((bf16[864,128]{1,0:T(8,128)(2,1)S(1)}, bf16[864,128]{1,0:T(8,128)(2,1)S(1)}, u32[]{:S(2)}, u32[]{:S(2)}) %collective-permute-start.4) | collective-permute-done | bytes 221216 | tf_op jit(solution)/shard_map/ppermute | solution.py:383
  8.8 0.7 %collective-permute-start.5 = (bf16[864,128]{1,0:T(8,128)(2,1)S(1)}, bf16[864,128]{1,0:T(8,128)(2,1)S(1)}, u32[]{:S(2)}, u32[]{:S(2)}) collective-permute-start(bf16[864,128]{1,0:T(8,128)(2,1)S(1)} %add_convert_fusion.2), channel_id=1, source_target_pairs={{0,2},{1,9},{2,0},{3,11},{4,6},{5,13},{6,4},{7,15},{8,10},{9,1},{1... | collective-permute-start | bytes 663560 | tf_op jit(solution)/shard_map/ppermute | solution.py:390
  9.4 5.3 %collective-permute-done.5 = bf16[864,128]{1,0:T(8,128)(2,1)S(1)} collective-permute-done((bf16[864,128]{1,0:T(8,128)(2,1)S(1)}, bf16[864,128]{1,0:T(8,128)(2,1)S(1)}, u32[]{:S(2)}, u32[]{:S(2)}) %collective-permute-start.5) | collective-permute-done | bytes 221216 | tf_op jit(solution)/shard_map/ppermute | solution.py:390
  14.8 0.1 add_convert_fusion.1
  14.8 0.5 %collective-permute-start.6 = (bf16[864,128]{1,0:T(8,128)(2,1)S(1)}, bf16[864,128]{1,0:T(8,128)(2,1)S(1)}, u32[]{:S(2)}, u32[]{:S(2)}) collective-permute-start(bf16[864,128]{1,0:T(8,128)(2,1)S(1)} %add_convert_fusion.1), channel_id=1, source_target_pairs={{0,4},{1,3},{2,6},{3,1},{4,0},{5,7},{6,2},{7,5},{8,12},{9,11},{10,... | collective-permute-start | bytes 663560 | tf_op jit(solution)/shard_map/ppermute | solution.py:390
  15.3 5.5 %collective-permute-done.6 = bf16[864,128]{1,0:T(8,128)(2,1)S(1)} collective-permute-done((bf16[864,128]{1,0:T(8,128)(2,1)S(1)}, bf16[864,128]{1,0:T(8,128)(2,1)S(1)}, u32[]{:S(2)}, u32[]{:S(2)}) %collective-permute-start.6) | collective-permute-done | bytes 221216 | tf_op jit(solution)/shard_map/ppermute | solution.py:390
  20.8 0.1 add_convert_fusion
  20.9 0.4 %collective-permute-start.7 = (bf16[864,128]{1,0:T(8,128)(2,1)S(1)}, bf16[864,128]{1,0:T(8,128)(2,1)S(1)}, u32[]{:S(2)}, u32[]{:S(2)}) collective-permute-start(bf16[864,128]{1,0:T(8,128)(2,1)S(1)} %add_convert_fusion), channel_id=1, source_target_pairs={{0,8},{1,5},{2,10},{3,7},{4,12},{5,1},{6,14},{7,3},{8,0},{9,13},{1... | collective-permute-start | bytes 663560 | tf_op jit(solution)/shard_map/ppermute | solution.py:390
  21.3 8.8 %collective-permute-done.7 = bf16[864,128]{1,0:T(8,128)(2,1)S(1)} collective-permute-done((bf16[864,128]{1,0:T(8,128)(2,1)S(1)}, bf16[864,128]{1,0:T(8,128)(2,1)S(1)}, u32[]{:S(2)}, u32[]{:S(2)}) %collective-permute-start.7) | collective-permute-done | bytes 221216 | tf_op jit(solution)/shard_map/ppermute | solution.py:390
  30.1 0.1 multiply_convert_fusion.own_ref
  30.2 0.1 collective-permute-start.8
  30.2 0.5 %collective-permute-start.2 = (bf16[128,128]{1,0:T(8,128)(2,1)S(1)}, bf16[128,128]{1,0:T(8,128)(2,1)S(1)}, u32[]{:S(2)}, u32[]{:S(2)}) collective-permute-start(bf16[128,128]{1,0:T(8,128)(2,1)S(1)} %get-tuple-element.46), channel_id=1, source_target_pairs={{0,1},{1,0},{2,3},{3,2},{4,5},{5,4},{6,7},{7,6},{8,9},{9,8},{10,11... | collective-permute-start | bytes 98312 | tf_op jit(solution)/shard_map/ppermute | solution.py:499
  30.7 0.0 collective-permute-start.3
  30.8 1.0 %collective-permute-done.2.near_ref = bf16[128,128]{1,0:T(8,128)(2,1)S(1)} collective-permute-done((bf16[128,128]{1,0:T(8,128)(2,1)S(1)}, bf16[128,128]{1,0:T(8,128)(2,1)S(1)}, u32[]{:S(2)}, u32[]{:S(2)}) %collective-permute-start.2) | collective-permute-done | bytes 32800 | tf_op jit(solution)/shard_map/ppermute | solution.py:499
  31.8 3.2 %collective-permute-done.3.far_ref = bf16[128,128]{1,0:T(8,128)(2,1)S(1)} collective-permute-done((bf16[128,128]{1,0:T(8,128)(2,1)S(1)}, bf16[128,128]{1,0:T(8,128)(2,1)S(1)}, u32[]{:S(2)}, u32[]{:S(2)}) %collective-permute-start.3) | collective-permute-done | bytes 32800 | tf_op jit(solution)/shard_map/ppermute | solution.py:500
  35.0 2.4 %shard_map.97 = (bf16[64,384]{1,0:T(8,128)(2,1)}, bf16[64,384]{1,0:T(8,128)(2,1)}) custom-call(bf16[128,128]{1,0:T(8,128)(2,1)S(1)} %collective-permute-done.2.near_ref, bf16[128,128]{1,0:T(8,128)(2,1)S(1)} %collective-permute-done.3.far_ref, bf16[3,128,128]{2,1,0:T(8,128)(2,1)S(1)} %get-tuple-element.48.state_ref, ...), custom_call_target="tpu_custom_call" | custom-call | flops 509607936 | bytes 2654208 | tf_op jit(solution)/shard_map/pallas_call | solution.py:515
  37.4 0.8 %shard_map.99 = (f32[64,1728]{1,0:T(8,128)}, f32[64,1728]{1,0:T(8,128)}) custom-call(bf16[864,128]{1,0:T(8,128)(2,1)S(1)} %multiply_convert_fusion.own_ref), custom_call_target="tpu_custom_call" | custom-call | tf_op jit(solution)/shard_map/pallas_call | solution.py:404
  38.2 0.0 collective-permute-done.8.other_ref
  38.2 0.8 %shard_map.100 = (f32[64,1728]{1,0:T(8,128)}, f32[64,1728]{1,0:T(8,128)}) custom-call(bf16[864,128]{1,0:T(8,128)(2,1)S(1)} %collective-permute-done.8.other_ref, f32[64,1728]{1,0:T(8,128)} %get-tuple-element.54.first_in, f32[64,1728]{1,0:T(8,128)} %get-tuple-element.55.second_in), custom_call_target="tpu_custom_call", output_to_operand_aliasing={{0}: (1, {}), {1}: (2, {})} | custom-call | tf_op jit(solution)/shard_map/pallas_call | solution.py:405
  (1 shorter events, 0.0 us)
Async XLA Ops:
  1.7 4.3 %collective-permute-start = (bf16[128,128]{1,0:T(8,128)(2,1)S(1)}, bf16[128,128]{1,0:T(8,128)(2,1)S(1)}, u32[]{:S(2)}, u32[]{:S(2)}) collective-permute-start(bf16[128,128]{1,0:T(8,128)(2,1)S(1)} %get-tuple-element.32), channel_id=1, source_target_pairs={{0,16},{1,2},{2,1},{3,4},{4,3},{5,6},{6,5},{7,8},{8,7},{9,10},{10,... | collective-permute-start | bytes 98312 | tf_op jit(solution)/shard_map/ppermute | solution.py:449
  2.6 1.9 %collective-permute-start.1 = (bf16[128,128]{1,0:T(8,128)(2,1)S(1)}, bf16[128,128]{1,0:T(8,128)(2,1)S(1)}, u32[]{:S(2)}, u32[]{:S(2)}) collective-permute-start(bf16[128,128]{1,0:T(8,128)(2,1)S(1)} %get-tuple-element.33), channel_id=1, source_target_pairs={{0,1},{1,0},{2,3},{3,2},{4,5},{5,4},{6,7},{7,6},{8,9},{9,8},{10,11... | collective-permute-start | bytes 98312 | tf_op jit(solution)/shard_map/ppermute | solution.py:450
  7.2 1.5 %collective-permute-start.4 = (bf16[864,128]{1,0:T(8,128)(2,1)S(1)}, bf16[864,128]{1,0:T(8,128)(2,1)S(1)}, u32[]{:S(2)}, u32[]{:S(2)}) collective-permute-start(bf16[864,128]{1,0:T(8,128)(2,1)S(1)} %get-tuple-element.53), channel_id=1, source_target_pairs={{0,1},{1,0},{2,3},{3,2},{4,5},{5,4},{6,7},{7,6},{8,9},{9,8},{10,11... | collective-permute-start | bytes 663560 | tf_op jit(solution)/shard_map/ppermute | solution.py:383
  8.8 6.0 %collective-permute-start.5 = (bf16[864,128]{1,0:T(8,128)(2,1)S(1)}, bf16[864,128]{1,0:T(8,128)(2,1)S(1)}, u32[]{:S(2)}, u32[]{:S(2)}) collective-permute-start(bf16[864,128]{1,0:T(8,128)(2,1)S(1)} %add_convert_fusion.2), channel_id=1, source_target_pairs={{0,2},{1,9},{2,0},{3,11},{4,6},{5,13},{6,4},{7,15},{8,10},{9,1},{1... | collective-permute-start | bytes 663560 | tf_op jit(solution)/shard_map/ppermute | solution.py:390
  14.8 6.0 %collective-permute-start.6 = (bf16[864,128]{1,0:T(8,128)(2,1)S(1)}, bf16[864,128]{1,0:T(8,128)(2,1)S(1)}, u32[]{:S(2)}, u32[]{:S(2)}) collective-permute-start(bf16[864,128]{1,0:T(8,128)(2,1)S(1)} %add_convert_fusion.1), channel_id=1, source_target_pairs={{0,4},{1,3},{2,6},{3,1},{4,0},{5,7},{6,2},{7,5},{8,12},{9,11},{10,... | collective-permute-start | bytes 663560 | tf_op jit(solution)/shard_map/ppermute | solution.py:390
  20.9 9.2 %collective-permute-start.7 = (bf16[864,128]{1,0:T(8,128)(2,1)S(1)}, bf16[864,128]{1,0:T(8,128)(2,1)S(1)}, u32[]{:S(2)}, u32[]{:S(2)}) collective-permute-start(bf16[864,128]{1,0:T(8,128)(2,1)S(1)} %add_convert_fusion), channel_id=1, source_target_pairs={{0,8},{1,5},{2,10},{3,7},{4,12},{5,1},{6,14},{7,3},{8,0},{9,13},{1... | collective-permute-start | bytes 663560 | tf_op jit(solution)/shard_map/ppermute | solution.py:390
  30.2 8.0 %collective-permute-start.8 = (bf16[864,128]{1,0:T(8,128)(2,1)S(1)}, bf16[864,128]{1,0:T(8,128)(2,1)S(1)}, u32[]{:S(2)}, u32[]{:S(2)}) collective-permute-start(bf16[864,128]{1,0:T(8,128)(2,1)S(1)} %multiply_convert_fusion.own_ref), channel_id=1, source_target_pairs={{0,1},{1,0},{2,3},{3,2},{4,5},{5,4},{6,7},{7,6},{8,9},{9,8},{10,11... | collective-permute-start | bytes 663560 | tf_op jit(solution)/shard_map/ppermute | solution.py:393
  30.2 1.5 %collective-permute-start.2 = (bf16[128,128]{1,0:T(8,128)(2,1)S(1)}, bf16[128,128]{1,0:T(8,128)(2,1)S(1)}, u32[]{:S(2)}, u32[]{:S(2)}) collective-permute-start(bf16[128,128]{1,0:T(8,128)(2,1)S(1)} %get-tuple-element.46), channel_id=1, source_target_pairs={{0,1},{1,0},{2,3},{3,2},{4,5},{5,4},{6,7},{7,6},{8,9},{9,8},{10,11... | collective-permute-start | bytes 98312 | tf_op jit(solution)/shard_map/ppermute | solution.py:499
  30.7 4.2 %collective-permute-start.3 = (bf16[128,128]{1,0:T(8,128)(2,1)S(1)}, bf16[128,128]{1,0:T(8,128)(2,1)S(1)}, u32[]{:S(2)}, u32[]{:S(2)}) collective-permute-start(bf16[128,128]{1,0:T(8,128)(2,1)S(1)} %get-tuple-element.47), channel_id=1, source_target_pairs={{0,16},{1,2},{2,1},{3,4},{4,3},{5,6},{6,5},{7,8},{8,7},{9,10},{10,... | collective-permute-start | bytes 98312 | tf_op jit(solution)/shard_map/ppermute | solution.py:500

commit v12 on v11

--- a/solution.py
+++ b/solution.py
@@ -36,15 +36,13 @@
 
 
 def load_kernel(
-    lists_hbm, x_hbm, g_hbm, rule_hbm, w2_hbm,
-    near_ref, far_ref, lists_out, x_ref, g_ref, rule_ref, w2_ref,
+    lists_hbm, x_hbm, g_hbm, rule_hbm,
+    near_ref, far_ref, lists_out, x_ref, g_ref, rule_ref,
     lists_ref, sems,
 ):
     width, rows = x_ref.shape
     copies = fetch(
-        (lists_hbm, x_hbm, g_hbm, rule_hbm, w2_hbm),
-        (lists_ref, x_ref, g_ref, rule_ref, w2_ref),
-        sems,
+        (lists_hbm, x_hbm, g_hbm, rule_hbm), (lists_ref, x_ref, g_ref, rule_ref), sems
     )
     for copy in copies[:3]:
         copy.wait()
@@ -166,9 +164,11 @@
 
 
 def own_gather_kernel(
-    rule_ref, x_ref, g_ref, w1_hbm, xs_ref, gs_ref, w1_ref, table_ref, sems
+    rule_ref, x_ref, g_ref, w2_hbm, w1_hbm,
+    xs_ref, gs_ref, w2_ref, w1_ref,
+    table_ref, sems,
 ):
-    copies = fetch((w1_hbm,), (w1_ref,), sems)
+    copies = fetch((w2_hbm, w1_hbm), (w2_ref, w1_ref), sems)
     width, rows = x_ref.shape
     blocks = rows // BLOCK
     for block in range(blocks):
@@ -308,7 +308,7 @@
 def put(source_ref, for_odd, for_even, staging_ref, sems):
     width, depth = staging_ref.shape
     pairs = depth // BLOCK
-    cuts = [0, pairs // 3 * BLOCK, 2 * pairs // 3 * BLOCK, depth]
+    cuts = [0, pairs // 2 * BLOCK, 6 * pairs // 7 * BLOCK, depth]
 
     def unpack(low, high):
         for at in range(low, high, BLOCK):
@@ -383,7 +383,7 @@
     received = lax.ppermute(send, "tile", cores)
     total = keep + received.astype(F32)
     bits = [1 << b for b in range(1, count.bit_length() - 1)]
-    for step, (even_bit, odd_bit) in enumerate(zip(bits, bits[-1:] + bits[:-1])):
+    for step, (even_bit, odd_bit) in enumerate(zip(bits[-1:] + bits[:-1], bits[-2:] + bits[:-2])):
         wire = BF16 if step >= len(bits) - 3 else F32
         pairs = [(i, i ^ (odd_bit if i % 2 else even_bit)) for i in range(count)]
         sent = total.astype(wire)
@@ -435,17 +435,17 @@
     state_shape = shape((blocks, 2 * width, BLOCK), BF16)
     table = pltpu.VMEM((blocks + 2, 2 * width, BLOCK), BF16)
 
-    near, far, lists, x, g, rule, w2 = pl.pallas_call(
+    near, far, lists, x, g, rule = pl.pallas_call(
         load_kernel,
         out_shape=(
             rim, rim, shape((2, 8, BLOCK), jnp.int32), values, values,
-            shape(rulebook.shape, jnp.int32), weight,
+            shape(rulebook.shape, jnp.int32),
         ),
-        in_specs=[HBM] * 5,
-        out_specs=(VMEM,) * 7,
-        scratch_shapes=[pltpu.SMEM((2,), jnp.int32), pltpu.SemaphoreType.DMA((5,))],
-        compiler_params=MEDIUM,
-    )(send_lists, features, cotangent, rulebook, weight_second)
+        in_specs=[HBM] * 4,
+        out_specs=(VMEM,) * 6,
+        scratch_shapes=[pltpu.SMEM((2,), jnp.int32), pltpu.SemaphoreType.DMA((4,))],
+        compiler_params=MEDIUM,
+    )(send_lists, features, cotangent, rulebook)
     far = lax.ppermute(far, axes, far_pairs)
     near = lax.ppermute(near, axes, near_pairs)
 
@@ -456,14 +456,14 @@
     )
     own_gather = pl.pallas_call(
         own_gather_kernel,
-        out_shape=(gathered, gathered, weight),
-        in_specs=[VMEM] * 3 + [HBM],
-        out_specs=(VMEM,) * 3,
-        scratch_shapes=[table, pltpu.SemaphoreType.DMA((1,))],
+        out_shape=(gathered, gathered, weight, weight),
+        in_specs=[VMEM] * 3 + [HBM] * 2,
+        out_specs=(VMEM,) * 4,
+        scratch_shapes=[table, pltpu.SemaphoreType.DMA((2,))],
         compiler_params=MEDIUM,
         cost_estimate=work,
     )
-    xs, gs, w1 = own_gather(rule, x, g, weight_first)
+    xs, gs, w2, w1 = own_gather(rule, x, g, weight_second, weight_first)
     own_conv = pl.pallas_call(
         own_conv_kernel,
         out_shape=(sums, sums, weight, gathered, gathered),

time: 39.2 us -> 39 us (level)
  transfers between devices with their start and end apart: 9 -> 9, of which waited for: 7 -> 7; matrix products, arithmetic and copies ran while one was open for 0% -> 0% of each run, Pallas kernels for 15% -> 16%
where the time goes in v12:
time: 39 us; the launch traced here: 38.8 us
  waiting for transfers between devices  25.5 us (65%)
  Pallas kernels  8.88 us (23%)
  starting transfers between devices  3.48 us (9%)
  between operations  0.73 us (2%)
    ppermute x3, waiting for transfers between devices, total_over_tiles(): received = lax.ppermute(sent, 'tile', pairs)  20 us
    ppermute x2, waiting for transfers between devices, body(): far = lax.ppermute(far, axes, far_pairs)  3.61 us
    pallas_call x1, Pallas kernels, body(): second_phase(near, far, state, rule, x, g, w1, w2)  2.36 us
    ppermute x2, starting transfers between devices, body(): near = lax.ppermute(near, axes, near_pairs)  1.29 us
    pallas_call x1, Pallas kernels, body(): xs, gs, w2, w1 = own_gather(rule, x, g, weight_second, weight_first)  1.23 us
    ppermute x3, starting transfers between devices, total_over_tiles(): received = lax.ppermute(sent, 'tile', pairs)  1.17 us
    pallas_call x1, Pallas kernels, body(): pl.pallas_call(rim_kernel, out_shape=(state_shape, rim, rim, shape(packed...  1.15 us
    ppermute x2, waiting for transfers between devices, body(): near = lax.ppermute(near, axes, near_pairs)  1.01 us
  transfers between devices with their start and end apart: 9, of which 7 were waited for; matrix products, arithmetic and copies ran while one was open for 0% of the time, Pallas kernels for 16%

profile of v12, /device:TPU:28, one launch (start us, length us, event | category | flops | bytes accessed | tf_op | source)
XLA Modules:
  0.0 38.8 jit_solution(2525674639460253178)
XLA Ops:
  0.6 0.9 %shard_map.93 = (bf16[128,128]{1,0:T(8,128)(2,1)S(1)}, bf16[128,128]{1,0:T(8,128)(2,1)S(1)}, s32[2,8,128]{2,1,0:T(8,128)S(1)}, bf16[64,384]{1,0:T(8,128)(2,1)S(1...) custom-call(s32[2]{0:T(128)} %bitcast.1, bf16[64,384]{1,0:T(8,128)(2,1)} %x_hbm.1, bf16[64,384]{1,0:T(8,128)(2,1)} %g_hbm.1, ...), custom_call_target="tpu_custom_call" | custom-call | tf_op jit(solution)/shard_map/pallas_call | solution.py:438
  1.5 0.9 %collective-permute-start = (bf16[128,128]{1,0:T(8,128)(2,1)S(1)}, bf16[128,128]{1,0:T(8,128)(2,1)S(1)}, u32[]{:S(2)}, u32[]{:S(2)}) collective-permute-start(bf16[128,128]{1,0:T(8,128)(2,1)S(1)} %get-tuple-element.32), channel_id=1, source_target_pairs={{0,16},{1,2},{2,1},{3,4},{4,3},{5,6},{6,5},{7,8},{8,7},{9,10},{10,... | collective-permute-start | bytes 98312 | tf_op jit(solution)/shard_map/ppermute | solution.py:449
  2.4 0.8 %collective-permute-start.1 = (bf16[128,128]{1,0:T(8,128)(2,1)S(1)}, bf16[128,128]{1,0:T(8,128)(2,1)S(1)}, u32[]{:S(2)}, u32[]{:S(2)}) collective-permute-start(bf16[128,128]{1,0:T(8,128)(2,1)S(1)} %get-tuple-element.33), channel_id=1, source_target_pairs={{0,1},{1,0},{2,3},{3,2},{4,5},{5,4},{6,7},{7,6},{8,9},{9,8},{10,11... | collective-permute-start | bytes 98312 | tf_op jit(solution)/shard_map/ppermute | solution.py:450
  3.2 1.2 %shard_map.94 = (bf16[1728,384]{1,0:T(8,128)(2,1)S(1)}, bf16[1728,384]{1,0:T(8,128)(2,1)S(1)}, bf16[64,1728]{1,0:T(8,128)(2,1)S(1)}, bf16[64,1728]{1,0:T(8,128)(2,1)S(1)}) custom-call(s32[27,384]{1,0:T(8,128)S(1)} %get-tuple-element.34.rule_ref, bf16[64,384]{1,0:T(8,128)(2,1)S(1)} %get-tuple-element.35.x_ref, bf16[64,384]{1,0:T(8,128)(2,1)S(1)} %get-tuple-element.36.g_ref, ...), custom_call_target="tpu_custom_call" | custom-call | flops 509607936 | bytes 2654208 | tf_op jit(solution)/shard_map/pallas_call | solution.py:466
  4.4 0.0 collective-permute-done.1.near_ref
  4.4 1.0 %shard_map.95 = (f32[64,384]{1,0:T(8,128)S(1)}, f32[64,384]{1,0:T(8,128)S(1)}, bf16[64,1728]{1,0:T(8,128)(2,1)S(1)}, bf16[1728,384]{1,0:T(8,128)(2,1)S(1)}, bf16[1728,384]{1,0:T(8,128)(2,1)S(1)}) custom-call(s32[2,8,128]{2,1,0:T(8,128)S(1)} %get-tuple-element.31.lists_ref, ...), custom_call_target="tpu_custom_call", output_to_operand_aliasing={{3}: (5, {}), {4}: (6, {})} | custom-call | flops 509607936 | bytes 2654208 | tf_op jit(solution)/shard_map/pallas_call | solution.py:476
  5.4 0.4 collective-permute-done.far_ref
  5.8 1.1 %shard_map.96 = (bf16[3,128,128]{2,1,0:T(8,128)(2,1)S(1)}, bf16[128,128]{1,0:T(8,128)(2,1)S(1)}, bf16[128,128]{1,0:T(8,128)(2,1)S(1)}, bf16[864,128]{1,0:T(8,128...) custom-call(s32[2,8,128]{2,1,0:T(8,128)S(1)} %get-tuple-element.31.l, ...), custom_call_target="tpu_custom_call", output_to_operand_aliasing={{4}: (7, {}), {5}: (8, {})} | custom-call | tf_op jit(solution)/shard_map/pallas_call | solution.py:477
  7.0 0.1 collective-permute-start.4
  7.1 0.6 %shard_map.98 = f32[864,128]{1,0:T(8,128)S(1)} custom-call(bf16[3,128,128]{2,1,0:T(8,128)(2,1)S(1)} %get-tuple-element.48.state_ref, bf16[1728,384]{1,0:T(8,128)(2,1)S(1)} %get-tuple-element.51.xs_ref, bf16[1728,384]{1,0:T(8,128)(2,1)S(1)} %get-tuple-element.52.gs_ref), custom_call_target="tpu_custom_call" | custom-call | tf_op jit(solution)/shard_map/pallas_call | solution.py:497
  7.7 0.8 %collective-permute-done.4 = bf16[864,128]{1,0:T(8,128)(2,1)S(1)} collective-permute-done((bf16[864,128]{1,0:T(8,128)(2,1)S(1)}, bf16[864,128]{1,0:T(8,128)(2,1)S(1)}, u32[]{:S(2)}, u32[]{:S(2)}) %collective-permute-start.4) | collective-permute-done | bytes 221216 | tf_op jit(solution)/shard_map/ppermute | solution.py:383
  8.6 0.4 %collective-permute-start.5 = (bf16[864,128]{1,0:T(8,128)(2,1)S(1)}, bf16[864,128]{1,0:T(8,128)(2,1)S(1)}, u32[]{:S(2)}, u32[]{:S(2)}) collective-permute-start(bf16[864,128]{1,0:T(8,128)(2,1)S(1)} %add_convert_fusion.2), channel_id=1, source_target_pairs={{0,8},{1,5},{2,10},{3,7},{4,12},{5,1},{6,14},{7,3},{8,0},{9,13},{1... | collective-permute-start | bytes 663560 | tf_op jit(solution)/shard_map/ppermute | solution.py:390
  9.0 8.8 %collective-permute-done.5 = bf16[864,128]{1,0:T(8,128)(2,1)S(1)} collective-permute-done((bf16[864,128]{1,0:T(8,128)(2,1)S(1)}, bf16[864,128]{1,0:T(8,128)(2,1)S(1)}, u32[]{:S(2)}, u32[]{:S(2)}) %collective-permute-start.5) | collective-permute-done | bytes 221216 | tf_op jit(solution)/shard_map/ppermute | solution.py:390
  17.8 0.1 add_convert_fusion.1
  17.8 0.7 %collective-permute-start.6 = (bf16[864,128]{1,0:T(8,128)(2,1)S(1)}, bf16[864,128]{1,0:T(8,128)(2,1)S(1)}, u32[]{:S(2)}, u32[]{:S(2)}) collective-permute-start(bf16[864,128]{1,0:T(8,128)(2,1)S(1)} %add_convert_fusion.1), channel_id=1, source_target_pairs={{0,2},{1,9},{2,0},{3,11},{4,6},{5,13},{6,4},{7,15},{8,10},{9,1},{1... | collective-permute-start | bytes 663560 | tf_op jit(solution)/shard_map/ppermute | solution.py:390
  18.6 5.3 %collective-permute-done.6 = bf16[864,128]{1,0:T(8,128)(2,1)S(1)} collective-permute-done((bf16[864,128]{1,0:T(8,128)(2,1)S(1)}, bf16[864,128]{1,0:T(8,128)(2,1)S(1)}, u32[]{:S(2)}, u32[]{:S(2)}) %collective-permute-start.6) | collective-permute-done | bytes 221216 | tf_op jit(solution)/shard_map/ppermute | solution.py:390
  23.8 0.1 add_convert_fusion
  23.9 0.1 collective-permute-start.7
  24.0 5.9 %collective-permute-done.7 = bf16[864,128]{1,0:T(8,128)(2,1)S(1)} collective-permute-done((bf16[864,128]{1,0:T(8,128)(2,1)S(1)}, bf16[864,128]{1,0:T(8,128)(2,1)S(1)}, u32[]{:S(2)}, u32[]{:S(2)}) %collective-permute-start.7) | collective-permute-done | bytes 221216 | tf_op jit(solution)/shard_map/ppermute | solution.py:390
  29.9 0.1 multiply_convert_fusion.own_ref
  30.0 0.1 collective-permute-start.8
  30.1 0.5 %collective-permute-start.2 = (bf16[128,128]{1,0:T(8,128)(2,1)S(1)}, bf16[128,128]{1,0:T(8,128)(2,1)S(1)}, u32[]{:S(2)}, u32[]{:S(2)}) collective-permute-start(bf16[128,128]{1,0:T(8,128)(2,1)S(1)} %get-tuple-element.46), channel_id=1, source_target_pairs={{0,1},{1,0},{2,3},{3,2},{4,5},{5,4},{6,7},{7,6},{8,9},{9,8},{10,11... | collective-permute-start | bytes 98312 | tf_op jit(solution)/shard_map/ppermute | solution.py:499
  30.6 0.0 collective-permute-start.3
  30.6 1.0 %collective-permute-done.2.near_ref = bf16[128,128]{1,0:T(8,128)(2,1)S(1)} collective-permute-done((bf16[128,128]{1,0:T(8,128)(2,1)S(1)}, bf16[128,128]{1,0:T(8,128)(2,1)S(1)}, u32[]{:S(2)}, u32[]{:S(2)}) %collective-permute-start.2) | collective-permute-done | bytes 32800 | tf_op jit(solution)/shard_map/ppermute | solution.py:499
  31.6 3.2 %collective-permute-done.3.far_ref = bf16[128,128]{1,0:T(8,128)(2,1)S(1)} collective-permute-done((bf16[128,128]{1,0:T(8,128)(2,1)S(1)}, bf16[128,128]{1,0:T(8,128)(2,1)S(1)}, u32[]{:S(2)}, u32[]{:S(2)}) %collective-permute-start.3) | collective-permute-done | bytes 32800 | tf_op jit(solution)/shard_map/ppermute | solution.py:500
  34.8 2.4 %shard_map.97 = (bf16[64,384]{1,0:T(8,128)(2,1)}, bf16[64,384]{1,0:T(8,128)(2,1)}) custom-call(bf16[128,128]{1,0:T(8,128)(2,1)S(1)} %collective-permute-done.2.near_ref, bf16[128,128]{1,0:T(8,128)(2,1)S(1)} %collective-permute-done.3.far_ref, bf16[3,128,128]{2,1,0:T(8,128)(2,1)S(1)} %get-tuple-element.48.state_ref, ...), custom_call_target="tpu_custom_call" | custom-call | flops 509607936 | bytes 2654208 | tf_op jit(solution)/shard_map/pallas_call | solution.py:515
  37.2 0.8 %shard_map.99 = (f32[64,1728]{1,0:T(8,128)}, f32[64,1728]{1,0:T(8,128)}) custom-call(bf16[864,128]{1,0:T(8,128)(2,1)S(1)} %multiply_convert_fusion.own_ref), custom_call_target="tpu_custom_call" | custom-call | tf_op jit(solution)/shard_map/pallas_call | solution.py:404
  38.0 0.0 collective-permute-done.8.other_ref
  38.0 0.8 %shard_map.100 = (f32[64,1728]{1,0:T(8,128)}, f32[64,1728]{1,0:T(8,128)}) custom-call(bf16[864,128]{1,0:T(8,128)(2,1)S(1)} %collective-permute-done.8.other_ref, f32[64,1728]{1,0:T(8,128)} %get-tuple-element.54.first_in, f32[64,1728]{1,0:T(8,128)} %get-tuple-element.55.second_in), custom_call_target="tpu_custom_call", output_to_operand_aliasing={{0}: (1, {}), {1}: (2, {})} | custom-call | tf_op jit(solution)/shard_map/pallas_call | solution.py:405
  (1 shorter events, 0.0 us)
Async XLA Ops:
  1.5 4.3 %collective-permute-start = (bf16[128,128]{1,0:T(8,128)(2,1)S(1)}, bf16[128,128]{1,0:T(8,128)(2,1)S(1)}, u32[]{:S(2)}, u32[]{:S(2)}) collective-permute-start(bf16[128,128]{1,0:T(8,128)(2,1)S(1)} %get-tuple-element.32), channel_id=1, source_target_pairs={{0,16},{1,2},{2,1},{3,4},{4,3},{5,6},{6,5},{7,8},{8,7},{9,10},{10,... | collective-permute-start | bytes 98312 | tf_op jit(solution)/shard_map/ppermute | solution.py:449
  2.4 2.0 %collective-permute-start.1 = (bf16[128,128]{1,0:T(8,128)(2,1)S(1)}, bf16[128,128]{1,0:T(8,128)(2,1)S(1)}, u32[]{:S(2)}, u32[]{:S(2)}) collective-permute-start(bf16[128,128]{1,0:T(8,128)(2,1)S(1)} %get-tuple-element.33), channel_id=1, source_target_pairs={{0,1},{1,0},{2,3},{3,2},{4,5},{5,4},{6,7},{7,6},{8,9},{9,8},{10,11... | collective-permute-start | bytes 98312 | tf_op jit(solution)/shard_map/ppermute | solution.py:450
  7.0 1.5 %collective-permute-start.4 = (bf16[864,128]{1,0:T(8,128)(2,1)S(1)}, bf16[864,128]{1,0:T(8,128)(2,1)S(1)}, u32[]{:S(2)}, u32[]{:S(2)}) collective-permute-start(bf16[864,128]{1,0:T(8,128)(2,1)S(1)} %get-tuple-element.53), channel_id=1, source_target_pairs={{0,1},{1,0},{2,3},{3,2},{4,5},{5,4},{6,7},{7,6},{8,9},{9,8},{10,11... | collective-permute-start | bytes 663560 | tf_op jit(solution)/shard_map/ppermute | solution.py:383
  8.6 9.2 %collective-permute-start.5 = (bf16[864,128]{1,0:T(8,128)(2,1)S(1)}, bf16[864,128]{1,0:T(8,128)(2,1)S(1)}, u32[]{:S(2)}, u32[]{:S(2)}) collective-permute-start(bf16[864,128]{1,0:T(8,128)(2,1)S(1)} %add_convert_fusion.2), channel_id=1, source_target_pairs={{0,8},{1,5},{2,10},{3,7},{4,12},{5,1},{6,14},{7,3},{8,0},{9,13},{1... | collective-permute-start | bytes 663560 | tf_op jit(solution)/shard_map/ppermute | solution.py:390
  17.8 6.0 %collective-permute-start.6 = (bf16[864,128]{1,0:T(8,128)(2,1)S(1)}, bf16[864,128]{1,0:T(8,128)(2,1)S(1)}, u32[]{:S(2)}, u32[]{:S(2)}) collective-permute-start(bf16[864,128]{1,0:T(8,128)(2,1)S(1)} %add_convert_fusion.1), channel_id=1, source_target_pairs={{0,2},{1,9},{2,0},{3,11},{4,6},{5,13},{6,4},{7,15},{8,10},{9,1},{1... | collective-permute-start | bytes 663560 | tf_op jit(solution)/shard_map/ppermute | solution.py:390
  23.9 6.0 %collective-permute-start.7 = (bf16[864,128]{1,0:T(8,128)(2,1)S(1)}, bf16[864,128]{1,0:T(8,128)(2,1)S(1)}, u32[]{:S(2)}, u32[]{:S(2)}) collective-permute-start(bf16[864,128]{1,0:T(8,128)(2,1)S(1)} %add_convert_fusion), channel_id=1, source_target_pairs={{0,4},{1,3},{2,6},{3,1},{4,0},{5,7},{6,2},{7,5},{8,12},{9,11},{10,... | collective-permute-start | bytes 663560 | tf_op jit(solution)/shard_map/ppermute | solution.py:390
  30.0 8.0 %collective-permute-start.8 = (bf16[864,128]{1,0:T(8,128)(2,1)S(1)}, bf16[864,128]{1,0:T(8,128)(2,1)S(1)}, u32[]{:S(2)}, u32[]{:S(2)}) collective-permute-start(bf16[864,128]{1,0:T(8,128)(2,1)S(1)} %multiply_convert_fusion.own_ref), channel_id=1, source_target_pairs={{0,1},{1,0},{2,3},{3,2},{4,5},{5,4},{6,7},{7,6},{8,9},{9,8},{10,11... | collective-permute-start | bytes 663560 | tf_op jit(solution)/shard_map/ppermute | solution.py:393
  30.1 1.5 %collective-permute-start.2 = (bf16[128,128]{1,0:T(8,128)(2,1)S(1)}, bf16[128,128]{1,0:T(8,128)(2,1)S(1)}, u32[]{:S(2)}, u32[]{:S(2)}) collective-permute-start(bf16[128,128]{1,0:T(8,128)(2,1)S(1)} %get-tuple-element.46), channel_id=1, source_target_pairs={{0,1},{1,0},{2,3},{3,2},{4,5},{5,4},{6,7},{7,6},{8,9},{9,8},{10,11... | collective-permute-start | bytes 98312 | tf_op jit(solution)/shard_map/ppermute | solution.py:499
  30.6 4.2 %collective-permute-start.3 = (bf16[128,128]{1,0:T(8,128)(2,1)S(1)}, bf16[128,128]{1,0:T(8,128)(2,1)S(1)}, u32[]{:S(2)}, u32[]{:S(2)}) collective-permute-start(bf16[128,128]{1,0:T(8,128)(2,1)S(1)} %get-tuple-element.47), channel_id=1, source_target_pairs={{0,16},{1,2},{2,1},{3,4},{4,3},{5,6},{6,5},{7,8},{8,7},{9,10},{10,... | collective-permute-start | bytes 98312 | tf_op jit(solution)/shard_map/ppermute | solution.py:500
